TPU v7x, 256 devices: a whole 4x4x8 slice. The times are simulated.
256 devices in a mesh: gx: 32 (over x, z), gy: 8 (over y, core).
Axes of the slice: x: 4, y: 4, z: 8, core: 2. Of those that a mesh axis runs over, the one named last changes fastest.
Arguments:
- scalar: float32 [8, 4096, 2048], P(None, 'gx', 'gy'), may hold values from -6 to 6
- diffusivity: float32 [8, 4096, 2048], P(None, 'gx', 'gy'), may hold values from 0.1 to 1
Outputs:
- grad_x: float32 [8, 4096, 2048], P(None, 'gx', 'gy')
- grad_y: float32 [8, 4096, 2048], P(None, 'gx', 'gy')
- diffusion: float32 [8, 4096, 2048], P(None, 'gx', 'gy')
All inputs are finite; a program needn't handle non-finite values.
Results may differ from a plain program's by a relative error of at most 0.000075.
Values sent between devices are 32-bit elements; how exact they have to be, the bound alone decides.
A program may use at most 128 MiB of HBM per device.

v0:
```python
import jax
import jax.numpy as jnp
from jax import lax
from jax.sharding import PartitionSpec as P

FIRST_ALPHA = 1.0 / 3.0
FIRST_A = 14.0 / 9.0
FIRST_B = 1.0 / 9.0
SECOND_ALPHA = 2.0 / 11.0
SECOND_A = 12.0 / 11.0
SECOND_B = 3.0 / 11.0
HIGHEST_PRECISION = lax.Precision.HIGHEST


def extended(block, sides, width):
    for axis, dim in sides:
        count = lax.axis_size(axis)
        forward = [(i, i + 1) for i in range(count - 1)]
        forward.append((count - 1, 0))
        backward = [(target, source) for source, target in forward]
        low = lax.ppermute(
            lax.slice_in_dim(block, block.shape[dim] - width, None, axis=dim), axis, forward
        )
        high = lax.ppermute(lax.slice_in_dim(block, 0, width, axis=dim), axis, backward)
        block = jnp.concatenate([low, block, high], axis=dim)
    return block


def line_inverse(cells, alpha):
    indices = jnp.arange(cells)
    distance = jnp.abs(indices[:, None] - indices[None, :])
    matrix = jnp.where(distance == 0, 1.0, jnp.where(distance == 1, alpha, 0.0)).astype(jnp.float32)
    factor = jnp.linalg.cholesky(matrix)
    return jax.scipy.linalg.cho_solve((factor, True), jnp.eye(cells, dtype=jnp.float32))


def shifted(padded, axis_dim, offset, row_count):
    return lax.slice_in_dim(padded, 2 + offset, 2 + offset + row_count, axis=axis_dim)


def first_rhs(padded, axis_dim, row_count):
    inner = shifted(padded, axis_dim, 1, row_count) - shifted(padded, axis_dim, -1, row_count)
    outer = shifted(padded, axis_dim, 2, row_count) - shifted(padded, axis_dim, -2, row_count)
    return 0.5 * FIRST_A * inner + 0.25 * FIRST_B * outer


def second_rhs(padded, axis_dim, row_count):
    centre = 2.0 * shifted(padded, axis_dim, 0, row_count)
    inner = (
        shifted(padded, axis_dim, 1, row_count) + shifted(padded, axis_dim, -1, row_count) - centre
    )
    outer = (
        shifted(padded, axis_dim, 2, row_count) + shifted(padded, axis_dim, -2, row_count) - centre
    )
    return SECOND_A * inner + 0.25 * SECOND_B * outer


def solve_lines_x(along_x, inverse_first, inverse_second):
    row_count = inverse_first.shape[1]
    return jnp.concatenate(
        [
            jnp.einsum(
                "ij,cpjk->cpik",
                inverse_first,
                first_rhs(along_x, 2, row_count),
                precision=HIGHEST_PRECISION,
            ),
            jnp.einsum(
                "ij,pjk->pik",
                inverse_second,
                second_rhs(along_x[0], 1, row_count),
                precision=HIGHEST_PRECISION,
            )[None],
        ],
        axis=0,
    )


def solve_lines_y(along_y, inverse_first, inverse_second):
    row_count = inverse_first.shape[1]
    return jnp.concatenate(
        [
            jnp.einsum(
                "cpkj,ij->cpki",
                first_rhs(along_y, 3, row_count),
                inverse_first,
                precision=HIGHEST_PRECISION,
            ),
            jnp.einsum(
                "pkj,ij->pki",
                second_rhs(along_y[0], 2, row_count),
                inverse_second,
                precision=HIGHEST_PRECISION,
            )[None],
        ],
        axis=0,
    )


def line_tables(cells):
    first_table = line_inverse(cells, FIRST_ALPHA)
    second_table = line_inverse(cells, SECOND_ALPHA)
    return (first_table, second_table, jnp.stack([first_table, first_table, second_table]))


def as_column(columns, axis_dim):
    column_shape = [columns.shape[0], 1, 1, 1]
    column_shape[axis_dim] = columns.shape[1]
    return columns.reshape(column_shape)


def along_line(columns, values, axis_dim):
    return as_column(columns, axis_dim) * jnp.expand_dims(values, axis_dim)


def pair_values(prev_last, own_first, own_last, next_first, inverses, alphas):
    pair_gain = (alphas * inverses[:, 0, 0])[:, None, None]
    scale = 1.0 / (1.0 - pair_gain * pair_gain)
    left_end = (prev_last - pair_gain * own_first) * scale
    right_end = (next_first - pair_gain * own_last) * scale
    return (left_end, right_end)


def coupled_lines(local_lines, prev_last, next_first, inverses, alphas, axis_dim):
    cells = local_lines.shape[axis_dim]
    own_first = lax.index_in_dim(local_lines, 0, axis_dim, keepdims=False)
    own_last = lax.index_in_dim(local_lines, cells - 1, axis_dim, keepdims=False)
    left_end, right_end = pair_values(prev_last, own_first, own_last, next_first, inverses, alphas)
    gains = alphas.reshape(3, 1, 1, 1)
    return local_lines - gains * (
        along_line(inverses[:, :, 0], left_end, axis_dim)
        + along_line(inverses[:, :, cells - 1], right_end, axis_dim)
    )


def local(scalar, diffusivity):
    cells_x = scalar.shape[1]
    cells_y = scalar.shape[2]
    alphas = jnp.array([FIRST_ALPHA, FIRST_ALPHA, SECOND_ALPHA], jnp.float32)
    both_fields = jnp.stack([scalar, diffusivity])
    first_x, second_x, inverses_x = line_tables(cells_x)
    first_y, second_y, inverses_y = line_tables(cells_y)
    padded = extended(both_fields, (("gx", 2), ("gy", 3)), 2)
    local_x = solve_lines_x(padded[:, :, :, 2:-2], first_x, second_x)
    local_y = solve_lines_y(padded[:, :, 2:-2, :], first_y, second_y)
    rims_x = extended(local_x, (("gx", 2),), 1)
    rims_y = extended(local_y, (("gy", 3),), 1)
    full_x = coupled_lines(
        local_x, rims_x[:, :, 0, :], rims_x[:, :, cells_x + 1, :], inverses_x, alphas, 2
    )
    full_y = coupled_lines(
        local_y, rims_y[:, :, :, 0], rims_y[:, :, :, cells_y + 1], inverses_y, alphas, 3
    )
    grad_x = full_x[0]
    grad_y = full_y[0]
    diffusion = diffusivity * (full_x[2] + full_y[2]) + full_x[1] * grad_x + full_y[1] * grad_y
    return (grad_x, grad_y, diffusion)


def solution(mesh):
    placed = (P(None, "gx", "gy"), P(None, "gx", "gy"))
    return jax.shard_map(
        local,
        mesh=mesh,
        in_specs=placed,
        out_specs=(P(None, "gx", "gy"), P(None, "gx", "gy"), P(None, "gx", "gy")),
        check_vma=False,
    )
```

profile of v0, /device:TPU:1, one launch (start us, length us, event | category | flops | bytes accessed | tf_op | source)
XLA Modules:
  0.0 302.1 jit_solution(6846068421516825345)
XLA Ops:
  4.0 8.6 %collective-permute-start = (f32[2,8,2,256]{3,1,2,0:T(8,128)}, f32[2,8,2,256]{3,1,2,0:T(8,128)S(1)}, u32[]{:S(2)}, u32[]{:S(2)}) collective-permute-start(f32[2,8,2,256]{3,1,2,0:T(8,128)} %get-tuple-element.71), channel_id=1, source_target_pairs={{8,0},{16,8},{24,16},{32,24},{40,32},{48,40},{56,48},{64,56},{72,6... | collective-permute-start | bytes 98312 | tf_op jit(solution)/shard_map/ppermute | solution.py:24
  13.4 11.7 %cholesky.228 = f32[128,128]{1,0:T(8,128)S(1)} custom-call(f32[128,128]{1,0:T(8,128)S(1)} %cholesky.261), custom_call_target="Cholesky" | custom-call | tf_op jit(solution)/shard_map/jit(cholesky)/cholesky | solution.py:33
  25.1 9.8 %custom-call.27 = f32[1,128,128]{1,2,0:T(8,128)S(1)} custom-call(f32[1,128,128]{2,1,0:T(8,128)S(1)} %get-tuple-element.83), custom_call_target="InvertDiagBlocksLowerTriangular" | custom-call | tf_op jit(solution)/shard_map/jit(cholesky)/cholesky | solution.py:33
  35.4 11.7 %cholesky.245 = f32[128,128]{1,0:T(8,128)S(1)} custom-call(f32[128,128]{1,0:T(8,128)S(1)} %convolution_subtract_fusion.4), custom_call_target="Cholesky" | custom-call | tf_op jit(solution)/shard_map/jit(cholesky)/cholesky | solution.py:33
  49.2 3.8 %while.5 = (s32[]{:T(128)}, f32[256,256]{1,0:T(8,128)S(1)}, s32[2,2]{1,0:T(2,128)S(1)}, f32[2,128,128]{2,1,0:T(8,128)S(1)}, s32[]{:T(128)}) while((s32[]{:T(128)}, f32[256,256]{1,0:T(8,128)S(1)}, s32[2,2]{1,0:T(2,128)S(1)}, f32[2,128,128]{2,1,0:T(8,128)S(1)}, s32[]{:T(128)}) %tuple.71), condition=%wide.while_cond.clone, body=%wide.while_body.clone.sunk | while | flops 2 | bytes 131189 | solution.py:34
  53.0 19.9 %custom-call.28 = f32[2,128,128]{1,2,0:T(8,128)S(1)} custom-call(f32[2,128,128]{2,1,0:T(8,128)S(1)} %get-tuple-element.22), custom_call_target="InvertDiagBlocksLowerTriangular" | custom-call | tf_op jit(solution)/shard_map/jit(_cho_solve)/triangular_solve | solution.py:34
  76.0 11.7 %cholesky.194 = f32[128,128]{1,0:T(8,128)S(1)} custom-call(f32[128,128]{1,0:T(8,128)S(1)} %cholesky.258), custom_call_target="Cholesky" | custom-call | tf_op jit(solution)/shard_map/jit(cholesky)/cholesky | solution.py:33
  87.8 9.8 %custom-call.25 = f32[1,128,128]{1,2,0:T(8,128)S(1)} custom-call(f32[1,128,128]{2,1,0:T(8,128)S(1)} %get-tuple-element.79), custom_call_target="InvertDiagBlocksLowerTriangular" | custom-call | tf_op jit(solution)/shard_map/jit(cholesky)/cholesky | solution.py:33
  98.1 11.7 %cholesky.211 = f32[128,128]{1,0:T(8,128)S(1)} custom-call(f32[128,128]{1,0:T(8,128)S(1)} %convolution_subtract_fusion.5), custom_call_target="Cholesky" | custom-call | tf_op jit(solution)/shard_map/jit(cholesky)/cholesky | solution.py:33
  111.8 3.8 %while.4 = (s32[]{:T(128)}, f32[256,256]{1,0:T(8,128)S(1)}, s32[2,2]{1,0:T(2,128)S(1)}, f32[2,128,128]{2,1,0:T(8,128)S(1)}, s32[]{:T(128)}) while((s32[]{:T(128)}, f32[256,256]{1,0:T(8,128)S(1)}, s32[2,2]{1,0:T(2,128)S(1)}, f32[2,128,128]{2,1,0:T(8,128)S(1)}, s32[]{:T(128)}) %tuple.77), condition=%wide.while_cond, body=%wide.while_body.sunk | while | flops 2 | bytes 131189 | solution.py:34
  115.6 20.1 %custom-call.26 = f32[2,128,128]{1,2,0:T(8,128)S(1)} custom-call(f32[2,128,128]{2,1,0:T(8,128)S(1)} %get-tuple-element.21), custom_call_target="InvertDiagBlocksLowerTriangular" | custom-call | tf_op jit(solution)/shard_map/jit(_cho_solve)/triangular_solve | solution.py:34
  139.2 11.7 %cholesky.181 = f32[128,128]{1,0:T(8,128)S(1)} custom-call(f32[128,128]{1,0:T(8,128)S(1)} %fusion.71), custom_call_target="Cholesky" | custom-call | tf_op jit(solution)/shard_map/jit(cholesky)/cholesky | solution.py:33
  152.3 9.8 %custom-call.24 = f32[1,128,128]{1,2,0:T(8,128)S(1)} custom-call(f32[1,128,128]{2,1,0:T(8,128)S(1)} %fusion.60), custom_call_target="InvertDiagBlocksLowerTriangular" | custom-call | tf_op jit(solution)/shard_map/jit(_cho_solve)/triangular_solve | solution.py:34
  162.8 11.7 %cholesky.170 = f32[128,128]{1,0:T(8,128)S(1)} custom-call(f32[128,128]{1,0:T(8,128)S(1)} %fusion.76), custom_call_target="Cholesky" | custom-call | tf_op jit(solution)/shard_map/jit(cholesky)/cholesky | solution.py:33
  176.0 9.8 %custom-call.23 = f32[1,128,128]{1,2,0:T(8,128)S(1)} custom-call(f32[1,128,128]{2,1,0:T(8,128)S(1)} %fusion.59), custom_call_target="InvertDiagBlocksLowerTriangular" | custom-call | tf_op jit(solution)/shard_map/jit(_cho_solve)/triangular_solve | solution.py:34
  208.5 3.4 %convolution_bitcast_fusion = f32[2,8,128,256]{2,1,3,0:T(8,128)S(1)} fusion(f32[2,8,128,256]{2,1,3,0:T(8,128)} %copy.153, f32[128,128]{0,1:T(8,128)S(1)} %fusion.73), kind=kOutput, calls=%fused_computation.36 | convolution fusion | flops 805306368 | bytes 4259840 | tf_op jit(solution)/shard_map/ij,cpjk->cpik/dot_general | solution.py:62
  211.9 5.4 %broadcast_multiply_fusion.2 = (f32[3,8,1,256]{2,1,3,0:T(8,128)}, f32[3,8,1,256]{2,1,3,0:T(8,128)}, f32[3,8,1,256]{2,1,3,0:T(8,128)}, f32[3,8,1,256]{2,1,3,0:T(8,128)}) fusion(f32[3]{0:T(128)S(1)} %get-tuple-element.35, f32[1,8,128,256]{2,1,3,0:T(8,128)S(1)} %convolution_bitcast_fusion.1, f32[2,8,128,256]{2,1,3,0:T(8,128)S(1)} %convolution_bitcast_fusion), kind=kLoop, calls=%fused_computation.45 | loop fusion | flops 24576 | bytes 3244044 | tf_op jit(solution)/shard_map/mul | solution.py:120
  222.6 5.1 %collective-permute-start.3 = (f32[3,8,1,256]{3,1,2,0:T(8,128)S(1)}, f32[3,8,1,256]{3,1,2,0:T(8,128)}, u32[]{:S(2)}, u32[]{:S(2)}) collective-permute-start(f32[3,8,1,256]{3,1,2,0:T(8,128)S(1)} %copy.163), channel_id=1, source_target_pairs={{8,0},{16,8},{24,16},{32,24},{40,32},{48,40},{56,48},{64,56},{72,6... | collective-permute-start | bytes 73736 | tf_op jit(solution)/shard_map/ppermute | solution.py:24
  238.0 3.6 %pad_maximum_fusion.2 = (f32[2,8,132,258]{3,1,2,0:T(8,128)S(1)}, f32[2,8,132,258]{3,1,2,0:T(8,128)S(1)}) fusion(f32[2,8,132,2]{3,1,2,0:T(8,128)} %copy-done.3, f32[2,8,2,256]{3,1,2,0:T(8,128)S(1)} %collective-permute-done, f32[1,8,128,256]{3,1,2,0:T(8,128)S(1)} %get-tuple-element.92, f32[1,8,128,256]{3,1,2,0:T(8,128)S(1)} %get-tuple-element.93, ...), kind=kLoop, calls=%fused_computation.14 | loop fusion | flops 4359168 | bytes 6555648 | tf_op jit(solution)/shard_map/concatenate | solution.py:25
  241.7 4.3 %fusion.6 = f32[2,8,128,256]{3,1,2,0:T(8,128)} fusion(f32[2,8,132,258]{3,1,2,0:T(8,128)S(1)} %get-tuple-element.65, f32[2,8,132,258]{3,1,2,0:T(8,128)S(1)} %get-tuple-element.64, f32[128,256]{0,1:T(8,128)S(1)} %copy-done.9, f32[128,256]{0,1:T(8,128)S(1)} %copy-done.11), kind=kOutput, calls=%fused_computation.26 | convolution fusion | flops 1613299712 | bytes 10747904 | tf_op jit(solution)/shard_map/cpkj,ij->cpki/dot_general | solution.py:83
  264.9 5.0 %broadcast_multiply_fusion.1 = (f32[3,8,1,256]{2,1,3,0:T(8,128)}, f32[3,8,1,256]{2,1,3,0:T(8,128)}) fusion(f32[3,8,1,256]{2,1,3,0:T(8,128)S(1)} %copy-done.2, f32[3]{0:T(128)S(1)} %copy-done.23, f32[3,8,1,256]{2,1,3,0:T(8,128)} %copy.165), kind=kLoop, calls=%fused_computation.44 | loop fusion | flops 12288 | bytes 98316 | tf_op jit(solution)/shard_map/mul | solution.py:119
  270.0 6.0 %copy.203 = f32[3,8,1,256]{1,3,0,2:T(8,128)S(1)} copy(f32[3,8,1,256]{2,1,3,0:T(8,128)} %get-tuple-element.87) | data formatting | bytes 49152 | tf_op jit(solution)/shard_map/mul | solution.py:113
  276.0 6.7 %copy.202 = f32[3,8,1,256]{1,3,0,2:T(8,128)} copy(f32[3,8,1,256]{2,1,3,0:T(8,128)} %get-tuple-element.86) | data formatting | bytes 49152 | tf_op jit(solution)/shard_map/mul | solution.py:113
  283.5 8.0 %fusion.2 = (f32[3,8,128,256]{2,1,3,0:T(8,128)}, f32[3,8,128,256]{2,1,3,0:T(8,128)S(1)}) fusion(f32[1,8,128,256]{2,1,3,0:T(8,128)S(1)} %bitcast.179, f32[2,8,128,256]{2,1,3,0:T(8,128)S(1)} %copy.185, f32[3,8,128]{2,1,0:T(8,128)S(1)} %multiply_bitcast_fusion, f32[3,256]{1,0:T(4,128)S(1)} %bitcast.186, f32[3,8,128]{2,1,0:T(8,128)S(1)} %get-tuple-element.52, ...), kind=kLoop, calls=%fused_computation.18 | loop fusion | flops 9437184 | bytes 12665868 | tf_op jit(solution)/shard_map/sub | solution.py:130
  (180 shorter events, 92.4 us)
Async XLA Ops:
  4.0 183.8 %collective-permute-start = (f32[2,8,2,256]{3,1,2,0:T(8,128)}, f32[2,8,2,256]{3,1,2,0:T(8,128)S(1)}, u32[]{:S(2)}, u32[]{:S(2)}) collective-permute-start(f32[2,8,2,256]{3,1,2,0:T(8,128)} %get-tuple-element.71), channel_id=1, source_target_pairs={{8,0},{16,8},{24,16},{32,24},{40,32},{48,40},{56,48},{64,56},{72,6... | collective-permute-start | bytes 98312 | tf_op jit(solution)/shard_map/ppermute | solution.py:24
  12.6 175.2 %collective-permute-start.1 = (f32[2,8,2,256]{3,1,2,0:T(8,128)}, f32[2,8,2,256]{3,1,2,0:T(8,128)S(1)}, u32[]{:S(2)}, u32[]{:S(2)}) collective-permute-start(f32[2,8,2,256]{3,1,2,0:T(8,128)} %get-tuple-element.70), channel_id=1, source_target_pairs={{0,8},{8,16},{16,24},{24,32},{32,40},{40,48},{48,56},{56,64},{64,7... | collective-permute-start | bytes 98312 | tf_op jit(solution)/shard_map/ppermute | solution.py:21
  136.0 50.4 %copy-start.16 = (f32[128,256]{0,1:T(8,128)S(1)}, f32[128,256]{0,1:T(8,128)}, u32[]{:S(2)}) copy-start(f32[128,256]{0,1:T(8,128)} %copy.181) | copy-start | bytes 393220
  136.8 50.3 %copy-start.24 = (f32[3,1,1]{1,2,0:T(1,128)S(1)}, f32[3,1,1]{1,2,0:T(1,128)}, u32[]{:S(2)}) copy-start(f32[3,1,1]{1,2,0:T(1,128)} %constant.148) | copy-start | bytes 40
  136.9 50.3 %copy-start.25 = (f32[3,1,1]{1,2,0:T(1,128)S(1)}, f32[3,1,1]{1,2,0:T(1,128)}, u32[]{:S(2)}) copy-start(f32[3,1,1]{1,2,0:T(1,128)} %constant.150) | copy-start | bytes 40
  137.0 50.8 %copy-start.8 = (f32[128,256]{0,1:T(8,128)}, f32[128,256]{0,1:T(8,128)S(1)}, u32[]{:S(2)}) copy-start(f32[128,256]{0,1:T(8,128)S(1)} %copy.174) | copy-start | bytes 393220
  138.7 49.3 %copy-start.18 = (f32[128,256]{0,1:T(8,128)}, f32[128,256]{0,1:T(8,128)S(1)}, u32[]{:S(2)}) copy-start(f32[128,256]{0,1:T(8,128)S(1)} %fusion.82) | copy-start | bytes 393220
  139.1 48.9 %copy-start.10 = (f32[128,256]{0,1:T(8,128)}, f32[128,256]{0,1:T(8,128)S(1)}, u32[]{:S(2)}) copy-start(f32[128,256]{0,1:T(8,128)S(1)} %fusion.79) | copy-start | bytes 393220
  162.7 25.3 %copy-start.12 = (f32[128,128]{0,1:T(8,128)}, f32[128,128]{0,1:T(8,128)S(1)}, u32[]{:S(2)}) copy-start(f32[128,128]{0,1:T(8,128)S(1)} %fusion.68) | copy-start | bytes 196612
  192.6 35.1 %collective-permute-start.4 = (f32[2,8,132,2]{2,1,3,0:T(8,128)}, f32[2,8,132,2]{2,1,3,0:T(8,128)}, u32[]{:S(2)}, u32[]{:S(2)}) collective-permute-start(f32[2,8,132,2]{2,1,3,0:T(8,128)} %copy.168), channel_id=1, source_target_pairs={{1,0},{2,1},{3,2},{4,3},{5,4},{6,5},{7,6},{0,7},{9,8},{10,9},{11,1... | collective-permute-start | bytes 50696 | tf_op jit(solution)/shard_map/ppermute | solution.py:24
  196.1 33.2 %collective-permute-start.5 = (f32[2,8,132,2]{2,1,3,0:T(8,128)}, f32[2,8,132,2]{2,1,3,0:T(8,128)}, u32[]{:S(2)}, u32[]{:S(2)}) collective-permute-start(f32[2,8,132,2]{2,1,3,0:T(8,128)} %copy.170), channel_id=1, source_target_pairs={{0,1},{1,2},{2,3},{3,4},{4,5},{5,6},{6,7},{7,0},{8,9},{9,10},{10,1... | collective-permute-start | bytes 50696 | tf_op jit(solution)/shard_map/ppermute | solution.py:21
  198.5 4.8 %copy-start.14 = (f32[2,8,2,256]{3,1,2,0:T(8,128)S(1)}, f32[2,8,2,256]{3,1,2,0:T(8,128)}, u32[]{:S(2)}) copy-start(f32[2,8,2,256]{3,1,2,0:T(8,128)} %copy-done.13) | copy-start | bytes 98308
  203.3 8.5 %copy-start.4 = (f32[1,8,128,256]{2,1,3,0:T(8,128)}, f32[1,8,128,256]{2,1,3,0:T(8,128)S(1)}, u32[]{:S(2)}) copy-start(f32[1,8,128,256]{2,1,3,0:T(8,128)S(1)} %convolution_bitcast_fusion.1) | copy-start | bytes 3145732
  211.8 5.4 %copy-start = (f32[2,8,128,256]{2,1,3,0:T(8,128)}, f32[2,8,128,256]{2,1,3,0:T(8,128)S(1)}, u32[]{:S(2)}) copy-start(f32[2,8,128,256]{2,1,3,0:T(8,128)S(1)} %convolution_bitcast_fusion) | copy-start | bytes 6291460
  220.2 36.9 %collective-permute-start.2 = (f32[3,8,1,256]{3,1,2,0:T(8,128)}, f32[3,8,1,256]{3,1,2,0:T(8,128)}, u32[]{:S(2)}, u32[]{:S(2)}) collective-permute-start(f32[3,8,1,256]{3,1,2,0:T(8,128)} %copy.158), channel_id=1, source_target_pairs={{0,8},{8,16},{16,24},{24,32},{32,40},{40,48},{48,56},{56,64},{64,7... | collective-permute-start | bytes 73736 | tf_op jit(solution)/shard_map/ppermute | solution.py:21
  220.2 11.5 %copy-start.15 = (f32[2,8,2,256]{3,1,2,0:T(8,128)S(1)}, f32[2,8,2,256]{3,1,2,0:T(8,128)}, u32[]{:S(2)}) copy-start(f32[2,8,2,256]{3,1,2,0:T(8,128)} %copy-done.13) | copy-start | bytes 98308
  222.6 37.4 %collective-permute-start.3 = (f32[3,8,1,256]{3,1,2,0:T(8,128)S(1)}, f32[3,8,1,256]{3,1,2,0:T(8,128)}, u32[]{:S(2)}, u32[]{:S(2)}) collective-permute-start(f32[3,8,1,256]{3,1,2,0:T(8,128)S(1)} %copy.163), channel_id=1, source_target_pairs={{8,0},{16,8},{24,16},{32,24},{40,32},{48,40},{56,48},{64,56},{72,6... | collective-permute-start | bytes 73736 | tf_op jit(solution)/shard_map/ppermute | solution.py:24
  229.2 4.2 %copy-start.3 = (f32[2,8,132,2]{3,1,2,0:T(8,128)}, f32[2,8,132,2]{3,1,2,0:T(8,128)S(1)}, u32[]{:S(2)}) copy-start(f32[2,8,132,2]{3,1,2,0:T(8,128)S(1)} %copy.169) | copy-start | bytes 50692
  238.0 3.7 %copy-start.9 = (f32[128,256]{0,1:T(8,128)S(1)}, f32[128,256]{0,1:T(8,128)}, u32[]{:S(2)}) copy-start(f32[128,256]{0,1:T(8,128)} %copy-done.8) | copy-start | bytes 393220
  238.0 3.7 %copy-start.11 = (f32[128,256]{0,1:T(8,128)S(1)}, f32[128,256]{0,1:T(8,128)}, u32[]{:S(2)}) copy-start(f32[128,256]{0,1:T(8,128)} %copy-done.10) | copy-start | bytes 393220
  248.3 6.4 %copy-start.20 = (f32[3,8,128,1]{2,1,3,0:T(8,128)}, f32[3,8,128,1]{2,1,3,0:T(8,128)S(1)}, u32[]{:S(2)}) copy-start(f32[3,8,128,1]{2,1,3,0:T(8,128)S(1)} %fusion.89) | copy-start | bytes 36868
  248.3 14.7 %collective-permute-start.6 = (f32[3,8,128,1]{2,1,3,0:T(8,128)S(1)}, f32[3,8,128,1]{2,1,3,0:T(8,128)S(1)}, u32[]{:S(2)}, u32[]{:S(2)}) collective-permute-start(f32[3,8,128,1]{2,1,3,0:T(8,128)S(1)} %fusion.89), channel_id=1, source_target_pairs={{0,1},{1,2},{2,3},{3,4},{4,5},{5,6},{6,7},{7,0},{8,9},{9,10},{10,1... | collective-permute-start | bytes 36872 | tf_op jit(solution)/shard_map/ppermute | solution.py:21
  260.1 3.0 copy-start.22
  263.6 19.0 %collective-permute-start.7 = (f32[3,8,128,1]{2,1,3,0:T(8,128)}, f32[3,8,128,1]{2,1,3,0:T(8,128)}, u32[]{:S(2)}, u32[]{:S(2)}) collective-permute-start(f32[3,8,128,1]{2,1,3,0:T(8,128)} %get-tuple-element.53), channel_id=1, source_target_pairs={{1,0},{2,1},{3,2},{4,3},{5,4},{6,5},{7,6},{0,7},{9,8},{10,9},{11,1... | collective-permute-start | bytes 36872 | tf_op jit(solution)/shard_map/ppermute | solution.py:24
  (10 other events, 17.5 us)
where the time goes:
time: 306 us; the launch traced here: 302 us
  other arithmetic  189 us (62%)
  local copies, waits for them, and re-layouts  70.9 us (23%)
  matrix products  20 us (7%)
  starting transfers between devices  18.4 us (6%)
  between operations  4.04 us (1%)
    another operation x18, other arithmetic, line_inverse(): factor = jnp.linalg.cholesky(matrix)  92.9 us
    another operation x9, other arithmetic, line_inverse(): jax.scipy.linalg.cho_solve((factor, True), jnp.eye(cells, dtype=jnp.float...  60.9 us
    ppermute x4, starting transfers between devices, extended(): lax.ppermute(lax.slice_in_dim(block, 0, width, axis=dim), axis, backward)  15.9 us
    mul x2, local copies, waits for them, and re-layouts, along_line(): return as_column(columns, axis_dim) * jnp.expand_dims(values, axis_dim)  12.7 us
    unnamed x59, local copies, waits for them, and re-layouts  10.2 us
    another operation x17, local copies, waits for them, and re-layouts, line_inverse(): jax.scipy.linalg.cho_solve((factor, True), jnp.eye(cells, dtype=jnp.float...  8.44 us
    sub x1, other arithmetic, coupled_lines(): local_lines - gains * (along_line(inverses[:, :, 0], left_end, axis_dim)...  8.05 us
    slice x3, local copies, waits for them, and re-layouts, extended(): lax.slice_in_dim(block, block.shape[dim] - width, None, axis=dim)  7.12 us
  transfers between devices with their start and end apart: 8, of which 0 were waited for; matrix products, arithmetic and copies ran while one was open for 83% of the time, Pallas kernels for 0%

commit v1 on v0

v1 whole, which is shorter than its diff:
```python
import functools

import jax
import jax.numpy as jnp
import numpy as np
from jax import lax
from jax.experimental import pallas as pl
from jax.experimental.pallas import tpu as pltpu
from jax.sharding import PartitionSpec as P

FIRST_ALPHA = 1.0 / 3.0
FIRST_A = 14.0 / 9.0
FIRST_B = 1.0 / 9.0
SECOND_ALPHA = 2.0 / 11.0
SECOND_A = 12.0 / 11.0
SECOND_B = 3.0 / 11.0
MESH = pl.DeviceIdType.MESH
STRIP = 24
REACH = 32
FULL = 128


class Line:
    def __init__(self, alpha, taps):
        root = np.sqrt(1.0 - 4.0 * alpha * alpha)
        self.rho = (root - 1.0) / (2.0 * alpha)
        self.root, self.taps = root, taps
        self.ahead = sum(c * self.rho**m for m, c in taps.items()) / root
        self.behind = sum(c * self.rho**-m for m, c in taps.items()) / root

    def weight(self, n):
        n = np.asarray(n)
        return sum(c * self.rho ** np.abs(n + m) for m, c in self.taps.items()) / self.root

    def local(self, cells):
        i = np.arange(cells)
        table = self.weight(i[:, None] - i[None, :])
        table[:, cells - 1] = 0.0
        return table

    def low_sum(self, reach):
        power = self.rho ** np.arange(reach - 1)
        weights = np.zeros(reach)
        weights[1:] += power
        weights[:-1] -= power
        return weights


FIRST = Line(
    FIRST_ALPHA,
    {
        1: 0.25 * FIRST_B,
        0: 0.5 * FIRST_A + 0.25 * FIRST_B,
        -1: 0.5 * FIRST_A + 0.25 * FIRST_B,
        -2: 0.25 * FIRST_B,
    },
)
SECOND = Line(
    SECOND_ALPHA,
    {
        1: 0.25 * SECOND_B,
        0: SECOND_A + 0.25 * SECOND_B,
        -1: -SECOND_A - 0.25 * SECOND_B,
        -2: -0.25 * SECOND_B,
    },
)


def halves(table):
    high = np.asarray(table, np.float32).astype(jnp.bfloat16)
    low = (table - high.astype(np.float64)).astype(np.float32).astype(jnp.bfloat16)
    return high, low


def sum_tables(reach):
    rows = [FIRST.low_sum(reach), SECOND.low_sum(reach)]
    rows += [-row[::-1] for row in rows]
    return np.repeat(np.stack(rows)[:, :, None], 128, axis=2).astype(np.float32)


def x_table(cells):
    rows = []
    for line in (FIRST, SECOND):
        for half in halves(line.local(cells)):
            rows.append(np.concatenate([half, half], axis=1))
    return np.concatenate(rows, axis=0)


def y_table(cells):
    columns = []
    for line in (FIRST, SECOND):
        high, low = halves(line.local(cells).T)
        columns.append(np.concatenate([high, high, low], axis=0))
    return np.concatenate(columns, axis=1)


def y_edge_table(cells):
    i = np.arange(cells)
    table = np.zeros((16, 3 * cells))
    for line, sum_row, edge_row, place in (
        (FIRST, 0, 2, 0),
        (SECOND, 1, 2, 1),
        (FIRST, 3, 4, 2),
    ):
        span = slice(place * cells, (place + 1) * cells)
        table[sum_row, span] = line.ahead * line.rho ** (i + 2)
        table[edge_row, span] = line.weight(i + 1)
        table[8 + sum_row, span] = line.behind * line.rho ** (cells - i)
        table[8 + edge_row, span] = line.weight(i - cells + 1)
    high, low = halves(table)
    blank = np.zeros((FULL - 48, 3 * cells), high.dtype)
    return np.concatenate([high, high, low, blank], axis=0)


def x_edge_table():
    r = np.arange(STRIP)
    table = np.zeros((2, 4, STRIP))
    for k, line in enumerate((FIRST, SECOND)):
        table[0, k] = line.ahead * line.rho ** (r + 1)
        table[0, 2 + k, 0] = line.weight(1) - line.ahead * line.rho
        table[1, k] = (line.behind * line.rho**r)[::-1]
        table[1, 2 + k, STRIP - 1] = line.weight(0) - line.behind
    return np.repeat(table[:, :, :, None], 128, axis=3).astype(np.float32)


def split(values):
    high = values.astype(jnp.bfloat16)
    low = (values - high.astype(jnp.float32)).astype(jnp.bfloat16)
    return high, low


def matmul(left, right):
    return jnp.dot(left, right, preferred_element_type=jnp.float32)


def twice(tile):
    return jnp.concatenate([tile, tile], axis=1)


def exchange_kernel(
    counts,
    f_hbm,
    k_hbm,
    tx_hbm,
    ty_hbm,
    hx_hbm,
    hy_hbm,
    wy_hbm,
    gx,
    gy,
    dif,
    kx,
    kap,
    xc,
    fld,
    tx,
    ty,
    hx,
    hy,
    wy,
    curv,
    ky,
    xs,
    xr,
    ys,
    yr,
    in_sem,
    send_sem,
    recv_sem,
):
    planes, cells_x, cells_y = fld.shape
    top = cells_x - STRIP
    ix, iy = lax.axis_index("gx"), lax.axis_index("gy")
    nx, ny = counts
    left = (lax.rem(ix + nx - 1, nx), iy)
    right = (lax.rem(ix + 1, nx), iy)
    below = (ix, lax.rem(iy + ny - 1, ny))
    above = (ix, lax.rem(iy + 1, ny))

    barrier = pltpu.get_barrier_semaphore()
    for neighbour in (left, right, below, above):
        pl.semaphore_signal(barrier, inc=1, device_id=neighbour, device_id_type=MESH)

    loads = []

    def load(source, target):
        copy = pltpu.make_async_copy(source, target, in_sem.at[len(loads)])
        copy.start()
        loads.append(copy)
        return copy

    first_loads = [load(tx_hbm, tx)]
    for rows in (pl.ds(0, STRIP), pl.ds(top, STRIP)):
        first_loads.append(load(f_hbm.at[:, rows, :], fld.at[:, rows, :]))
        first_loads.append(load(k_hbm.at[:, rows, :], kap.at[:, rows, :]))
    middle = pl.ds(STRIP, top - STRIP)
    next_loads = [
        load(ty_hbm, ty),
        load(f_hbm.at[:, middle, :], fld.at[:, middle, :]),
        load(k_hbm.at[:, middle, :], kap.at[:, middle, :]),
    ]
    last_loads = [load(hx_hbm, hx), load(hy_hbm, hy), load(wy_hbm, wy)]
    ys[:, :, 5:8, :] = jnp.zeros((2, planes, 3, 128), jnp.float32)

    for copy in first_loads:
        copy.wait()
    for side, start in ((0, 0), (1, top)):
        edge = 0 if side == 0 else cells_x - 1
        with_first, with_second = twice(tx[2 * side]), twice(tx[2 * side + 1])
        for p in range(planes):
            rows = fld[p, start : start + STRIP, :]
            krows = kap[p, start : start + STRIP, :]
            xs[side, 0, p : p + 1, :] = jnp.sum(rows * with_first, axis=0, keepdims=True)
            xs[side, 1, p : p + 1, :] = jnp.sum(rows * with_second, axis=0, keepdims=True)
            xs[side, 2, p : p + 1, :] = fld[p, edge : edge + 1, :]
            xs[side, 3, p : p + 1, :] = jnp.sum(krows * with_first, axis=0, keepdims=True)
            xs[side, 4, p : p + 1, :] = kap[p, edge : edge + 1, :]

    for copy in next_loads:
        copy.wait()
    lane = lax.broadcasted_iota(jnp.int32, (cells_x, 128), 1)
    for p in range(planes):
        f_low, f_high = fld[p, :, 0:128], fld[p, :, cells_y - 128 : cells_y]
        k_low, k_high = kap[p, :, 0:128], kap[p, :, cells_y - 128 : cells_y]
        packed = jnp.where(
            lane < REACH,
            f_low,
            jnp.where(
                lane < 2 * REACH,
                pltpu.roll(k_low, REACH, 1),
                jnp.where(lane < 3 * REACH, pltpu.roll(k_high, 128 - REACH, 1), f_high),
            ),
        )
        turned = packed.T
        for side, f_part, k_part, f_edge, k_edge in (
            (0, turned[0:32], turned[32:64], turned[0:1], turned[32:33]),
            (1, turned[96:128], turned[64:96], turned[127:128], turned[95:96]),
        ):
            with_first, with_second = ty[2 * side], ty[2 * side + 1]
            ys[side, p, 0:1, :] = jnp.sum(f_part * with_first, axis=0, keepdims=True)
            ys[side, p, 1:2, :] = jnp.sum(f_part * with_second, axis=0, keepdims=True)
            ys[side, p, 2:3, :] = f_edge
            ys[side, p, 3:4, :] = jnp.sum(k_part * with_first, axis=0, keepdims=True)
            ys[side, p, 4:5, :] = k_edge

    pl.semaphore_wait(barrier, 4)
    copies = []
    for place, (source, target, device) in enumerate(
        (
            (xs.at[0], xr.at[1], left),
            (xs.at[1], xr.at[0], right),
            (ys.at[0], yr.at[1], below),
            (ys.at[1], yr.at[0], above),
        )
    ):
        copy = pltpu.make_async_remote_copy(
            src_ref=source,
            dst_ref=target,
            send_sem=send_sem.at[place],
            recv_sem=recv_sem.at[place],
            device_id=device,
            device_id_type=MESH,
        )
        copy.start()
        copies.append(copy)

    for copy in last_loads:
        copy.wait()

    def local_pair(pair, carry):
        tall, ktall = [], []
        for q in range(2):
            p = 2 * pair + q
            f, k = fld[p], kap[p]
            high, low = split(pltpu.roll(f, cells_x - 1, 0) - f)
            along = matmul(hx[...], jnp.concatenate([high, low], axis=0))
            gx[p] = along[0:cells_x] + along[cells_x : 2 * cells_x]
            curv[p] = along[2 * cells_x : 3 * cells_x] + along[3 * cells_x : 4 * cells_x]
            high, low = split(pltpu.roll(k, cells_x - 1, 0) - k)
            along = matmul(hx[0 : 2 * cells_x, :], jnp.concatenate([high, low], axis=0))
            kx[p] = along[0:cells_x] + along[cells_x : 2 * cells_x]
            high, low = split(pltpu.roll(f, cells_y - 1, 1) - f)
            tall.append(jnp.concatenate([high, low, high], axis=1))
            high, low = split(pltpu.roll(k, cells_y - 1, 1) - k)
            ktall.append(jnp.concatenate([high, low, high], axis=1))
        across = matmul(jnp.concatenate(tall, axis=0), hy[...])
        kacross = matmul(jnp.concatenate(ktall, axis=0), hy[:, 0:cells_y])
        for q in range(2):
            p = 2 * pair + q
            rows = slice(q * cells_x, (q + 1) * cells_x)
            gy[p] = across[rows, 0:cells_y]
            curv[p] = curv[p] + across[rows, cells_y : 2 * cells_y]
            ky[p] = kacross[rows]
        return carry

    lax.fori_loop(0, planes // 2, local_pair, 0)

    copies[2].wait_recv()
    copies[3].wait_recv()
    row = lax.broadcasted_iota(jnp.int32, (8, 128), 0)
    is_edge = (row == 2) | (row == 4)

    def finish_plane(p, carry):
        from_below, from_above = yr[0, p], yr[1, p]
        from_below = jnp.where(is_edge, ys[0, p] - from_below, from_below)
        from_above = jnp.where(is_edge, from_above - ys[1, p], from_above)
        ends = jnp.concatenate([from_below, from_above], axis=0)
        high = ends.astype(jnp.bfloat16).astype(jnp.float32)
        stack = jnp.concatenate(
            [high, ends - high, high, jnp.zeros((FULL - 48, cells_x), jnp.float32)], axis=0
        )
        reach = matmul(stack.T.astype(jnp.bfloat16), wy[...])
        grad = gy[p] + reach[:, 0:cells_y]
        gy[p] = grad
        kappa = kap[p]
        part = kappa * (curv[p] + reach[:, cells_y : 2 * cells_y]) + (
            ky[p] + reach[:, 2 * cells_y :]
        ) * grad
        inner = slice(STRIP, top)
        dif[p, 0:STRIP, :] = part[0:STRIP]
        dif[p, inner, :] = part[inner] + kx[p, inner, :] * gx[p, inner, :]
        dif[p, top:, :] = part[top:]
        return carry

    lax.fori_loop(0, planes, finish_plane, 0)

    copies[0].wait_recv()
    copies[1].wait_recv()
    for side in range(2):
        sign = 1.0 if side == 0 else -1.0
        jump = sign * (xs[side, 2] - xr[side, 2])
        kjump = sign * (xs[side, 4] - xr[side, 4])
        xc[side, 0] = FIRST.rho * xr[side, 0] + jump
        xc[side, 1] = SECOND.rho * xr[side, 1] + jump
        xc[side, 2] = jump
        xc[side, 3] = FIRST.rho * xr[side, 3] + kjump
        xc[side, 4] = kjump
    for copy in copies:
        copy.wait_send()


def finish_kernel(gx, gy, dif, kx, kap, xc, wx, gx_out, gy_out, dif_out, gs, ds, sem):
    planes, cells_x, cells_y = gx.shape
    top = cells_x - STRIP
    middle = pl.ds(STRIP, top - STRIP)
    copies = []

    def store(source, target):
        copy = pltpu.make_async_copy(source, target, sem.at[len(copies)])
        copy.start()
        copies.append(copy)

    store(gy, gy_out)
    store(gx.at[:, middle, :], gx_out.at[:, middle, :])
    store(dif.at[:, middle, :], dif_out.at[:, middle, :])
    for side, start in ((0, 0), (1, top)):
        rows = slice(start, start + STRIP)
        decay, decay_second, end, end_second = (twice(wx[side, k]) for k in range(4))
        for p in range(planes):
            first, second, jump, kfirst, kjump = (xc[side, k, p : p + 1, :] for k in range(5))
            grad = gx[p, rows, :] + decay * first + end * jump
            bend = decay_second * second + end_second * jump
            kgrad = kx[p, rows, :] + decay * kfirst + end * kjump
            gs[side, p] = grad
            ds[side, p] = dif[p, rows, :] + kap[p, rows, :] * bend + kgrad * grad
        store(gs.at[side], gx_out.at[:, pl.ds(start, STRIP), :])
        store(ds.at[side], dif_out.at[:, pl.ds(start, STRIP), :])
    for copy in copies:
        copy.wait()


def local(counts, scalar, diffusivity):
    block = scalar.shape
    planes, cells_x, cells_y = block
    tables = (
        jnp.asarray(sum_tables(STRIP)),
        jnp.asarray(sum_tables(REACH)),
        jnp.asarray(x_table(cells_x)),
        jnp.asarray(y_table(cells_y)),
        jnp.asarray(y_edge_table(cells_y)),
    )
    vmem, hbm = pl.BlockSpec(memory_space=pltpu.VMEM), pl.BlockSpec(memory_space=pltpu.HBM)
    field = jax.ShapeDtypeStruct(block, jnp.float32)
    field_buffer = pltpu.VMEM(block, jnp.float32)
    parts = pl.pallas_call(
        functools.partial(exchange_kernel, counts),
        out_shape=(field,) * 5 + (jax.ShapeDtypeStruct((2, 5, planes, cells_y), jnp.float32),),
        in_specs=[hbm] * 7,
        out_specs=(vmem,) * 6,
        scratch_shapes=[field_buffer]
        + [pltpu.VMEM(table.shape, table.dtype) for table in tables]
        + [field_buffer, field_buffer]
        + [pltpu.VMEM((2, 5, planes, cells_y), jnp.float32)] * 2
        + [pltpu.VMEM((2, planes, 8, cells_x), jnp.float32)] * 2
        + [
            pltpu.SemaphoreType.DMA((11,)),
            pltpu.SemaphoreType.DMA((4,)),
            pltpu.SemaphoreType.DMA((4,)),
        ],
        compiler_params=pltpu.CompilerParams(
            collective_id=0, has_side_effects=True, vmem_limit_bytes=28 * 1024 * 1024
        ),
        name="exchange",
    )(*(pltpu.with_memory_space_constraint(array, pltpu.HBM) for array in (scalar, diffusivity) + tables))
    strip_buffer = pltpu.VMEM((2, planes, STRIP, cells_y), jnp.float32)
    return pl.pallas_call(
        finish_kernel,
        out_shape=(field,) * 3,
        in_specs=[vmem] * 7,
        out_specs=(hbm,) * 3,
        scratch_shapes=[strip_buffer, strip_buffer, pltpu.SemaphoreType.DMA((7,))],
        compiler_params=pltpu.CompilerParams(vmem_limit_bytes=28 * 1024 * 1024),
        name="finish",
    )(*parts, jnp.asarray(x_edge_table()))


def solution(mesh):
    placed = P(None, "gx", "gy")
    return jax.shard_map(
        functools.partial(local, (mesh.shape["gx"], mesh.shape["gy"])),
        mesh=mesh,
        in_specs=(placed, placed),
        out_specs=(placed,) * 3,
        check_vma=False,
    )
```

time: 306 us -> 17.6 us (0.06); the launches traced: 302 us -> 17.5 us
  other arithmetic: 189 us -> 0 us
  local copies, waits for them, and re-layouts: 70.9 us -> 0.01 us
  matrix products: 20 us -> 0 us
  starting transfers between devices: 18.4 us -> 0 us
  Pallas kernels: 0 us -> 16.9 us
  between operations: 4.04 us -> 0.65 us
    another operation x30 -> x0, other arithmetic: 154 us -> none  [the longest x18 92.9 us: line_inverse(): factor = jnp.linalg.cholesky(matrix)]
    ppermute x8 -> x0, starting transfers between devices: 18.4 us -> none  [the longest x4 15.9 us: extended(): lax.ppermute(lax.slice_in_dim(block, 0, width, axis=dim), axis, backward)]
    mul x4 -> x0, local copies, waits for them, and re-layouts: 17.4 us -> none  [the longest x2 12.7 us: along_line(): return as_column(columns, axis_dim) * jnp.expand_dims(values, axis_dim)]
    pallas_call x0 -> x2, Pallas kernels: none -> 16.9 us  [the longest x1 15.1 us: local(): pl.pallas_call(functools.partial(exchange_kernel, counts), out_shape=(fie...]
    dot_general x4 -> x0, matrix products: 12.6 us -> none  [the longest x1 4.28 us: solve_lines_y(): jnp.einsum('cpkj,ij->cpki', first_rhs(along_y, 3, row_count), inverse_fir...]
    mul x5 -> x0, other arithmetic: 12.5 us -> none  [the longest x1 5.39 us: pair_values(): right_end = (next_first - pair_gain * own_last) * scale]
    slice x5 -> x0, local copies, waits for them, and re-layouts: 12 us -> none  [the longest x3 7.12 us: extended(): lax.slice_in_dim(block, block.shape[dim] - width, None, axis=dim)]
    another operation x22 -> x0, local copies, waits for them, and re-layouts: 11.2 us -> none  [the longest x17 8.44 us: line_inverse(): jax.scipy.linalg.cho_solve((factor, True), jnp.eye(cells, dtype=jnp.float...]
  transfers between devices with their start and end apart: 8 -> 0, of which waited for: 0 -> 0; matrix products, arithmetic and copies ran while one was open for 83% -> 0% of each run, Pallas kernels for 0% -> 0%
where the time goes in v1:
time: 17.6 us; the launch traced here: 17.5 us
  Pallas kernels  16.9 us (96%)
  between operations  0.65 us (4%)
    pallas_call x1, Pallas kernels, local(): pl.pallas_call(functools.partial(exchange_kernel, counts), out_shape=(fie...  15.1 us
    pallas_call x1, Pallas kernels, local(): pl.pallas_call(finish_kernel, out_shape=(field,) * 3, in_specs=[vmem] * 7...  1.71 us

profile of v1, /device:TPU:1, one launch (start us, length us, event | category | flops | bytes accessed | tf_op | source)
XLA Modules:
  0.0 17.5 jit_solution(5471954939675590729)
XLA Ops:
  0.6 0.0 copy-start
  0.6 15.1 %exchange.1 = (f32[8,128,256]{2,1,0:T(8,128)S(1)}, f32[8,128,256]{2,1,0:T(8,128)S(1)}, f32[8,128,256]{2,1,0:T(8,128)S(1)}, f32[8,128,256]{2,1,0:T(8,128)S(1)}, f...) custom-call(f32[8,128,256]{2,1,0:T(8,128)} %f_hbm.1, f32[8,128,256]{2,1,0:T(8,128)} %k_hbm.1, ...), custom_call_target="tpu_custom_call" | custom-call | tf_op jit(solution)/shard_map/exchange/pallas_call | solution.py:385
  15.8 0.0 copy-done
  15.8 1.7 %finish.1 = (f32[8,128,256]{2,1,0:T(8,128)}, f32[8,128,256]{2,1,0:T(8,128)}, f32[8,128,256]{2,1,0:T(8,128)}) custom-call(f32[8,128,256]{2,1,0:T(8,128)S(1)} %get-tuple-element.9.gx, f32[8,128,256]{2,1,0:T(8,128)S(1)} %get-tuple-element.10.gy, f32[8,128,256]{2,1,0:T(8,128)S(1)} %get-tuple-element.11.dif, f32[8,128,256]{2,1,0:T(8,128)S(1)} %get-tuple-element.12.kx, ...), custom_call_target="tpu_custom_call" | custom-call | tf_op jit(solution)/shard_map/finish/pallas_call | solution.py:406
Async XLA Ops:
  0.6 15.2 %copy-start = (f32[2,4,24,128]{3,2,1,0:T(8,128)S(1)}, f32[2,4,24,128]{3,2,1,0:T(8,128)}, u32[]{:S(2)}) copy-start(f32[2,4,24,128]{3,2,1,0:T(8,128)} %constant.17.clone.wx) | copy-start | bytes 294916

commit v2 on v1

v2 whole, which is shorter than its diff:
```python
import functools

import jax
import jax.numpy as jnp
import numpy as np
from jax import lax
from jax.experimental import pallas as pl
from jax.experimental.pallas import tpu as pltpu
from jax.sharding import PartitionSpec as P

FIRST_ALPHA = 1.0 / 3.0
FIRST_A = 14.0 / 9.0
FIRST_B = 1.0 / 9.0
SECOND_ALPHA = 2.0 / 11.0
SECOND_A = 12.0 / 11.0
SECOND_B = 3.0 / 11.0
MESH = pl.DeviceIdType.MESH
STRIP = 24
REACH = 32
FULL = 128


class Line:
    def __init__(self, alpha, taps):
        root = np.sqrt(1.0 - 4.0 * alpha * alpha)
        self.rho = (root - 1.0) / (2.0 * alpha)
        self.root, self.taps = root, taps
        self.ahead = sum(c * self.rho**m for m, c in taps.items()) / root
        self.behind = sum(c * self.rho**-m for m, c in taps.items()) / root

    def weight(self, n):
        n = np.asarray(n)
        return sum(c * self.rho ** np.abs(n + m) for m, c in self.taps.items()) / self.root

    def local(self, cells):
        i = np.arange(cells)
        table = self.weight(i[:, None] - i[None, :])
        table[:, cells - 1] = 0.0
        return table

    def low_sum(self, reach):
        power = self.rho ** np.arange(reach - 1)
        weights = np.zeros(reach)
        weights[1:] += power
        weights[:-1] -= power
        return weights


FIRST = Line(
    FIRST_ALPHA,
    {
        1: 0.25 * FIRST_B,
        0: 0.5 * FIRST_A + 0.25 * FIRST_B,
        -1: 0.5 * FIRST_A + 0.25 * FIRST_B,
        -2: 0.25 * FIRST_B,
    },
)
SECOND = Line(
    SECOND_ALPHA,
    {
        1: 0.25 * SECOND_B,
        0: SECOND_A + 0.25 * SECOND_B,
        -1: -SECOND_A - 0.25 * SECOND_B,
        -2: -0.25 * SECOND_B,
    },
)


def halves(table):
    high = np.asarray(table, np.float32).astype(jnp.bfloat16)
    low = (table - high.astype(np.float64)).astype(np.float32).astype(jnp.bfloat16)
    return high, low


def stacked(columns):
    table = np.zeros((len(columns), 32, 128), np.float32)
    for place, column in enumerate(columns):
        table[place, : len(column)] = column[:, None]
    return table


def sum_columns(reach):
    low = [FIRST.low_sum(reach), SECOND.low_sum(reach)]
    return [-row[::-1] for row in low] + low


def high_end_columns():
    r = np.arange(STRIP)[::-1]
    columns = [(line.behind * line.rho**r) for line in (FIRST, SECOND)]
    for line in (FIRST, SECOND):
        column = np.zeros(8)
        column[7] = line.weight(0) - line.behind
        columns.append(column)
    return columns


def low_end_columns():
    r = np.arange(STRIP)
    columns = [(line.ahead * line.rho ** (r + 1)) for line in (FIRST, SECOND)]
    for line in (FIRST, SECOND):
        column = np.zeros(8)
        column[0] = line.weight(1) - line.ahead * line.rho
        columns.append(column)
    return columns


def x_table(cells):
    rows = []
    for line in (FIRST, SECOND):
        for half in halves(line.local(cells)):
            rows.append(np.concatenate([half, half], axis=1))
    return np.concatenate(rows, axis=0)


def y_table(cells):
    rows = []
    for line in (FIRST, SECOND):
        high, low = halves(line.local(cells).T)
        rows += [high, high, low]
    return np.concatenate(rows, axis=0)


def y_end_table(cells):
    i = np.arange(cells)
    blocks = []
    for line, sum_row, edge_row in ((FIRST, 0, 2), (SECOND, 1, 2), (FIRST, 3, 4)):
        table = np.zeros((16, cells))
        table[sum_row] = line.ahead * line.rho ** (i + 2)
        table[edge_row] = line.weight(i + 1)
        table[8 + sum_row] = line.behind * line.rho ** (cells - i)
        table[8 + edge_row] = line.weight(i - cells + 1)
        high, low = halves(table)
        blank = np.zeros((FULL - 48, cells), high.dtype)
        blocks += [high, high, low, blank]
    return np.concatenate(blocks, axis=0)


def split(values):
    high = values.astype(jnp.bfloat16)
    low = (values - high.astype(jnp.float32)).astype(jnp.bfloat16)
    return high, low


def matmul(left, right):
    return jnp.dot(left, right, preferred_element_type=jnp.float32)


def twice(tile):
    return jnp.concatenate([tile, tile], axis=1)


def ends_applied(side, grad, kgrad, part, kappa, columns, values):
    decay, decay_second, end, end_second = columns
    first, second, jump, kfirst, kjump = values
    grads, parts = [], []
    for tile in range(STRIP // 8):
        r = slice(8 * tile, 8 * tile + 8)
        g = grad[r] + decay[r] * first
        k = kgrad[r] + decay[r] * kfirst
        distance = tile if side == 0 else STRIP // 8 - 1 - tile
        d = part[r]
        if distance < 2:
            bend = decay_second[r] * second
            if distance == 0:
                g = g + end * jump
                k = k + end * kjump
                bend = bend + end_second * jump
            d = d + kappa[r] * bend
        grads.append(g)
        parts.append(d + k * g)
    return jnp.concatenate(grads, axis=0), jnp.concatenate(parts, axis=0)


def exchange_kernel(
    counts,
    f_hbm,
    k_hbm,
    tab_hbm,
    mats_hbm,
    gx,
    gy,
    dif,
    kx,
    kap,
    xc,
    fld,
    tab,
    mats,
    curv,
    ky,
    xs,
    xr,
    ys,
    yr,
    xh,
    in_sem,
    send_sem,
    recv_sem,
    left_ready,
    above_ready,
):
    planes, cells_x, cells_y = fld.shape
    top = cells_x - STRIP
    loads = []

    def load(source, target):
        copy = pltpu.make_async_copy(source, target, in_sem.at[len(loads)])
        copy.start()
        loads.append(copy)
        return copy

    def load_rows(rows):
        return [
            load(f_hbm.at[:, rows, :], fld.at[:, rows, :]),
            load(k_hbm.at[:, rows, :], kap.at[:, rows, :]),
        ]

    high_loads = load_rows(pl.ds(top, STRIP)) + [load(tab_hbm, tab)]
    low_loads = load_rows(pl.ds(0, STRIP))
    middle_loads = load_rows(pl.ds(STRIP, top - STRIP))
    table_load = load(mats_hbm, mats)

    ix, iy = lax.axis_index("gx"), lax.axis_index("gy")
    nx, ny = counts
    left = (jnp.where(ix == 0, nx - 1, ix - 1), iy)
    right = (jnp.where(ix == nx - 1, 0, ix + 1), iy)
    below = (ix, jnp.where(iy == 0, ny - 1, iy - 1))
    above = (ix, jnp.where(iy == ny - 1, 0, iy + 1))
    barrier = pltpu.get_barrier_semaphore()
    for neighbour in (left, above):
        pl.semaphore_signal(barrier, inc=1, device_id=neighbour, device_id_type=MESH)

    def send(place, source, target, device):
        copy = pltpu.make_async_remote_copy(
            src_ref=source,
            dst_ref=target,
            send_sem=send_sem.at[place],
            recv_sem=recv_sem.at[place],
            device_id=device,
            device_id_type=MESH,
        )
        copy.start()
        return copy

    def sum_x_edge(side, start, edge, place):
        with_first, with_second = twice(tab[place, 0:STRIP]), twice(tab[place + 1, 0:STRIP])
        for p in range(planes):
            rows = fld[p, start : start + STRIP, :]
            krows = kap[p, start : start + STRIP, :]
            xs[side, 0, p : p + 1, :] = jnp.sum(rows * with_first, axis=0, keepdims=True)
            xs[side, 1, p : p + 1, :] = jnp.sum(rows * with_second, axis=0, keepdims=True)
            xs[side, 2, p : p + 1, :] = fld[p, edge : edge + 1, :]
            xs[side, 3, p : p + 1, :] = jnp.sum(krows * with_first, axis=0, keepdims=True)
            xs[side, 4, p : p + 1, :] = kap[p, edge : edge + 1, :]

    for copy in high_loads:
        copy.wait()
    sum_x_edge(1, top, cells_x - 1, 0)
    pl.semaphore_wait(barrier, 2)
    to_right = send(1, xs.at[1], xr.at[0], right)
    pl.semaphore_signal(left_ready, inc=1, device_id=right, device_id_type=MESH)
    pl.semaphore_signal(above_ready, inc=1, device_id=below, device_id_type=MESH)
    for copy in low_loads:
        copy.wait()
    sum_x_edge(0, 0, 0, 2)

    for copy in middle_loads:
        copy.wait()
    ys[:, :, 5:8, :] = jnp.zeros((2, planes, 3, 128), jnp.float32)
    lane = lax.broadcasted_iota(jnp.int32, (cells_x, 128), 1)
    for p in range(planes):
        f_low, f_high = fld[p, :, 0:128], fld[p, :, cells_y - 128 : cells_y]
        k_low, k_high = kap[p, :, 0:128], kap[p, :, cells_y - 128 : cells_y]
        packed = jnp.where(
            lane < REACH,
            f_low,
            jnp.where(
                lane < 2 * REACH,
                pltpu.roll(k_low, REACH, 1),
                jnp.where(lane < 3 * REACH, pltpu.roll(k_high, 128 - REACH, 1), f_high),
            ),
        )
        turned = packed.T
        for side, place, f_part, k_part, f_edge, k_edge in (
            (0, 6, turned[0:32], turned[32:64], turned[0:1], turned[32:33]),
            (1, 4, turned[96:128], turned[64:96], turned[127:128], turned[95:96]),
        ):
            with_first, with_second = tab[place], tab[place + 1]
            ys[side, p, 0:1, :] = jnp.sum(f_part * with_first, axis=0, keepdims=True)
            ys[side, p, 1:2, :] = jnp.sum(f_part * with_second, axis=0, keepdims=True)
            ys[side, p, 2:3, :] = f_edge
            ys[side, p, 3:4, :] = jnp.sum(k_part * with_first, axis=0, keepdims=True)
            ys[side, p, 4:5, :] = k_edge
    to_below = send(2, ys.at[0], yr.at[1], below)
    pl.semaphore_wait(above_ready, 1)
    to_above = send(3, ys.at[1], yr.at[0], above)

    table_load.wait()
    x_rows = 4 * cells_x
    y_first = slice(x_rows, x_rows + 3 * cells_y)
    y_second = slice(x_rows + 3 * cells_y, x_rows + 6 * cells_y)
    end_rows = x_rows + 6 * cells_y

    def local_pair(pair, carry):
        tall, ktall = [], []
        for q in range(2):
            p = 2 * pair + q
            f, k = fld[p], kap[p]
            high, low = split(pltpu.roll(f, cells_x - 1, 0) - f)
            along = matmul(mats[0:x_rows, :], jnp.concatenate([high, low], axis=0))
            gx[p] = along[0:cells_x] + along[cells_x : 2 * cells_x]
            curv[p] = along[2 * cells_x : 3 * cells_x] + along[3 * cells_x : 4 * cells_x]
            high, low = split(pltpu.roll(k, cells_x - 1, 0) - k)
            along = matmul(mats[0 : 2 * cells_x, :], jnp.concatenate([high, low], axis=0))
            kx[p] = along[0:cells_x] + along[cells_x : 2 * cells_x]
            high, low = split(pltpu.roll(f, cells_y - 1, 1) - f)
            tall.append(jnp.concatenate([high, low, high], axis=1))
            high, low = split(pltpu.roll(k, cells_y - 1, 1) - k)
            ktall.append(jnp.concatenate([high, low, high], axis=1))
        across = matmul(jnp.concatenate(tall + ktall, axis=0), mats[y_first, :])
        bend = matmul(jnp.concatenate(tall, axis=0), mats[y_second, :])
        for q in range(2):
            p = 2 * pair + q
            gy[p] = across[q * cells_x : (q + 1) * cells_x]
            ky[p] = across[(q + 2) * cells_x : (q + 3) * cells_x]
            curv[p] = curv[p] + bend[q * cells_x : (q + 1) * cells_x]
        return carry

    lax.fori_loop(0, planes // 2, local_pair, 0)

    pl.semaphore_wait(left_ready, 1)
    to_left = send(0, xs.at[0], xr.at[1], left)

    to_below.wait_recv()
    to_above.wait_recv()
    row = lax.broadcasted_iota(jnp.int32, (8, 128), 0)
    is_edge = (row == 2) | (row == 4)

    def finish_pair(pair, carry):
        stacks = []
        for q in range(2):
            p = 2 * pair + q
            from_below, from_above = yr[0, p], yr[1, p]
            from_below = jnp.where(is_edge, ys[0, p] - from_below, from_below)
            from_above = jnp.where(is_edge, from_above - ys[1, p], from_above)
            ends = jnp.concatenate([from_below, from_above], axis=0)
            high = ends.astype(jnp.bfloat16).astype(jnp.float32)
            blank = jnp.zeros((FULL - 48, cells_x), jnp.float32)
            stacks.append(jnp.concatenate([high, ends - high, high, blank], axis=0).T)
        turned = jnp.concatenate(stacks, axis=0).astype(jnp.bfloat16)
        reach = [
            matmul(turned, mats[end_rows + n * FULL : end_rows + (n + 1) * FULL, :]) for n in range(3)
        ]
        for q in range(2):
            p = 2 * pair + q
            rows = slice(q * cells_x, (q + 1) * cells_x)
            grad = gy[p] + reach[0][rows]
            gy[p] = grad
            part = kap[p] * (curv[p] + reach[1][rows]) + (ky[p] + reach[2][rows]) * grad
            inner = slice(STRIP, top)
            dif[p, 0:STRIP, :] = part[0:STRIP]
            dif[p, inner, :] = part[inner] + kx[p, inner, :] * gx[p, inner, :]
            dif[p, top:, :] = part[top:]
        return carry

    lax.fori_loop(0, planes // 2, finish_pair, 0)

    def combine(side, out):
        sign = 1.0 if side == 0 else -1.0
        jump = sign * (xs[side, 2] - xr[side, 2])
        kjump = sign * (xs[side, 4] - xr[side, 4])
        out[0] = FIRST.rho * xr[side, 0] + jump
        out[1] = SECOND.rho * xr[side, 1] + jump
        out[2] = jump
        out[3] = FIRST.rho * xr[side, 3] + kjump
        out[4] = kjump

    to_left.wait_recv()
    combine(1, xh)
    columns = [twice(tab[n, 0:STRIP]) for n in (8, 9)] + [twice(tab[n, 0:8]) for n in (10, 11)]
    for p in range(planes):
        gx[p, top:, :], dif[p, top:, :] = ends_applied(
            1,
            gx[p, top:, :],
            kx[p, top:, :],
            dif[p, top:, :],
            kap[p, top:, :],
            columns,
            [xh[n, p : p + 1, :] for n in range(5)],
        )
    for copy in (to_left, to_right, to_below, to_above):
        copy.wait_send()
    to_right.wait_recv()
    combine(0, xc)


def finish_kernel(gx, gy, dif, kx, kap, xc, tab, gx_out, gy_out, dif_out, gs, ds, sem):
    planes, cells_x, cells_y = gx.shape
    copies = []

    def store(source, target):
        copy = pltpu.make_async_copy(source, target, sem.at[len(copies)])
        copy.start()
        copies.append(copy)

    rest = pl.ds(STRIP, cells_x - STRIP)
    store(gy, gy_out)
    store(gx.at[:, rest, :], gx_out.at[:, rest, :])
    store(dif.at[:, rest, :], dif_out.at[:, rest, :])
    columns = [twice(tab[n, 0:STRIP]) for n in (0, 1)] + [twice(tab[n, 0:8]) for n in (2, 3)]
    for p in range(planes):
        gs[p], ds[p] = ends_applied(
            0,
            gx[p, 0:STRIP, :],
            kx[p, 0:STRIP, :],
            dif[p, 0:STRIP, :],
            kap[p, 0:STRIP, :],
            columns,
            [xc[n, p : p + 1, :] for n in range(5)],
        )
    store(gs, gx_out.at[:, pl.ds(0, STRIP), :])
    store(ds, dif_out.at[:, pl.ds(0, STRIP), :])
    for copy in copies:
        copy.wait()


def local(counts, scalar, diffusivity):
    block = scalar.shape
    planes, cells_x, cells_y = block
    columns = sum_columns(STRIP) + sum_columns(REACH) + high_end_columns()
    tables = (
        jnp.asarray(stacked(columns)),
        jnp.asarray(
            np.concatenate([x_table(cells_x), y_table(cells_y), y_end_table(cells_y)], axis=0)
        ),
    )
    vmem, hbm = pl.BlockSpec(memory_space=pltpu.VMEM), pl.BlockSpec(memory_space=pltpu.HBM)
    field = jax.ShapeDtypeStruct(block, jnp.float32)
    field_buffer = pltpu.VMEM(block, jnp.float32)
    ends_shape = (5, planes, cells_y)
    operands = [
        pltpu.with_memory_space_constraint(array, pltpu.HBM)
        for array in (scalar, diffusivity) + tables
    ]
    parts = pl.pallas_call(
        functools.partial(exchange_kernel, counts),
        out_shape=(field,) * 5 + (jax.ShapeDtypeStruct(ends_shape, jnp.float32),),
        in_specs=[hbm] * 4,
        out_specs=(vmem,) * 6,
        scratch_shapes=[field_buffer]
        + [pltpu.VMEM(table.shape, table.dtype) for table in tables]
        + [field_buffer, field_buffer]
        + [pltpu.VMEM((2,) + ends_shape, jnp.float32)] * 2
        + [pltpu.VMEM((2, planes, 8, cells_x), jnp.float32)] * 2
        + [
            pltpu.VMEM(ends_shape, jnp.float32),
            pltpu.SemaphoreType.DMA((8,)),
            pltpu.SemaphoreType.DMA((4,)),
            pltpu.SemaphoreType.DMA((4,)),
            pltpu.SemaphoreType.REGULAR,
            pltpu.SemaphoreType.REGULAR,
        ],
        compiler_params=pltpu.CompilerParams(
            collective_id=0, has_side_effects=True, vmem_limit_bytes=28 * 1024 * 1024
        ),
        name="exchange",
    )(*operands)
    strip_buffer = pltpu.VMEM((planes, STRIP, cells_y), jnp.float32)
    return pl.pallas_call(
        finish_kernel,
        out_shape=(field,) * 3,
        in_specs=[vmem] * 7,
        out_specs=(hbm,) * 3,
        scratch_shapes=[strip_buffer, strip_buffer, pltpu.SemaphoreType.DMA((5,))],
        compiler_params=pltpu.CompilerParams(vmem_limit_bytes=28 * 1024 * 1024),
        name="finish",
    )(*parts, jnp.asarray(stacked(low_end_columns())))


def solution(mesh):
    placed = P(None, "gx", "gy")
    return jax.shard_map(
        functools.partial(local, (mesh.shape["gx"], mesh.shape["gy"])),
        mesh=mesh,
        in_specs=(placed, placed),
        out_specs=(placed,) * 3,
        check_vma=False,
    )
```

time: 17.6 us -> 13.9 us (0.79)
  Pallas kernels: 16.9 us -> 13.1 us
    pallas_call x1, Pallas kernels: 15.1 us -> 11.4 us  [local(): pl.pallas_call(functools.partial(exchange_kernel, counts), out_shape=(fie...]
where the time goes in v2:
time: 13.9 us; the launch traced here: 13.8 us
  Pallas kernels  13.1 us (94%)
  between operations  0.65 us (5%)
    pallas_call x1, Pallas kernels, local(): pl.pallas_call(functools.partial(exchange_kernel, counts), out_shape=(fie...  11.4 us
    pallas_call x1, Pallas kernels, local(): pl.pallas_call(finish_kernel, out_shape=(field,) * 3, in_specs=[vmem] * 7...  1.7 us

profile of v2, /device:TPU:1, one launch (start us, length us, event | category | flops | bytes accessed | tf_op | source)
XLA Modules:
  0.0 13.8 jit_solution(10510090861169334358)
XLA Ops:
  0.6 0.0 copy-start
  0.6 11.4 %exchange.1 = (f32[8,128,256]{2,1,0:T(8,128)S(1)}, f32[8,128,256]{2,1,0:T(8,128)S(1)}, f32[8,128,256]{2,1,0:T(8,128)S(1)}, f32[8,128,256]{2,1,0:T(8,128)S(1)}, f...) custom-call(f32[8,128,256]{2,1,0:T(8,128)} %f_hbm.1, f32[8,128,256]{2,1,0:T(8,128)} %k_hbm.1, ...), custom_call_target="tpu_custom_call" | custom-call | tf_op jit(solution)/shard_map/exchange/pallas_call | solution.py:445
  12.1 0.0 copy-done
  12.1 1.7 %finish.1 = (f32[8,128,256]{2,1,0:T(8,128)}, f32[8,128,256]{2,1,0:T(8,128)}, f32[8,128,256]{2,1,0:T(8,128)}) custom-call(f32[8,128,256]{2,1,0:T(8,128)S(1)} %get-tuple-element.9.gx, f32[8,128,256]{2,1,0:T(8,128)S(1)} %get-tuple-element.10.gy, f32[8,128,256]{2,1,0:T(8,128)S(1)} %get-tuple-element.11.dif, f32[8,128,256]{2,1,0:T(8,128)S(1)} %get-tuple-element.12.kx, ...), custom_call_target="tpu_custom_call" | custom-call | tf_op jit(solution)/shard_map/finish/pallas_call | solution.py:469
Async XLA Ops:
  0.6 11.4 %copy-start = (f32[4,32,128]{2,1,0:T(8,128)S(1)}, f32[4,32,128]{2,1,0:T(8,128)}, u32[]{:S(2)}) copy-start(f32[4,32,128]{2,1,0:T(8,128)} %constant.8.clone.tab) | copy-start | bytes 196612

commit v3 on v2

--- a/solution.py
+++ b/solution.py
@@ -18,6 +18,7 @@
 STRIP = 24
 REACH = 32
 FULL = 128
+RUN = 8
 
 
 class Line:
@@ -230,8 +231,8 @@
     for neighbour in (left, above):
         pl.semaphore_signal(barrier, inc=1, device_id=neighbour, device_id_type=MESH)
 
-    def send(place, source, target, device):
-        copy = pltpu.make_async_remote_copy(
+    def message(place, source, target, device):
+        return pltpu.make_async_remote_copy(
             src_ref=source,
             dst_ref=target,
             send_sem=send_sem.at[place],
@@ -239,30 +240,39 @@
             device_id=device,
             device_id_type=MESH,
         )
+
+    def send(*what):
+        copy = message(*what)
         copy.start()
         return copy
 
-    def sum_x_edge(side, start, edge, place):
+    def take_x_edge(side, edge):
+        for p in range(planes):
+            xs[side, 0, p : p + 1, :] = fld[p, edge : edge + 1, :]
+            xs[side, 1, p : p + 1, :] = kap[p, edge : edge + 1, :]
+
+    def sum_x_edge(side, start, place):
         with_first, with_second = twice(tab[place, 0:STRIP]), twice(tab[place + 1, 0:STRIP])
         for p in range(planes):
             rows = fld[p, start : start + STRIP, :]
             krows = kap[p, start : start + STRIP, :]
-            xs[side, 0, p : p + 1, :] = jnp.sum(rows * with_first, axis=0, keepdims=True)
-            xs[side, 1, p : p + 1, :] = jnp.sum(rows * with_second, axis=0, keepdims=True)
-            xs[side, 2, p : p + 1, :] = fld[p, edge : edge + 1, :]
-            xs[side, 3, p : p + 1, :] = jnp.sum(krows * with_first, axis=0, keepdims=True)
-            xs[side, 4, p : p + 1, :] = kap[p, edge : edge + 1, :]
+            xs[side, 2, p : p + 1, :] = jnp.sum(rows * with_first, axis=0, keepdims=True)
+            xs[side, 3, p : p + 1, :] = jnp.sum(rows * with_second, axis=0, keepdims=True)
+            xs[side, 4, p : p + 1, :] = jnp.sum(krows * with_first, axis=0, keepdims=True)
 
     for copy in high_loads:
         copy.wait()
-    sum_x_edge(1, top, cells_x - 1, 0)
+    take_x_edge(1, cells_x - 1)
     pl.semaphore_wait(barrier, 2)
-    to_right = send(1, xs.at[1], xr.at[0], right)
+    to_right = [send(1, xs.at[1, 0:2], xr.at[0, 0:2], right)]
+    sum_x_edge(1, top, 0)
+    to_right.append(send(2, xs.at[1, 2:5], xr.at[0, 2:5], right))
     pl.semaphore_signal(left_ready, inc=1, device_id=right, device_id_type=MESH)
     pl.semaphore_signal(above_ready, inc=1, device_id=below, device_id_type=MESH)
     for copy in low_loads:
         copy.wait()
-    sum_x_edge(0, 0, 0, 2)
+    take_x_edge(0, 0)
+    sum_x_edge(0, 0, 2)
 
     for copy in middle_loads:
         copy.wait()
@@ -291,9 +301,18 @@
             ys[side, p, 2:3, :] = f_edge
             ys[side, p, 3:4, :] = jnp.sum(k_part * with_first, axis=0, keepdims=True)
             ys[side, p, 4:5, :] = k_edge
-    to_below = send(2, ys.at[0], yr.at[1], below)
+    to_below = send(3, ys.at[0], yr.at[1], below)
     pl.semaphore_wait(above_ready, 1)
-    to_above = send(3, ys.at[1], yr.at[0], above)
+    to_above = send(4, ys.at[1], yr.at[0], above)
+
+    to_left = message(0, xs.at[0], xr.at[1], left)
+    run_begins = lax.rem(ix, RUN) == 0
+
+    def send_left():
+        pl.semaphore_wait(left_ready, 1)
+        to_left.start()
+
+    pl.when(jnp.logical_not(run_begins))(send_left)
 
     table_load.wait()
     x_rows = 4 * cells_x
@@ -327,9 +346,6 @@
         return carry
 
     lax.fori_loop(0, planes // 2, local_pair, 0)
-
-    pl.semaphore_wait(left_ready, 1)
-    to_left = send(0, xs.at[0], xr.at[1], left)
 
     to_below.wait_recv()
     to_above.wait_recv()
@@ -364,15 +380,16 @@
         return carry
 
     lax.fori_loop(0, planes // 2, finish_pair, 0)
+    pl.when(run_begins)(send_left)
 
     def combine(side, out):
         sign = 1.0 if side == 0 else -1.0
-        jump = sign * (xs[side, 2] - xr[side, 2])
-        kjump = sign * (xs[side, 4] - xr[side, 4])
-        out[0] = FIRST.rho * xr[side, 0] + jump
-        out[1] = SECOND.rho * xr[side, 1] + jump
+        jump = sign * (xs[side, 0] - xr[side, 0])
+        kjump = sign * (xs[side, 1] - xr[side, 1])
+        out[0] = FIRST.rho * xr[side, 2] + jump
+        out[1] = SECOND.rho * xr[side, 3] + jump
         out[2] = jump
-        out[3] = FIRST.rho * xr[side, 3] + kjump
+        out[3] = FIRST.rho * xr[side, 4] + kjump
         out[4] = kjump
 
     to_left.wait_recv()
@@ -388,9 +405,10 @@
             columns,
             [xh[n, p : p + 1, :] for n in range(5)],
         )
-    for copy in (to_left, to_right, to_below, to_above):
+    for copy in [to_left, to_below, to_above] + to_right:
         copy.wait_send()
-    to_right.wait_recv()
+    for copy in to_right:
+        copy.wait_recv()
     combine(0, xc)
 
 
@@ -455,8 +473,8 @@
         + [
             pltpu.VMEM(ends_shape, jnp.float32),
             pltpu.SemaphoreType.DMA((8,)),
-            pltpu.SemaphoreType.DMA((4,)),
-            pltpu.SemaphoreType.DMA((4,)),
+            pltpu.SemaphoreType.DMA((5,)),
+            pltpu.SemaphoreType.DMA((5,)),
             pltpu.SemaphoreType.REGULAR,
             pltpu.SemaphoreType.REGULAR,
         ],

time: 13.9 us -> 13.8 us (level)
  no operation moved by 1% of the time
where the time goes in v3:
time: 13.8 us; the launch traced here: 13.7 us
  Pallas kernels  13 us (94%)
  between operations  0.65 us (5%)
    pallas_call x1, Pallas kernels, local(): pl.pallas_call(functools.partial(exchange_kernel, counts), out_shape=(fie...  11.3 us
    pallas_call x1, Pallas kernels, local(): pl.pallas_call(finish_kernel, out_shape=(field,) * 3, in_specs=[vmem] * 7...  1.7 us

profile of v3, /device:TPU:1, one launch (start us, length us, event | category | flops | bytes accessed | tf_op | source)
XLA Modules:
  0.0 13.7 jit_solution(12846824607823553204)
XLA Ops:
  0.6 0.0 copy-start
  0.6 11.3 %exchange.1 = (f32[8,128,256]{2,1,0:T(8,128)S(1)}, f32[8,128,256]{2,1,0:T(8,128)S(1)}, f32[8,128,256]{2,1,0:T(8,128)S(1)}, f32[8,128,256]{2,1,0:T(8,128)S(1)}, f...) custom-call(f32[8,128,256]{2,1,0:T(8,128)} %f_hbm.1, f32[8,128,256]{2,1,0:T(8,128)} %k_hbm.1, ...), custom_call_target="tpu_custom_call" | custom-call | tf_op jit(solution)/shard_map/exchange/pallas_call | solution.py:463
  12.0 0.0 copy-done
  12.0 1.7 %finish.1 = (f32[8,128,256]{2,1,0:T(8,128)}, f32[8,128,256]{2,1,0:T(8,128)}, f32[8,128,256]{2,1,0:T(8,128)}) custom-call(f32[8,128,256]{2,1,0:T(8,128)S(1)} %get-tuple-element.9.gx, f32[8,128,256]{2,1,0:T(8,128)S(1)} %get-tuple-element.10.gy, f32[8,128,256]{2,1,0:T(8,128)S(1)} %get-tuple-element.11.dif, f32[8,128,256]{2,1,0:T(8,128)S(1)} %get-tuple-element.12.kx, ...), custom_call_target="tpu_custom_call" | custom-call | tf_op jit(solution)/shard_map/finish/pallas_call | solution.py:487
Async XLA Ops:
  0.6 11.3 %copy-start = (f32[4,32,128]{2,1,0:T(8,128)S(1)}, f32[4,32,128]{2,1,0:T(8,128)}, u32[]{:S(2)}) copy-start(f32[4,32,128]{2,1,0:T(8,128)} %constant.8.clone.tab) | copy-start | bytes 196612

commit v4 on v3

--- a/solution.py
+++ b/solution.py
@@ -15,6 +15,7 @@
 SECOND_A = 12.0 / 11.0
 SECOND_B = 3.0 / 11.0
 MESH = pl.DeviceIdType.MESH
+LIMIT = 28 * 1024 * 1024
 STRIP = 24
 REACH = 32
 FULL = 128
@@ -199,6 +200,7 @@
     recv_sem,
     left_ready,
     above_ready,
+    below_ready,
 ):
     planes, cells_x, cells_y = fld.shape
     top = cells_x - STRIP
@@ -216,8 +218,8 @@
             load(k_hbm.at[:, rows, :], kap.at[:, rows, :]),
         ]
 
-    high_loads = load_rows(pl.ds(top, STRIP)) + [load(tab_hbm, tab)]
-    low_loads = load_rows(pl.ds(0, STRIP))
+    high_loads = load_rows(pl.ds(top, STRIP)) + [load(tab_hbm.at[0:4], tab.at[0:4])]
+    low_loads = load_rows(pl.ds(0, STRIP)) + [load(tab_hbm.at[4:], tab.at[4:])]
     middle_loads = load_rows(pl.ds(STRIP, top - STRIP))
     table_load = load(mats_hbm, mats)
 
@@ -227,9 +229,19 @@
     right = (jnp.where(ix == nx - 1, 0, ix + 1), iy)
     below = (ix, jnp.where(iy == 0, ny - 1, iy - 1))
     above = (ix, jnp.where(iy == ny - 1, 0, iy + 1))
+    first_y, last_y = iy == 0, iy == ny - 1
     barrier = pltpu.get_barrier_semaphore()
-    for neighbour in (left, above):
-        pl.semaphore_signal(barrier, inc=1, device_id=neighbour, device_id_type=MESH)
+
+    def tell(semaphore, neighbour, when=None):
+        def signal():
+            pl.semaphore_signal(semaphore, inc=1, device_id=neighbour, device_id_type=MESH)
+
+        signal() if when is None else pl.when(when)(signal)
+
+    tell(barrier, left)
+    tell(barrier, above, jnp.logical_not(last_y))
+    tell(barrier, below, first_y)
+    heard = 1 + jnp.where(first_y, 0, 1) + jnp.where(last_y, 1, 0)
 
     def message(place, source, target, device):
         return pltpu.make_async_remote_copy(
@@ -263,12 +275,13 @@
     for copy in high_loads:
         copy.wait()
     take_x_edge(1, cells_x - 1)
-    pl.semaphore_wait(barrier, 2)
+    pl.semaphore_wait(barrier, heard)
     to_right = [send(1, xs.at[1, 0:2], xr.at[0, 0:2], right)]
     sum_x_edge(1, top, 0)
     to_right.append(send(2, xs.at[1, 2:5], xr.at[0, 2:5], right))
-    pl.semaphore_signal(left_ready, inc=1, device_id=right, device_id_type=MESH)
-    pl.semaphore_signal(above_ready, inc=1, device_id=below, device_id_type=MESH)
+    tell(left_ready, right)
+    tell(above_ready, below, jnp.logical_not(first_y))
+    tell(below_ready, above, last_y)
     for copy in low_loads:
         copy.wait()
     take_x_edge(0, 0)
@@ -301,8 +314,9 @@
             ys[side, p, 2:3, :] = f_edge
             ys[side, p, 3:4, :] = jnp.sum(k_part * with_first, axis=0, keepdims=True)
             ys[side, p, 4:5, :] = k_edge
+    pl.when(first_y)(lambda: pl.semaphore_wait(below_ready, 1))
     to_below = send(3, ys.at[0], yr.at[1], below)
-    pl.semaphore_wait(above_ready, 1)
+    pl.when(jnp.logical_not(last_y))(lambda: pl.semaphore_wait(above_ready, 1))
     to_above = send(4, ys.at[1], yr.at[0], above)
 
     to_left = message(0, xs.at[0], xr.at[1], left)
@@ -412,19 +426,56 @@
     combine(0, xc)
 
 
-def finish_kernel(gx, gy, dif, kx, kap, xc, tab, gx_out, gy_out, dif_out, gs, ds, sem):
+def writes_early():
+    return (lax.axis_index("gx") == 0) & (lax.axis_index("gy") != 0)
+
+
+def early_kernel(f_hbm, mats_hbm, gx_out, fld, mats, gx, in_sem, out_sem):
+    planes, cells_x, _ = fld.shape
+    inner = pl.ds(STRIP, cells_x - 2 * STRIP)
+
+    @pl.when(writes_early())
+    def work():
+        table_load = pltpu.make_async_copy(
+            mats_hbm.at[pl.ds(0, 2 * cells_x), :], mats, in_sem.at[planes]
+        )
+        table_load.start()
+        loads, stores = [], []
+        for p in range(planes):
+            loads.append(pltpu.make_async_copy(f_hbm.at[p], fld.at[p], in_sem.at[p]))
+            loads[p].start()
+        table_load.wait()
+        for p in range(planes):
+            loads[p].wait()
+            high, low = split(pltpu.roll(fld[p], cells_x - 1, 0) - fld[p])
+            along = matmul(mats[...], jnp.concatenate([high, low], axis=0))
+            gx[p] = along[0:cells_x] + along[cells_x : 2 * cells_x]
+            stores.append(
+                pltpu.make_async_copy(gx.at[p, inner, :], gx_out.at[p, inner, :], out_sem.at[p])
+            )
+            stores[p].start()
+        for copy in stores:
+            copy.wait()
+
+
+def finish_kernel(started, gx, gy, dif, kx, kap, xc, tab, gx_out, gy_out, dif_out, gs, ds, sem):
     planes, cells_x, cells_y = gx.shape
-    copies = []
-
-    def store(source, target):
-        copy = pltpu.make_async_copy(source, target, sem.at[len(copies)])
+    top = cells_x - STRIP
+    early = writes_early()
+
+    def copy_of(place, source, target):
+        return pltpu.make_async_copy(source, target, sem.at[place])
+
+    rest, high, inner = pl.ds(STRIP, top), pl.ds(top, STRIP), pl.ds(STRIP, top - STRIP)
+    copies = [
+        copy_of(0, gy, gy_out),
+        copy_of(1, dif.at[:, rest, :], dif_out.at[:, rest, :]),
+        copy_of(2, gx.at[:, high, :], gx_out.at[:, high, :]),
+    ]
+    for copy in copies:
         copy.start()
-        copies.append(copy)
-
-    rest = pl.ds(STRIP, cells_x - STRIP)
-    store(gy, gy_out)
-    store(gx.at[:, rest, :], gx_out.at[:, rest, :])
-    store(dif.at[:, rest, :], dif_out.at[:, rest, :])
+    inner_copy = copy_of(3, gx.at[:, inner, :], gx_out.at[:, inner, :])
+    pl.when(jnp.logical_not(early))(inner_copy.start)
     columns = [twice(tab[n, 0:STRIP]) for n in (0, 1)] + [twice(tab[n, 0:8]) for n in (2, 3)]
     for p in range(planes):
         gs[p], ds[p] = ends_applied(
@@ -436,8 +487,11 @@
             columns,
             [xc[n, p : p + 1, :] for n in range(5)],
         )
-    store(gs, gx_out.at[:, pl.ds(0, STRIP), :])
-    store(ds, dif_out.at[:, pl.ds(0, STRIP), :])
+    low = pl.ds(0, STRIP)
+    for place, source, target in ((4, gs, gx_out), (5, ds, dif_out)):
+        copies.append(copy_of(place, source, target.at[:, low, :]))
+        copies[-1].start()
+    pl.when(jnp.logical_not(early))(inner_copy.wait)
     for copy in copies:
         copy.wait()
 
@@ -460,6 +514,21 @@
         pltpu.with_memory_space_constraint(array, pltpu.HBM)
         for array in (scalar, diffusivity) + tables
     ]
+    started = pl.pallas_call(
+        early_kernel,
+        out_shape=field,
+        in_specs=[hbm] * 2,
+        out_specs=hbm,
+        scratch_shapes=[
+            field_buffer,
+            pltpu.VMEM((2 * cells_x, tables[1].shape[1]), tables[1].dtype),
+            field_buffer,
+            pltpu.SemaphoreType.DMA((planes + 1,)),
+            pltpu.SemaphoreType.DMA((planes,)),
+        ],
+        compiler_params=pltpu.CompilerParams(vmem_limit_bytes=LIMIT),
+        name="early",
+    )(operands[0], operands[3])
     parts = pl.pallas_call(
         functools.partial(exchange_kernel, counts),
         out_shape=(field,) * 5 + (jax.ShapeDtypeStruct(ends_shape, jnp.float32),),
@@ -472,14 +541,15 @@
         + [pltpu.VMEM((2, planes, 8, cells_x), jnp.float32)] * 2
         + [
             pltpu.VMEM(ends_shape, jnp.float32),
-            pltpu.SemaphoreType.DMA((8,)),
+            pltpu.SemaphoreType.DMA((9,)),
             pltpu.SemaphoreType.DMA((5,)),
             pltpu.SemaphoreType.DMA((5,)),
             pltpu.SemaphoreType.REGULAR,
             pltpu.SemaphoreType.REGULAR,
+            pltpu.SemaphoreType.REGULAR,
         ],
         compiler_params=pltpu.CompilerParams(
-            collective_id=0, has_side_effects=True, vmem_limit_bytes=28 * 1024 * 1024
+            collective_id=0, has_side_effects=True, vmem_limit_bytes=LIMIT
         ),
         name="exchange",
     )(*operands)
@@ -487,12 +557,13 @@
     return pl.pallas_call(
         finish_kernel,
         out_shape=(field,) * 3,
-        in_specs=[vmem] * 7,
+        in_specs=[hbm] + [vmem] * 7,
         out_specs=(hbm,) * 3,
-        scratch_shapes=[strip_buffer, strip_buffer, pltpu.SemaphoreType.DMA((5,))],
-        compiler_params=pltpu.CompilerParams(vmem_limit_bytes=28 * 1024 * 1024),
+        scratch_shapes=[strip_buffer, strip_buffer, pltpu.SemaphoreType.DMA((6,))],
+        input_output_aliases={0: 0},
+        compiler_params=pltpu.CompilerParams(vmem_limit_bytes=LIMIT),
         name="finish",
-    )(*parts, jnp.asarray(stacked(low_end_columns())))
+    )(started, *parts, jnp.asarray(stacked(low_end_columns())))
 
 
 def solution(mesh):

time: 13.8 us -> 15.2 us (1.10)
  Pallas kernels: 13 us -> 14.4 us
    pallas_call x1 -> x2, Pallas kernels: 1.7 us -> 5.01 us  [the longest x1 3.52 us: local(): pl.pallas_call(early_kernel, out_shape=field, in_specs=[hbm] * 2, out_spe...]
    pallas_call x1, Pallas kernels: 11.3 us -> 9.4 us  [local(): pl.pallas_call(functools.partial(exchange_kernel, counts), out_shape=(fie...]
where the time goes in v4:
time: 15.2 us; the launch traced here: 15.1 us
  Pallas kernels  14.4 us (95%)
  between operations  0.66 us (4%)
    pallas_call x1, Pallas kernels, local(): pl.pallas_call(functools.partial(exchange_kernel, counts), out_shape=(fie...  9.4 us
    pallas_call x1, Pallas kernels, local(): pl.pallas_call(early_kernel, out_shape=field, in_specs=[hbm] * 2, out_spe...  3.52 us
    pallas_call x1, Pallas kernels, local(): pl.pallas_call(finish_kernel, out_shape=(field,) * 3, in_specs=[hbm] + [v...  1.49 us

profile of v4, /device:TPU:1, one launch (start us, length us, event | category | flops | bytes accessed | tf_op | source)
XLA Modules:
  0.0 15.1 jit_solution(11587512575398444411)
XLA Ops:
  0.6 3.5 %early.1.started = f32[8,128,256]{2,1,0:T(8,128)} custom-call(f32[8,128,256]{2,1,0:T(8,128)} %f_hbm.3, bf16[2432,256]{1,0:T(8,128)(2,1)} %constant.7.clone.mats_hbm), custom_call_target="tpu_custom_call" | custom-call | tf_op jit(solution)/shard_map/early/pallas_call | solution.py:517
  4.2 0.0 copy-start
  4.2 9.4 %exchange.1 = (f32[8,128,256]{2,1,0:T(8,128)S(1)}, f32[8,128,256]{2,1,0:T(8,128)S(1)}, f32[8,128,256]{2,1,0:T(8,128)S(1)}, f32[8,128,256]{2,1,0:T(8,128)S(1)}, f...) custom-call(f32[8,128,256]{2,1,0:T(8,128)} %f_hbm.3, f32[8,128,256]{2,1,0:T(8,128)} %k_hbm.1, ...), custom_call_target="tpu_custom_call" | custom-call | tf_op jit(solution)/shard_map/exchange/pallas_call | solution.py:532
  13.6 0.0 copy-done
  13.6 1.5 %finish.1 = (f32[8,128,256]{2,1,0:T(8,128)}, f32[8,128,256]{2,1,0:T(8,128)}, f32[8,128,256]{2,1,0:T(8,128)}) custom-call(f32[8,128,256]{2,1,0:T(8,128)} %early.1.started, f32[8,128,256]{2,1,0:T(8,128)S(1)} %get-tuple-element.9.gx, f32[8,128,256]{2,1,0:T(8,128)S(1)} %get-tuple-element.10.gy, ...), custom_call_target="tpu_custom_call", output_to_operand_aliasing={{0}: (0, {})} | custom-call | tf_op jit(solution)/shard_map/finish/pallas_call | solution.py:557
Async XLA Ops:
  4.2 9.4 %copy-start = (f32[4,32,128]{2,1,0:T(8,128)S(1)}, f32[4,32,128]{2,1,0:T(8,128)}, u32[]{:S(2)}) copy-start(f32[4,32,128]{2,1,0:T(8,128)} %constant.8.clone.tab) | copy-start | bytes 196612

commit v5 on v3

--- a/solution.py
+++ b/solution.py
@@ -170,6 +170,27 @@
         grads.append(g)
         parts.append(d + k * g)
     return jnp.concatenate(grads, axis=0), jnp.concatenate(parts, axis=0)
+
+
+def sums_kernel(f_hbm, k_hbm, tab_hbm, out, fst, kst, tab, sem):
+    planes, cells_x = f_hbm.shape[0], f_hbm.shape[1]
+    rows = pl.ds(cells_x - STRIP, STRIP)
+    copies = [
+        pltpu.make_async_copy(f_hbm.at[:, rows, :], fst, sem.at[0]),
+        pltpu.make_async_copy(k_hbm.at[:, rows, :], kst, sem.at[1]),
+        pltpu.make_async_copy(tab_hbm.at[0:2], tab, sem.at[2]),
+    ]
+    for copy in copies:
+        copy.start()
+    for copy in copies:
+        copy.wait()
+    with_first, with_second = twice(tab[0, 0:STRIP]), twice(tab[1, 0:STRIP])
+    for p in range(planes):
+        out[0, p : p + 1, :] = fst[p, STRIP - 1 : STRIP, :]
+        out[1, p : p + 1, :] = kst[p, STRIP - 1 : STRIP, :]
+        out[2, p : p + 1, :] = jnp.sum(fst[p] * with_first, axis=0, keepdims=True)
+        out[3, p : p + 1, :] = jnp.sum(fst[p] * with_second, axis=0, keepdims=True)
+        out[4, p : p + 1, :] = jnp.sum(kst[p] * with_first, axis=0, keepdims=True)
 
 
 def exchange_kernel(
@@ -264,9 +285,6 @@
         copy.wait()
     take_x_edge(1, cells_x - 1)
     pl.semaphore_wait(barrier, 2)
-    to_right = [send(1, xs.at[1, 0:2], xr.at[0, 0:2], right)]
-    sum_x_edge(1, top, 0)
-    to_right.append(send(2, xs.at[1, 2:5], xr.at[0, 2:5], right))
     pl.semaphore_signal(left_ready, inc=1, device_id=right, device_id_type=MESH)
     pl.semaphore_signal(above_ready, inc=1, device_id=below, device_id_type=MESH)
     for copy in low_loads:
@@ -405,27 +423,36 @@
             columns,
             [xh[n, p : p + 1, :] for n in range(5)],
         )
-    for copy in [to_left, to_below, to_above] + to_right:
+    xc[0] = xs[0, 0]
+    xc[1] = xs[0, 1]
+    for copy in (to_left, to_below, to_above):
         copy.wait_send()
-    for copy in to_right:
-        copy.wait_recv()
-    combine(0, xc)
-
-
-def finish_kernel(gx, gy, dif, kx, kap, xc, tab, gx_out, gy_out, dif_out, gs, ds, sem):
-    planes, cells_x, cells_y = gx.shape
+
+
+def bulk_kernel(gx, gy, dif, gx_out, gy_out, dif_out, sem):
+    rest = pl.ds(STRIP, gx.shape[1] - STRIP)
+    copies = [
+        pltpu.make_async_copy(gy, gy_out, sem.at[0]),
+        pltpu.make_async_copy(gx.at[:, rest, :], gx_out.at[:, rest, :], sem.at[1]),
+        pltpu.make_async_copy(dif.at[:, rest, :], dif_out.at[:, rest, :], sem.at[2]),
+    ]
+    for copy in copies:
+        copy.start()
+    for copy in copies:
+        copy.wait()
+
+
+def finish_kernel(gx_in, dif_in, gx, dif, kx, kap, edges, came, tab, gx_out, dif_out, gs, ds, xc, sem):
+    planes = gx.shape[0]
+    jump, kjump = edges[0] - came[0], edges[1] - came[1]
+    xc[0] = FIRST.rho * came[2] + jump
+    xc[1] = SECOND.rho * came[3] + jump
+    xc[2] = jump
+    xc[3] = FIRST.rho * came[4] + kjump
+    xc[4] = kjump
+    columns = [twice(tab[n, 0:STRIP]) for n in (0, 1)] + [twice(tab[n, 0:8]) for n in (2, 3)]
+    low = pl.ds(0, STRIP)
     copies = []
-
-    def store(source, target):
-        copy = pltpu.make_async_copy(source, target, sem.at[len(copies)])
-        copy.start()
-        copies.append(copy)
-
-    rest = pl.ds(STRIP, cells_x - STRIP)
-    store(gy, gy_out)
-    store(gx.at[:, rest, :], gx_out.at[:, rest, :])
-    store(dif.at[:, rest, :], dif_out.at[:, rest, :])
-    columns = [twice(tab[n, 0:STRIP]) for n in (0, 1)] + [twice(tab[n, 0:8]) for n in (2, 3)]
     for p in range(planes):
         gs[p], ds[p] = ends_applied(
             0,
@@ -436,8 +463,15 @@
             columns,
             [xc[n, p : p + 1, :] for n in range(5)],
         )
-    store(gs, gx_out.at[:, pl.ds(0, STRIP), :])
-    store(ds, dif_out.at[:, pl.ds(0, STRIP), :])
+        if p % 4 == 3:
+            some = pl.ds(p - 3, 4)
+            for source, target in ((gs, gx_out), (ds, dif_out)):
+                copies.append(
+                    pltpu.make_async_copy(
+                        source.at[some], target.at[some, low, :], sem.at[len(copies)]
+                    )
+                )
+                copies[-1].start()
     for copy in copies:
         copy.wait()
 
@@ -460,9 +494,25 @@
         pltpu.with_memory_space_constraint(array, pltpu.HBM)
         for array in (scalar, diffusivity) + tables
     ]
+    strip_shape = (planes, STRIP, cells_y)
+    message = pl.pallas_call(
+        sums_kernel,
+        out_shape=jax.ShapeDtypeStruct(ends_shape, jnp.float32),
+        in_specs=[hbm] * 3,
+        out_specs=vmem,
+        scratch_shapes=[
+            pltpu.VMEM(strip_shape, jnp.float32),
+            pltpu.VMEM(strip_shape, jnp.float32),
+            pltpu.VMEM((2, 32, 128), jnp.float32),
+            pltpu.SemaphoreType.DMA((3,)),
+        ],
+        compiler_params=pltpu.CompilerParams(vmem_limit_bytes=28 * 1024 * 1024),
+        name="sums",
+    )(*operands[:3])
+    came = lax.ppermute(message, "gx", [(i, (i + 1) % counts[0]) for i in range(counts[0])])
     parts = pl.pallas_call(
         functools.partial(exchange_kernel, counts),
-        out_shape=(field,) * 5 + (jax.ShapeDtypeStruct(ends_shape, jnp.float32),),
+        out_shape=(field,) * 5 + (jax.ShapeDtypeStruct((2,) + ends_shape[1:], jnp.float32),),
         in_specs=[hbm] * 4,
         out_specs=(vmem,) * 6,
         scratch_shapes=[field_buffer]
@@ -481,18 +531,37 @@
         compiler_params=pltpu.CompilerParams(
             collective_id=0, has_side_effects=True, vmem_limit_bytes=28 * 1024 * 1024
         ),
+        cost_estimate=pl.CostEstimate(flops=2 * 10**9, bytes_accessed=8 * 2**20, transcendentals=0),
         name="exchange",
     )(*operands)
     strip_buffer = pltpu.VMEM((planes, STRIP, cells_y), jnp.float32)
-    return pl.pallas_call(
+    grad_x, grad_y, dif, kx, kap, edges = parts
+    gx_out, gy_out, dif_out = pl.pallas_call(
+        bulk_kernel,
+        out_shape=(field,) * 3,
+        in_specs=[vmem] * 3,
+        out_specs=(hbm,) * 3,
+        scratch_shapes=[pltpu.SemaphoreType.DMA((3,))],
+        compiler_params=pltpu.CompilerParams(vmem_limit_bytes=28 * 1024 * 1024),
+        cost_estimate=pl.CostEstimate(flops=0, bytes_accessed=3 * 2**20, transcendentals=0),
+        name="bulk",
+    )(grad_x, grad_y, dif)
+    gx_out, dif_out = pl.pallas_call(
         finish_kernel,
-        out_shape=(field,) * 3,
-        in_specs=[vmem] * 7,
-        out_specs=(hbm,) * 3,
-        scratch_shapes=[strip_buffer, strip_buffer, pltpu.SemaphoreType.DMA((5,))],
+        out_shape=(field,) * 2,
+        in_specs=[hbm] * 2 + [vmem] * 7,
+        out_specs=(hbm,) * 2,
+        scratch_shapes=[
+            strip_buffer,
+            strip_buffer,
+            pltpu.VMEM(ends_shape, jnp.float32),
+            pltpu.SemaphoreType.DMA((4,)),
+        ],
+        input_output_aliases={0: 0, 1: 1},
         compiler_params=pltpu.CompilerParams(vmem_limit_bytes=28 * 1024 * 1024),
         name="finish",
-    )(*parts, jnp.asarray(stacked(low_end_columns())))
+    )(gx_out, dif_out, grad_x, dif, kx, kap, edges, came, jnp.asarray(stacked(low_end_columns())))
+    return gx_out, gy_out, dif_out
 
 
 def solution(mesh):

time: 13.8 us -> 16.2 us (1.17)
  starting transfers between devices: 0 us -> 2.53 us
    ppermute x0 -> x1, starting transfers between devices: none -> 2.53 us  [local(): lax.ppermute(message, 'gx', [(i, (i + 1) % counts[0]) for i in range(coun...]
    pallas_call x1, Pallas kernels: 11.3 us -> 9.38 us  [local(): pl.pallas_call(functools.partial(exchange_kernel, counts), out_shape=(fie...]
    pallas_call x1 -> x3, Pallas kernels: 1.7 us -> 3.52 us  [the longest x1 1.56 us: local(): pl.pallas_call(bulk_kernel, out_shape=(field,) * 3, in_specs=[vmem] * 3,...]
  transfers between devices with their start and end apart: 0 -> 1, of which waited for: 0 -> 0; matrix products, arithmetic and copies ran while one was open for 0% -> 0% of each run, Pallas kernels for 0% -> 68%
where the time goes in v5:
time: 16.2 us; the launch traced here: 16.1 us
  Pallas kernels  12.9 us (80%)
  starting transfers between devices  2.53 us (16%)
  between operations  0.68 us (4%)
    pallas_call x1, Pallas kernels, local(): pl.pallas_call(functools.partial(exchange_kernel, counts), out_shape=(fie...  9.38 us
    ppermute x1, starting transfers between devices, local(): lax.ppermute(message, 'gx', [(i, (i + 1) % counts[0]) for i in range(coun...  2.53 us
    pallas_call x1, Pallas kernels, local(): pl.pallas_call(bulk_kernel, out_shape=(field,) * 3, in_specs=[vmem] * 3,...  1.56 us
    pallas_call x1, Pallas kernels, local(): pl.pallas_call(sums_kernel, out_shape=jax.ShapeDtypeStruct(ends_shape, jn...  1.14 us
    pallas_call x1, Pallas kernels, local(): pl.pallas_call(finish_kernel, out_shape=(field,) * 2, in_specs=[hbm] * 2...  0.82 us
  transfers between devices with their start and end apart: 1, of which 0 were waited for; matrix products, arithmetic and copies ran while one was open for 0% of the time, Pallas kernels for 68%

profile of v5, /device:TPU:1, one launch (start us, length us, event | category | flops | bytes accessed | tf_op | source)
XLA Modules:
  0.0 16.1 jit_solution(4148787133601155416)
XLA Ops:
  0.6 1.1 %sums.1 = f32[5,8,256]{2,1,0:T(8,128)S(1)} custom-call(f32[8,128,256]{2,1,0:T(8,128)} %f_hbm.3, f32[8,128,256]{2,1,0:T(8,128)} %k_hbm.3, f32[12,32,128]{2,1,0:T(8,128)} %constant.6.clone.tab_hbm), custom_call_target="tpu_custom_call" | custom-call | tf_op jit(solution)/shard_map/sums/pallas_call | solution.py:498
  1.8 2.5 %collective-permute-start = (f32[5,8,256]{2,1,0:T(8,128)S(1)}, f32[5,8,256]{2,1,0:T(8,128)S(1)}, u32[]{:S(2)}, u32[]{:S(2)}) collective-permute-start(f32[5,8,256]{2,1,0:T(8,128)S(1)} %sums.1), channel_id=1, source_target_pairs={{0,8},{8,16},{16,24},{24,32},{32,40},{40,48},{48,56},{56,64},{64,7... | collective-permute-start | bytes 122888 | tf_op jit(solution)/shard_map/ppermute | solution.py:512
  4.3 9.4 %exchange.1 = (f32[8,128,256]{2,1,0:T(8,128)S(1)}, f32[8,128,256]{2,1,0:T(8,128)S(1)}, f32[8,128,256]{2,1,0:T(8,128)S(1)}, f32[8,128,256]{2,1,0:T(8,128)S(1)}, f...) custom-call(f32[8,128,256]{2,1,0:T(8,128)} %f_hbm.3, f32[8,128,256]{2,1,0:T(8,128)} %k_hbm.3, ...), custom_call_target="tpu_custom_call" | custom-call | flops 2000000000 | bytes 8388608 | tf_op jit(solution)/shard_map/exchange/pallas_call | solution.py:513
  13.7 0.0 copy-start
  13.7 1.6 %bulk.1 = (f32[8,128,256]{2,1,0:T(8,128)}, f32[8,128,256]{2,1,0:T(8,128)}, f32[8,128,256]{2,1,0:T(8,128)}) custom-call(f32[8,128,256]{2,1,0:T(8,128)S(1)} %get-tuple-element.14.gx, f32[8,128,256]{2,1,0:T(8,128)S(1)} %get-tuple-element.15.gy, f32[8,128,256]{2,1,0:T(8,128)S(1)} %get-tuple-element.16.dif), custom_call_target="tpu_custom_call" | custom-call | bytes 3145728 | tf_op jit(solution)/shard_map/bulk/pallas_call | solution.py:539
  15.3 0.0 collective-permute-done.came
  15.3 0.0 copy-done
  15.3 0.8 %finish.1 = (f32[8,128,256]{2,1,0:T(8,128)}, f32[8,128,256]{2,1,0:T(8,128)}) custom-call(f32[8,128,256]{2,1,0:T(8,128)} %get-tuple-element.17.gx_in, f32[8,128,256]{2,1,0:T(8,128)} %get-tuple-element.18.dif_in, f32[8,128,256]{2,1,0:T(8,128)S(1)} %get-tuple-element.14.gx, ...), custom_call_target="tpu_custom_call", output_to_operand_aliasing={{0}: (0, {}), {1}: (1, {})} | custom-call | tf_op jit(solution)/shard_map/finish/pallas_call | solution.py:549
Async XLA Ops:
  1.8 13.5 %collective-permute-start = (f32[5,8,256]{2,1,0:T(8,128)S(1)}, f32[5,8,256]{2,1,0:T(8,128)S(1)}, u32[]{:S(2)}, u32[]{:S(2)}) collective-permute-start(f32[5,8,256]{2,1,0:T(8,128)S(1)} %sums.1), channel_id=1, source_target_pairs={{0,8},{8,16},{16,24},{24,32},{32,40},{40,48},{48,56},{56,64},{64,7... | collective-permute-start | bytes 122888 | tf_op jit(solution)/shard_map/ppermute | solution.py:512
  13.7 1.6 %copy-start = (f32[4,32,128]{2,1,0:T(8,128)S(1)}, f32[4,32,128]{2,1,0:T(8,128)}, u32[]{:S(2)}) copy-start(f32[4,32,128]{2,1,0:T(8,128)} %constant.8.clone.tab) | copy-start | bytes 196612

commit v6 on v5

--- a/solution.py
+++ b/solution.py
@@ -15,6 +15,7 @@
 SECOND_A = 12.0 / 11.0
 SECOND_B = 3.0 / 11.0
 MESH = pl.DeviceIdType.MESH
+LIMIT = 28 * 1024 * 1024
 STRIP = 24
 REACH = 32
 FULL = 128
@@ -200,21 +201,21 @@
     tab_hbm,
     mats_hbm,
     gx,
-    gy,
-    dif,
     kx,
     kap,
-    xc,
+    curv,
+    gy,
+    ky,
+    yends,
+    xh,
+    edges,
     fld,
     tab,
     mats,
-    curv,
-    ky,
     xs,
     xr,
     ys,
     yr,
-    xh,
     in_sem,
     send_sem,
     recv_sem,
@@ -222,7 +223,7 @@
     above_ready,
 ):
     planes, cells_x, cells_y = fld.shape
-    top = cells_x - STRIP
+    half = planes // 2
     loads = []
 
     def load(source, target):
@@ -231,16 +232,13 @@
         loads.append(copy)
         return copy
 
-    def load_rows(rows):
-        return [
-            load(f_hbm.at[:, rows, :], fld.at[:, rows, :]),
-            load(k_hbm.at[:, rows, :], kap.at[:, rows, :]),
-        ]
-
-    high_loads = load_rows(pl.ds(top, STRIP)) + [load(tab_hbm, tab)]
-    low_loads = load_rows(pl.ds(0, STRIP))
-    middle_loads = load_rows(pl.ds(STRIP, top - STRIP))
-    table_load = load(mats_hbm, mats)
+    table_load = load(tab_hbm, tab)
+    field_loads = []
+    for part in (pl.ds(0, half), pl.ds(half, half)):
+        field_loads.append(
+            [load(f_hbm.at[part], fld.at[part]), load(k_hbm.at[part], kap.at[part])]
+        )
+    mats_load = load(mats_hbm, mats)
 
     ix, iy = lax.axis_index("gx"), lax.axis_index("gy")
     nx, ny = counts
@@ -248,9 +246,23 @@
     right = (jnp.where(ix == nx - 1, 0, ix + 1), iy)
     below = (ix, jnp.where(iy == 0, ny - 1, iy - 1))
     above = (ix, jnp.where(iy == ny - 1, 0, iy + 1))
+    run_begins, run_ends = lax.rem(ix, RUN) == 0, lax.rem(ix, RUN) == RUN - 1
+    run_goes_on = jnp.logical_not(run_ends)
     barrier = pltpu.get_barrier_semaphore()
-    for neighbour in (left, above):
-        pl.semaphore_signal(barrier, inc=1, device_id=neighbour, device_id_type=MESH)
+
+    def tell(semaphore, neighbour):
+        pl.semaphore_signal(semaphore, inc=1, device_id=neighbour, device_id_type=MESH)
+
+    tell(barrier, left)
+    tell(barrier, above)
+    pl.when(run_goes_on)(lambda: tell(barrier, below))
+
+    def meet():
+        pl.semaphore_wait(barrier, jnp.where(run_ends, 2, 3))
+        tell(left_ready, right)
+        pl.when(run_ends)(lambda: tell(above_ready, below))
+
+    pl.when(run_ends)(meet)
 
     def message(place, source, target, device):
         return pltpu.make_async_remote_copy(
@@ -262,41 +274,21 @@
             device_id_type=MESH,
         )
 
-    def send(*what):
-        copy = message(*what)
-        copy.start()
-        return copy
-
-    def take_x_edge(side, edge):
-        for p in range(planes):
-            xs[side, 0, p : p + 1, :] = fld[p, edge : edge + 1, :]
-            xs[side, 1, p : p + 1, :] = kap[p, edge : edge + 1, :]
-
-    def sum_x_edge(side, start, place):
-        with_first, with_second = twice(tab[place, 0:STRIP]), twice(tab[place + 1, 0:STRIP])
-        for p in range(planes):
-            rows = fld[p, start : start + STRIP, :]
-            krows = kap[p, start : start + STRIP, :]
-            xs[side, 2, p : p + 1, :] = jnp.sum(rows * with_first, axis=0, keepdims=True)
-            xs[side, 3, p : p + 1, :] = jnp.sum(rows * with_second, axis=0, keepdims=True)
-            xs[side, 4, p : p + 1, :] = jnp.sum(krows * with_first, axis=0, keepdims=True)
-
-    for copy in high_loads:
-        copy.wait()
-    take_x_edge(1, cells_x - 1)
-    pl.semaphore_wait(barrier, 2)
-    pl.semaphore_signal(left_ready, inc=1, device_id=right, device_id_type=MESH)
-    pl.semaphore_signal(above_ready, inc=1, device_id=below, device_id_type=MESH)
-    for copy in low_loads:
-        copy.wait()
-    take_x_edge(0, 0)
-    sum_x_edge(0, 0, 2)
-
-    for copy in middle_loads:
-        copy.wait()
+    to_left = message(0, xs, xr, left)
+    to_below = message(1, ys.at[0], yr.at[1], below)
+    to_above = message(2, ys.at[1], yr.at[0], above)
+
+    def send_left():
+        pl.semaphore_wait(left_ready, 1)
+        to_left.start()
+
     ys[:, :, 5:8, :] = jnp.zeros((2, planes, 3, 128), jnp.float32)
     lane = lax.broadcasted_iota(jnp.int32, (cells_x, 128), 1)
+    table_load.wait()
     for p in range(planes):
+        if p % half == 0:
+            for copy in field_loads[p // half]:
+                copy.wait()
         f_low, f_high = fld[p, :, 0:128], fld[p, :, cells_y - 128 : cells_y]
         k_low, k_high = kap[p, :, 0:128], kap[p, :, cells_y - 128 : cells_y]
         packed = jnp.where(
@@ -319,24 +311,23 @@
             ys[side, p, 2:3, :] = f_edge
             ys[side, p, 3:4, :] = jnp.sum(k_part * with_first, axis=0, keepdims=True)
             ys[side, p, 4:5, :] = k_edge
-    to_below = send(3, ys.at[0], yr.at[1], below)
-    pl.semaphore_wait(above_ready, 1)
-    to_above = send(4, ys.at[1], yr.at[0], above)
-
-    to_left = message(0, xs.at[0], xr.at[1], left)
-    run_begins = lax.rem(ix, RUN) == 0
-
-    def send_left():
-        pl.semaphore_wait(left_ready, 1)
-        to_left.start()
-
-    pl.when(jnp.logical_not(run_begins))(send_left)
-
-    table_load.wait()
+    with_first, with_second = twice(tab[2, 0:STRIP]), twice(tab[3, 0:STRIP])
+    for p in range(planes):
+        rows, krows = fld[p, 0:STRIP, :], kap[p, 0:STRIP, :]
+        xs[0, p : p + 1, :] = fld[p, 0:1, :]
+        xs[1, p : p + 1, :] = kap[p, 0:1, :]
+        xs[2, p : p + 1, :] = jnp.sum(rows * with_first, axis=0, keepdims=True)
+        xs[3, p : p + 1, :] = jnp.sum(rows * with_second, axis=0, keepdims=True)
+        xs[4, p : p + 1, :] = jnp.sum(krows * with_first, axis=0, keepdims=True)
+        edges[0, p : p + 1, :] = fld[p, 0:1, :]
+        edges[1, p : p + 1, :] = kap[p, 0:1, :]
+        edges[2, p : p + 1, :] = fld[p, cells_x - 1 : cells_x, :]
+        edges[3, p : p + 1, :] = kap[p, cells_x - 1 : cells_x, :]
+
+    mats_load.wait()
     x_rows = 4 * cells_x
     y_first = slice(x_rows, x_rows + 3 * cells_y)
     y_second = slice(x_rows + 3 * cells_y, x_rows + 6 * cells_y)
-    end_rows = x_rows + 6 * cells_y
 
     def local_pair(pair, carry):
         tall, ktall = [], []
@@ -363,86 +354,90 @@
             curv[p] = curv[p] + bend[q * cells_x : (q + 1) * cells_x]
         return carry
 
-    lax.fori_loop(0, planes // 2, local_pair, 0)
+    pairs = planes // 2
+    lax.fori_loop(0, pairs // 2, local_pair, 0)
+
+    pl.when(run_goes_on)(meet)
+    to_below.start()
+    pl.when(run_ends)(lambda: pl.semaphore_wait(above_ready, 1))
+    to_above.start()
+    pl.when(jnp.logical_not(run_begins))(send_left)
+
+    lax.fori_loop(pairs // 2, pairs, local_pair, 0)
 
     to_below.wait_recv()
     to_above.wait_recv()
     row = lax.broadcasted_iota(jnp.int32, (8, 128), 0)
     is_edge = (row == 2) | (row == 4)
-
-    def finish_pair(pair, carry):
+    for p in range(planes):
+        from_below, from_above = yr[0, p], yr[1, p]
+        yends[p, 0:8] = jnp.where(is_edge, ys[0, p] - from_below, from_below)
+        yends[p, 8:16] = jnp.where(is_edge, from_above - ys[1, p], from_above)
+    to_below.wait_send()
+    to_above.wait_send()
+
+    pl.when(run_begins)(send_left)
+    to_left.wait_recv()
+    jump, kjump = xr[0] - edges[2], xr[1] - edges[3]
+    xh[0] = FIRST.rho * xr[2] + jump
+    xh[1] = SECOND.rho * xr[3] + jump
+    xh[2] = jump
+    xh[3] = FIRST.rho * xr[4] + kjump
+    xh[4] = kjump
+    to_left.wait_send()
+
+
+def bulk_kernel(
+    gx, kx, kap, curv, gy, ky, yends, xh, tab, ends, dif_low, gx_out, gy_out, dif_out, gyf, dif, gh, sem
+):
+    planes, cells_x, cells_y = gx.shape
+    top = cells_x - STRIP
+    rest, high_rows = pl.ds(STRIP, top), pl.ds(top, STRIP)
+    inner_rows, inner = pl.ds(STRIP, top - STRIP), slice(STRIP, top)
+    copies = []
+
+    def store(source, target):
+        copy = pltpu.make_async_copy(source, target, sem.at[len(copies)])
+        copy.start()
+        copies.append(copy)
+
+    store(gx.at[:, inner_rows, :], gx_out.at[:, inner_rows, :])
+    columns = [twice(tab[n, 0:STRIP]) for n in (0, 1)] + [twice(tab[n, 0:8]) for n in (2, 3)]
+    for pair in range(planes // 2):
         stacks = []
         for q in range(2):
-            p = 2 * pair + q
-            from_below, from_above = yr[0, p], yr[1, p]
-            from_below = jnp.where(is_edge, ys[0, p] - from_below, from_below)
-            from_above = jnp.where(is_edge, from_above - ys[1, p], from_above)
-            ends = jnp.concatenate([from_below, from_above], axis=0)
-            high = ends.astype(jnp.bfloat16).astype(jnp.float32)
+            values = yends[2 * pair + q]
+            high = values.astype(jnp.bfloat16).astype(jnp.float32)
             blank = jnp.zeros((FULL - 48, cells_x), jnp.float32)
-            stacks.append(jnp.concatenate([high, ends - high, high, blank], axis=0).T)
+            stacks.append(jnp.concatenate([high, values - high, high, blank], axis=0).T)
         turned = jnp.concatenate(stacks, axis=0).astype(jnp.bfloat16)
-        reach = [
-            matmul(turned, mats[end_rows + n * FULL : end_rows + (n + 1) * FULL, :]) for n in range(3)
-        ]
+        reach = [matmul(turned, ends[n * FULL : (n + 1) * FULL, :]) for n in range(3)]
         for q in range(2):
             p = 2 * pair + q
             rows = slice(q * cells_x, (q + 1) * cells_x)
             grad = gy[p] + reach[0][rows]
-            gy[p] = grad
+            gyf[p] = grad
             part = kap[p] * (curv[p] + reach[1][rows]) + (ky[p] + reach[2][rows]) * grad
-            inner = slice(STRIP, top)
-            dif[p, 0:STRIP, :] = part[0:STRIP]
+            dif_low[p] = part[0:STRIP]
             dif[p, inner, :] = part[inner] + kx[p, inner, :] * gx[p, inner, :]
-            dif[p, top:, :] = part[top:]
-        return carry
-
-    lax.fori_loop(0, planes // 2, finish_pair, 0)
-    pl.when(run_begins)(send_left)
-
-    def combine(side, out):
-        sign = 1.0 if side == 0 else -1.0
-        jump = sign * (xs[side, 0] - xr[side, 0])
-        kjump = sign * (xs[side, 1] - xr[side, 1])
-        out[0] = FIRST.rho * xr[side, 2] + jump
-        out[1] = SECOND.rho * xr[side, 3] + jump
-        out[2] = jump
-        out[3] = FIRST.rho * xr[side, 4] + kjump
-        out[4] = kjump
-
-    to_left.wait_recv()
-    combine(1, xh)
-    columns = [twice(tab[n, 0:STRIP]) for n in (8, 9)] + [twice(tab[n, 0:8]) for n in (10, 11)]
-    for p in range(planes):
-        gx[p, top:, :], dif[p, top:, :] = ends_applied(
-            1,
-            gx[p, top:, :],
-            kx[p, top:, :],
-            dif[p, top:, :],
-            kap[p, top:, :],
-            columns,
-            [xh[n, p : p + 1, :] for n in range(5)],
-        )
-    xc[0] = xs[0, 0]
-    xc[1] = xs[0, 1]
-    for copy in (to_left, to_below, to_above):
-        copy.wait_send()
-
-
-def bulk_kernel(gx, gy, dif, gx_out, gy_out, dif_out, sem):
-    rest = pl.ds(STRIP, gx.shape[1] - STRIP)
-    copies = [
-        pltpu.make_async_copy(gy, gy_out, sem.at[0]),
-        pltpu.make_async_copy(gx.at[:, rest, :], gx_out.at[:, rest, :], sem.at[1]),
-        pltpu.make_async_copy(dif.at[:, rest, :], dif_out.at[:, rest, :], sem.at[2]),
-    ]
-    for copy in copies:
-        copy.start()
+            gh[p], dif[p, top:, :] = ends_applied(
+                1,
+                gx[p, top:, :],
+                kx[p, top:, :],
+                part[top:],
+                kap[p, top:, :],
+                columns,
+                [xh[n, p : p + 1, :] for n in range(5)],
+            )
+        both = pl.ds(2 * pair, 2)
+        store(gyf.at[both], gy_out.at[both])
+        store(dif.at[both, rest, :], dif_out.at[both, rest, :])
+        store(gh.at[both], gx_out.at[both, high_rows, :])
     for copy in copies:
         copy.wait()
 
 
-def finish_kernel(gx_in, dif_in, gx, dif, kx, kap, edges, came, tab, gx_out, dif_out, gs, ds, xc, sem):
+def finish_kernel(gx_in, dif_in, gx, dif_low, kx, kap, edges, came, tab, gx_out, dif_out, gs, ds, xc, sem):
     planes = gx.shape[0]
     jump, kjump = edges[0] - came[0], edges[1] - came[1]
     xc[0] = FIRST.rho * came[2] + jump
@@ -458,7 +453,7 @@
             0,
             gx[p, 0:STRIP, :],
             kx[p, 0:STRIP, :],
-            dif[p, 0:STRIP, :],
+            dif_low[p],
             kap[p, 0:STRIP, :],
             columns,
             [xc[n, p : p + 1, :] for n in range(5)],
@@ -479,73 +474,81 @@
 def local(counts, scalar, diffusivity):
     block = scalar.shape
     planes, cells_x, cells_y = block
-    columns = sum_columns(STRIP) + sum_columns(REACH) + high_end_columns()
     tables = (
-        jnp.asarray(stacked(columns)),
-        jnp.asarray(
-            np.concatenate([x_table(cells_x), y_table(cells_y), y_end_table(cells_y)], axis=0)
-        ),
+        jnp.asarray(stacked(sum_columns(STRIP) + sum_columns(REACH))),
+        jnp.asarray(np.concatenate([x_table(cells_x), y_table(cells_y)], axis=0)),
     )
     vmem, hbm = pl.BlockSpec(memory_space=pltpu.VMEM), pl.BlockSpec(memory_space=pltpu.HBM)
     field = jax.ShapeDtypeStruct(block, jnp.float32)
     field_buffer = pltpu.VMEM(block, jnp.float32)
-    ends_shape = (5, planes, cells_y)
+    ends_shape, strip_shape = (5, planes, cells_y), (planes, STRIP, cells_y)
+    strip_buffer = pltpu.VMEM(strip_shape, jnp.float32)
+    y_shape = (2, planes, 8, cells_x)
     operands = [
         pltpu.with_memory_space_constraint(array, pltpu.HBM)
         for array in (scalar, diffusivity) + tables
     ]
-    strip_shape = (planes, STRIP, cells_y)
     message = pl.pallas_call(
         sums_kernel,
         out_shape=jax.ShapeDtypeStruct(ends_shape, jnp.float32),
         in_specs=[hbm] * 3,
         out_specs=vmem,
         scratch_shapes=[
-            pltpu.VMEM(strip_shape, jnp.float32),
-            pltpu.VMEM(strip_shape, jnp.float32),
+            strip_buffer,
+            strip_buffer,
             pltpu.VMEM((2, 32, 128), jnp.float32),
             pltpu.SemaphoreType.DMA((3,)),
         ],
-        compiler_params=pltpu.CompilerParams(vmem_limit_bytes=28 * 1024 * 1024),
+        compiler_params=pltpu.CompilerParams(vmem_limit_bytes=LIMIT),
         name="sums",
     )(*operands[:3])
     came = lax.ppermute(message, "gx", [(i, (i + 1) % counts[0]) for i in range(counts[0])])
-    parts = pl.pallas_call(
+    gx, kx, kap, curv, gy, ky, yends, xh, edges = pl.pallas_call(
         functools.partial(exchange_kernel, counts),
-        out_shape=(field,) * 5 + (jax.ShapeDtypeStruct((2,) + ends_shape[1:], jnp.float32),),
+        out_shape=(field,) * 6
+        + (
+            jax.ShapeDtypeStruct((planes, 16, cells_x), jnp.float32),
+            jax.ShapeDtypeStruct(ends_shape, jnp.float32),
+            jax.ShapeDtypeStruct((4, planes, cells_y), jnp.float32),
+        ),
         in_specs=[hbm] * 4,
-        out_specs=(vmem,) * 6,
+        out_specs=(vmem,) * 9,
         scratch_shapes=[field_buffer]
         + [pltpu.VMEM(table.shape, table.dtype) for table in tables]
-        + [field_buffer, field_buffer]
-        + [pltpu.VMEM((2,) + ends_shape, jnp.float32)] * 2
-        + [pltpu.VMEM((2, planes, 8, cells_x), jnp.float32)] * 2
+        + [pltpu.VMEM(ends_shape, jnp.float32)] * 2
+        + [pltpu.VMEM(y_shape, jnp.float32)] * 2
         + [
-            pltpu.VMEM(ends_shape, jnp.float32),
-            pltpu.SemaphoreType.DMA((8,)),
-            pltpu.SemaphoreType.DMA((5,)),
-            pltpu.SemaphoreType.DMA((5,)),
+            pltpu.SemaphoreType.DMA((6,)),
+            pltpu.SemaphoreType.DMA((3,)),
+            pltpu.SemaphoreType.DMA((3,)),
             pltpu.SemaphoreType.REGULAR,
             pltpu.SemaphoreType.REGULAR,
         ],
         compiler_params=pltpu.CompilerParams(
-            collective_id=0, has_side_effects=True, vmem_limit_bytes=28 * 1024 * 1024
+            collective_id=0, has_side_effects=True, vmem_limit_bytes=LIMIT
         ),
         cost_estimate=pl.CostEstimate(flops=2 * 10**9, bytes_accessed=8 * 2**20, transcendentals=0),
         name="exchange",
     )(*operands)
-    strip_buffer = pltpu.VMEM((planes, STRIP, cells_y), jnp.float32)
-    grad_x, grad_y, dif, kx, kap, edges = parts
-    gx_out, gy_out, dif_out = pl.pallas_call(
+    dif_low, gx_out, gy_out, dif_out = pl.pallas_call(
         bulk_kernel,
-        out_shape=(field,) * 3,
-        in_specs=[vmem] * 3,
-        out_specs=(hbm,) * 3,
-        scratch_shapes=[pltpu.SemaphoreType.DMA((3,))],
-        compiler_params=pltpu.CompilerParams(vmem_limit_bytes=28 * 1024 * 1024),
-        cost_estimate=pl.CostEstimate(flops=0, bytes_accessed=3 * 2**20, transcendentals=0),
+        out_shape=(jax.ShapeDtypeStruct(strip_shape, jnp.float32),) + (field,) * 3,
+        in_specs=[vmem] * 10,
+        out_specs=(vmem,) + (hbm,) * 3,
+        scratch_shapes=[
+            field_buffer,
+            field_buffer,
+            strip_buffer,
+            pltpu.SemaphoreType.DMA((1 + 3 * (planes // 2),)),
+        ],
+        compiler_params=pltpu.CompilerParams(vmem_limit_bytes=LIMIT),
+        cost_estimate=pl.CostEstimate(flops=2 * 10**8, bytes_accessed=3 * 2**20, transcendentals=0),
         name="bulk",
-    )(grad_x, grad_y, dif)
+    )(
+        *(gx, kx, kap, curv, gy, ky, yends, xh),
+        jnp.asarray(stacked(high_end_columns())),
+        jnp.asarray(y_end_table(cells_y)),
+    )
     gx_out, dif_out = pl.pallas_call(
         finish_kernel,
         out_shape=(field,) * 2,
@@ -558,9 +561,12 @@
             pltpu.SemaphoreType.DMA((4,)),
         ],
         input_output_aliases={0: 0, 1: 1},
-        compiler_params=pltpu.CompilerParams(vmem_limit_bytes=28 * 1024 * 1024),
+        compiler_params=pltpu.CompilerParams(vmem_limit_bytes=LIMIT),
         name="finish",
-    )(gx_out, dif_out, grad_x, dif, kx, kap, edges, came, jnp.asarray(stacked(low_end_columns())))
+    )(
+        *(gx_out, dif_out, gx, dif_low, kx, kap, edges, came),
+        jnp.asarray(stacked(low_end_columns())),
+    )
     return gx_out, gy_out, dif_out
 
 

time: 16.2 us -> 16.5 us (1.019)
  the two profiles are of different devices: /device:TPU:1 before, /device:TPU:100 now
where the time goes in v6:
time: 16.5 us; the launch traced here: 16.4 us
  Pallas kernels  12.4 us (75%)
  starting transfers between devices  3.21 us (19%)
  between operations  0.71 us (4%)
    pallas_call x1, Pallas kernels, local(): pl.pallas_call(functools.partial(exchange_kernel, counts), out_shape=(fie...  8.68 us
    ppermute x1, starting transfers between devices, local(): lax.ppermute(message, 'gx', [(i, (i + 1) % counts[0]) for i in range(coun...  3.21 us
    pallas_call x1, Pallas kernels, local(): pl.pallas_call(bulk_kernel, out_shape=(jax.ShapeDtypeStruct(strip_shape,...  1.78 us
    pallas_call x1, Pallas kernels, local(): pl.pallas_call(sums_kernel, out_shape=jax.ShapeDtypeStruct(ends_shape, jn...  1.14 us
    pallas_call x1, Pallas kernels, local(): pl.pallas_call(finish_kernel, out_shape=(field,) * 2, in_specs=[hbm] * 2...  0.83 us
  transfers between devices with their start and end apart: 1, of which 0 were waited for; matrix products, arithmetic and copies ran while one was open for 0% of the time, Pallas kernels for 64%

profile of v6, /device:TPU:100, one launch (start us, length us, event | category | flops | bytes accessed | tf_op | source)
XLA Modules:
  0.0 16.4 jit_solution(13081302377986976790)
XLA Ops:
  0.6 1.1 %sums.1 = f32[5,8,256]{2,1,0:T(8,128)S(1)} custom-call(f32[8,128,256]{2,1,0:T(8,128)} %f_hbm.3, f32[8,128,256]{2,1,0:T(8,128)} %k_hbm.3, f32[8,32,128]{2,1,0:T(8,128)} %constant.10.clone.tab_hbm), custom_call_target="tpu_custom_call" | custom-call | tf_op jit(solution)/shard_map/sums/pallas_call | solution.py:491
  1.8 0.0 copy-start
  1.8 0.0 copy-start.2
  1.8 3.2 %collective-permute-start = (f32[5,8,256]{2,1,0:T(8,128)S(1)}, f32[5,8,256]{2,1,0:T(8,128)S(1)}, u32[]{:S(2)}, u32[]{:S(2)}) collective-permute-start(f32[5,8,256]{2,1,0:T(8,128)S(1)} %sums.1), channel_id=1, source_target_pairs={{0,8},{8,16},{16,24},{24,32},{32,40},{40,48},{48,56},{56,64},{64,7... | collective-permute-start | bytes 122888 | tf_op jit(solution)/shard_map/ppermute | solution.py:505
  5.0 8.7 %exchange.1 = (f32[8,128,256]{2,1,0:T(8,128)S(1)}, f32[8,128,256]{2,1,0:T(8,128)S(1)}, f32[8,128,256]{2,1,0:T(8,128)S(1)}, f32[8,128,256]{2,1,0:T(8,128)S(1)}, f...) custom-call(f32[8,128,256]{2,1,0:T(8,128)} %f_hbm.3, ...), custom_call_target="tpu_custom_call" | custom-call | flops 2000000000 | bytes 8388608 | tf_op jit(solution)/shard_map/exchange/pallas_call | solution.py:506
  13.7 0.0 copy-done
  13.7 0.0 copy-done.2
  13.7 0.0 copy-start.1
  13.7 1.8 %bulk.1 = (f32[8,24,256]{2,1,0:T(8,128)S(1)}, f32[8,128,256]{2,1,0:T(8,128)}, f32[8,128,256]{2,1,0:T(8,128)}, f32[8,128,256]{2,1,0:T(8,128)}) custom-call(f32[8,128,256]{2,1,0:T(8,128)S(1)} %get-tuple-element.18.gx, f32[8,128,256]{2,1,0:T(8,128)S(1)} %get-tuple-element.19.kx, f32[8,128,256]{2,1,0:T(8,128)S(1)} %get-tuple-element.20.kap, ...), custom_call_target="tpu_custom_call" | custom-call | flops 200000000 | bytes 3145728 | tf_op jit(solution)/shard_map/bulk/pallas_call | solution.py:533
  15.5 0.0 collective-permute-done.came
  15.5 0.0 copy-done.1
  15.5 0.8 %finish.1 = (f32[8,128,256]{2,1,0:T(8,128)}, f32[8,128,256]{2,1,0:T(8,128)}) custom-call(f32[8,128,256]{2,1,0:T(8,128)} %get-tuple-element.26.gx_in, f32[8,128,256]{2,1,0:T(8,128)} %get-tuple-element.27.dif_in, f32[8,128,256]{2,1,0:T(8,128)S(1)} %get-tuple-element.18.gx, ...), custom_call_target="tpu_custom_call", output_to_operand_aliasing={{0}: (0, {}), {1}: (1, {})} | custom-call | tf_op jit(solution)/shard_map/finish/pallas_call | solution.py:552
Async XLA Ops:
  1.8 11.9 %copy-start = (bf16[384,256]{1,0:T(8,128)(2,1)S(1)}, bf16[384,256]{1,0:T(8,128)(2,1)}, u32[]{:S(2)}) copy-start(bf16[384,256]{1,0:T(8,128)(2,1)} %constant.13.clone.ends) | copy-start | bytes 589828
  1.8 11.9 %copy-start.2 = (f32[4,32,128]{2,1,0:T(8,128)S(1)}, f32[4,32,128]{2,1,0:T(8,128)}, u32[]{:S(2)}) copy-start(f32[4,32,128]{2,1,0:T(8,128)} %constant.12.clone.tab) | copy-start | bytes 196612
  1.8 13.7 %collective-permute-start = (f32[5,8,256]{2,1,0:T(8,128)S(1)}, f32[5,8,256]{2,1,0:T(8,128)S(1)}, u32[]{:S(2)}, u32[]{:S(2)}) collective-permute-start(f32[5,8,256]{2,1,0:T(8,128)S(1)} %sums.1), channel_id=1, source_target_pairs={{0,8},{8,16},{16,24},{24,32},{32,40},{40,48},{48,56},{56,64},{64,7... | collective-permute-start | bytes 122888 | tf_op jit(solution)/shard_map/ppermute | solution.py:505
  13.7 1.8 %copy-start.1 = (f32[4,32,128]{2,1,0:T(8,128)S(1)}, f32[4,32,128]{2,1,0:T(8,128)}, u32[]{:S(2)}) copy-start(f32[4,32,128]{2,1,0:T(8,128)} %constant.14.clone.tab) | copy-start | bytes 196612

commit v7 on v3

--- a/solution.py
+++ b/solution.py
@@ -15,6 +15,7 @@
 SECOND_A = 12.0 / 11.0
 SECOND_B = 3.0 / 11.0
 MESH = pl.DeviceIdType.MESH
+LIMIT = 28 * 1024 * 1024
 STRIP = 24
 REACH = 32
 FULL = 128
@@ -172,6 +173,30 @@
     return jnp.concatenate(grads, axis=0), jnp.concatenate(parts, axis=0)
 
 
+def sums_kernel(last, f_hbm, k_hbm, tab_hbm, out, fst, kst, tab, sem):
+    planes, cells_x = f_hbm.shape[0], f_hbm.shape[1]
+    rows = pl.ds(cells_x - STRIP, STRIP)
+    copies = [
+        pltpu.make_async_copy(f_hbm.at[:, rows, :], fst, sem.at[0]),
+        pltpu.make_async_copy(k_hbm.at[:, rows, :], kst, sem.at[1]),
+        pltpu.make_async_copy(tab_hbm.at[0:2], tab, sem.at[2]),
+    ]
+
+    @pl.when(lax.axis_index("gx") == last)
+    def work():
+        for copy in copies:
+            copy.start()
+        for copy in copies:
+            copy.wait()
+        with_first, with_second = twice(tab[0, 0:STRIP]), twice(tab[1, 0:STRIP])
+        for p in range(planes):
+            out[0, p : p + 1, :] = fst[p, STRIP - 1 : STRIP, :]
+            out[1, p : p + 1, :] = kst[p, STRIP - 1 : STRIP, :]
+            out[2, p : p + 1, :] = jnp.sum(fst[p] * with_first, axis=0, keepdims=True)
+            out[3, p : p + 1, :] = jnp.sum(fst[p] * with_second, axis=0, keepdims=True)
+            out[4, p : p + 1, :] = jnp.sum(kst[p] * with_first, axis=0, keepdims=True)
+
+
 def exchange_kernel(
     counts,
     f_hbm,
@@ -184,6 +209,7 @@
     kx,
     kap,
     xc,
+    edges,
     fld,
     tab,
     mats,
@@ -264,9 +290,14 @@
         copy.wait()
     take_x_edge(1, cells_x - 1)
     pl.semaphore_wait(barrier, 2)
-    to_right = [send(1, xs.at[1, 0:2], xr.at[0, 0:2], right)]
+    sends_right, hears_left = ix != nx - 1, ix != 0
+    to_right = [
+        message(1, xs.at[1, 0:2], xr.at[0, 0:2], right),
+        message(2, xs.at[1, 2:5], xr.at[0, 2:5], right),
+    ]
+    pl.when(sends_right)(to_right[0].start)
     sum_x_edge(1, top, 0)
-    to_right.append(send(2, xs.at[1, 2:5], xr.at[0, 2:5], right))
+    pl.when(sends_right)(to_right[1].start)
     pl.semaphore_signal(left_ready, inc=1, device_id=right, device_id_type=MESH)
     pl.semaphore_signal(above_ready, inc=1, device_id=below, device_id_type=MESH)
     for copy in low_loads:
@@ -405,28 +436,25 @@
             columns,
             [xh[n, p : p + 1, :] for n in range(5)],
         )
-    for copy in [to_left, to_below, to_above] + to_right:
+    edges[...] = xs[0, 0:2]
+    for copy in (to_left, to_below, to_above):
         copy.wait_send()
-    for copy in to_right:
-        copy.wait_recv()
-    combine(0, xc)
-
-
-def finish_kernel(gx, gy, dif, kx, kap, xc, tab, gx_out, gy_out, dif_out, gs, ds, sem):
-    planes, cells_x, cells_y = gx.shape
-    copies = []
-
-    def store(source, target):
-        copy = pltpu.make_async_copy(source, target, sem.at[len(copies)])
-        copy.start()
-        copies.append(copy)
-
-    rest = pl.ds(STRIP, cells_x - STRIP)
-    store(gy, gy_out)
-    store(gx.at[:, rest, :], gx_out.at[:, rest, :])
-    store(dif.at[:, rest, :], dif_out.at[:, rest, :])
+
+    @pl.when(sends_right)
+    def sent():
+        for copy in to_right:
+            copy.wait_send()
+
+    @pl.when(hears_left)
+    def hear():
+        for copy in to_right:
+            copy.wait_recv()
+        combine(0, xc)
+
+
+def low_rows(gx, dif, kx, kap, values, tab, gs, ds):
     columns = [twice(tab[n, 0:STRIP]) for n in (0, 1)] + [twice(tab[n, 0:8]) for n in (2, 3)]
-    for p in range(planes):
+    for p in range(gx.shape[0]):
         gs[p], ds[p] = ends_applied(
             0,
             gx[p, 0:STRIP, :],
@@ -434,12 +462,56 @@
             dif[p, 0:STRIP, :],
             kap[p, 0:STRIP, :],
             columns,
-            [xc[n, p : p + 1, :] for n in range(5)],
+            [values[n, p : p + 1, :] for n in range(5)],
         )
-    store(gs, gx_out.at[:, pl.ds(0, STRIP), :])
-    store(ds, dif_out.at[:, pl.ds(0, STRIP), :])
+
+
+def low_copies(gs, ds, gx_out, dif_out, sem):
+    low = pl.ds(0, STRIP)
+    return [
+        pltpu.make_async_copy(gs, gx_out.at[:, low, :], sem.at[0]),
+        pltpu.make_async_copy(ds, dif_out.at[:, low, :], sem.at[1]),
+    ]
+
+
+def bulk_kernel(gx, gy, dif, kx, kap, xc, tab, gx_out, gy_out, dif_out, gs, ds, sem, low_sem):
+    rest = pl.ds(STRIP, gx.shape[1] - STRIP)
+    copies = [
+        pltpu.make_async_copy(gy, gy_out, sem.at[0]),
+        pltpu.make_async_copy(gx.at[:, rest, :], gx_out.at[:, rest, :], sem.at[1]),
+        pltpu.make_async_copy(dif.at[:, rest, :], dif_out.at[:, rest, :], sem.at[2]),
+    ]
+    for copy in copies:
+        copy.start()
+
+    @pl.when(lax.axis_index("gx") != 0)
+    def low():
+        low_rows(gx, dif, kx, kap, xc, tab, gs, ds)
+        for copy in low_copies(gs, ds, gx_out, dif_out, low_sem):
+            copy.start()
+        for copy in low_copies(gs, ds, gx_out, dif_out, low_sem):
+            copy.wait()
+
     for copy in copies:
         copy.wait()
+
+
+def finish_kernel(
+    gx_in, dif_in, gx, dif, kx, kap, edges, came, tab, gx_out, dif_out, gs, ds, values, low_sem
+):
+    @pl.when(lax.axis_index("gx") == 0)
+    def low():
+        jump, kjump = edges[0] - came[0], edges[1] - came[1]
+        values[0] = FIRST.rho * came[2] + jump
+        values[1] = SECOND.rho * came[3] + jump
+        values[2] = jump
+        values[3] = FIRST.rho * came[4] + kjump
+        values[4] = kjump
+        low_rows(gx, dif, kx, kap, values, tab, gs, ds)
+        for copy in low_copies(gs, ds, gx_out, dif_out, low_sem):
+            copy.start()
+        for copy in low_copies(gs, ds, gx_out, dif_out, low_sem):
+            copy.wait()
 
 
 def local(counts, scalar, diffusivity):
@@ -460,11 +532,29 @@
         pltpu.with_memory_space_constraint(array, pltpu.HBM)
         for array in (scalar, diffusivity) + tables
     ]
+    strip_shape = (planes, STRIP, cells_y)
+    strip_buffer = pltpu.VMEM(strip_shape, jnp.float32)
+    last = counts[0] - 1
+    message = pl.pallas_call(
+        functools.partial(sums_kernel, last),
+        out_shape=jax.ShapeDtypeStruct(ends_shape, jnp.float32),
+        in_specs=[hbm] * 3,
+        out_specs=vmem,
+        scratch_shapes=[
+            strip_buffer,
+            strip_buffer,
+            pltpu.VMEM((2, 32, 128), jnp.float32),
+            pltpu.SemaphoreType.DMA((3,)),
+        ],
+        compiler_params=pltpu.CompilerParams(vmem_limit_bytes=LIMIT),
+        name="sums",
+    )(*operands[:3])
+    came = lax.ppermute(message, "gx", [(last, 0)])
     parts = pl.pallas_call(
         functools.partial(exchange_kernel, counts),
-        out_shape=(field,) * 5 + (jax.ShapeDtypeStruct(ends_shape, jnp.float32),),
+        out_shape=(field,) * 5 + (jax.ShapeDtypeStruct(ends_shape, jnp.float32), jax.ShapeDtypeStruct((2,) + ends_shape[1:], jnp.float32)),
         in_specs=[hbm] * 4,
-        out_specs=(vmem,) * 6,
+        out_specs=(vmem,) * 7,
         scratch_shapes=[field_buffer]
         + [pltpu.VMEM(table.shape, table.dtype) for table in tables]
         + [field_buffer, field_buffer]
@@ -479,20 +569,37 @@
             pltpu.SemaphoreType.REGULAR,
         ],
         compiler_params=pltpu.CompilerParams(
-            collective_id=0, has_side_effects=True, vmem_limit_bytes=28 * 1024 * 1024
+            collective_id=0, has_side_effects=True, vmem_limit_bytes=LIMIT
         ),
+        cost_estimate=pl.CostEstimate(flops=2 * 10**9, bytes_accessed=8 * 2**20, transcendentals=0),
         name="exchange",
     )(*operands)
-    strip_buffer = pltpu.VMEM((planes, STRIP, cells_y), jnp.float32)
-    return pl.pallas_call(
-        finish_kernel,
+    grad_x, grad_y, dif, kx, kap, xc, edges = parts
+    tab = jnp.asarray(stacked(low_end_columns()))
+    low_scratch = [strip_buffer, strip_buffer]
+    gx_out, gy_out, dif_out = pl.pallas_call(
+        bulk_kernel,
         out_shape=(field,) * 3,
         in_specs=[vmem] * 7,
         out_specs=(hbm,) * 3,
-        scratch_shapes=[strip_buffer, strip_buffer, pltpu.SemaphoreType.DMA((5,))],
-        compiler_params=pltpu.CompilerParams(vmem_limit_bytes=28 * 1024 * 1024),
+        scratch_shapes=low_scratch
+        + [pltpu.SemaphoreType.DMA((3,)), pltpu.SemaphoreType.DMA((2,))],
+        compiler_params=pltpu.CompilerParams(vmem_limit_bytes=LIMIT),
+        cost_estimate=pl.CostEstimate(flops=0, bytes_accessed=3 * 2**20, transcendentals=0),
+        name="bulk",
+    )(grad_x, grad_y, dif, kx, kap, xc, tab)
+    gx_out, dif_out = pl.pallas_call(
+        finish_kernel,
+        out_shape=(field,) * 2,
+        in_specs=[hbm] * 2 + [vmem] * 7,
+        out_specs=(hbm,) * 2,
+        scratch_shapes=low_scratch
+        + [pltpu.VMEM(ends_shape, jnp.float32), pltpu.SemaphoreType.DMA((2,))],
+        input_output_aliases={0: 0, 1: 1},
+        compiler_params=pltpu.CompilerParams(vmem_limit_bytes=LIMIT),
         name="finish",
-    )(*parts, jnp.asarray(stacked(low_end_columns())))
+    )(gx_out, dif_out, grad_x, dif, kx, kap, edges, came, tab)
+    return gx_out, gy_out, dif_out
 
 
 def solution(mesh):

time: 13.8 us -> 17 us (1.23)
  Pallas kernels: 13 us -> 14.7 us
  starting transfers between devices: 0 us -> 1.42 us
    ppermute x0 -> x1, starting transfers between devices: none -> 1.42 us  [local(): came = lax.ppermute(message, 'gx', [(last, 0)])]
    pallas_call x1, Pallas kernels: 11.3 us -> 12.2 us  [local(): pl.pallas_call(functools.partial(exchange_kernel, counts), out_shape=(fie...]
    pallas_call x1 -> x3, Pallas kernels: 1.7 us -> 2.49 us  [the longest x1 1.58 us: local(): pl.pallas_call(bulk_kernel, out_shape=(field,) * 3, in_specs=[vmem] * 7,...]
  transfers between devices with their start and end apart: 0 -> 1, of which waited for: 0 -> 0; matrix products, arithmetic and copies ran while one was open for 0% -> 0% of each run, Pallas kernels for 0% -> 82%
where the time goes in v7:
time: 17 us; the launch traced here: 16.8 us
  Pallas kernels  14.7 us (86%)
  starting transfers between devices  1.42 us (8%)
  between operations  0.68 us (4%)
    pallas_call x1, Pallas kernels, local(): pl.pallas_call(functools.partial(exchange_kernel, counts), out_shape=(fie...  12.2 us
    pallas_call x1, Pallas kernels, local(): pl.pallas_call(bulk_kernel, out_shape=(field,) * 3, in_specs=[vmem] * 7,...  1.58 us
    ppermute x1, starting transfers between devices, local(): came = lax.ppermute(message, 'gx', [(last, 0)])  1.42 us
    pallas_call x1, Pallas kernels, local(): pl.pallas_call(finish_kernel, out_shape=(field,) * 2, in_specs=[hbm] * 2...  0.87 us
  transfers between devices with their start and end apart: 1, of which 0 were waited for; matrix products, arithmetic and copies ran while one was open for 0% of the time, Pallas kernels for 82%

profile of v7, /device:TPU:1, one launch (start us, length us, event | category | flops | bytes accessed | tf_op | source)
XLA Modules:
  0.0 16.8 jit_solution(774403729850785168)
XLA Ops:
  0.7 0.0 copy-start
  0.7 1.4 %collective-permute-start = (f32[5,8,256]{2,1,0:T(8,128)S(1)}, f32[5,8,256]{2,1,0:T(8,128)S(1)}, u32[]{:S(2)}, u32[]{:S(2)}) collective-permute-start(f32[5,8,256]{2,1,0:T(8,128)S(1)} %sums.1), channel_id=1, source_target_pairs={{248,0},{249,1},{250,2},{251,3},{252,4},{253,5},{254,6},{255,7}} | collective-permute-start | bytes 122888 | tf_op jit(solution)/shard_map/ppermute | solution.py:552
  2.1 12.2 %exchange.1 = (f32[8,128,256]{2,1,0:T(8,128)S(1)}, f32[8,128,256]{2,1,0:T(8,128)S(1)}, f32[8,128,256]{2,1,0:T(8,128)S(1)}, f32[8,128,256]{2,1,0:T(8,128)S(1)}, f...) custom-call(f32[8,128,256]{2,1,0:T(8,128)} %f_hbm.3, f32[8,128,256]{2,1,0:T(8,128)} %k_hbm.3, ...), custom_call_target="tpu_custom_call" | custom-call | flops 2000000000 | bytes 8388608 | tf_op jit(solution)/shard_map/exchange/pallas_call | solution.py:553
  14.3 0.0 copy-done
  14.4 1.6 %bulk.1 = (f32[8,128,256]{2,1,0:T(8,128)}, f32[8,128,256]{2,1,0:T(8,128)}, f32[8,128,256]{2,1,0:T(8,128)}) custom-call(f32[8,128,256]{2,1,0:T(8,128)S(1)} %get-tuple-element.15.gx, f32[8,128,256]{2,1,0:T(8,128)S(1)} %get-tuple-element.16.gy, f32[8,128,256]{2,1,0:T(8,128)S(1)} %get-tuple-element.17.dif, f32[8,128,256]{2,1,0:T(8,128)S(1)} %get-tuple-element.18.kx, ...), custom_call_target="tpu_custom_call" | custom-call | bytes 3145728 | tf_op jit(solution)/shard_map/bulk/pallas_call | solution.py:580
  15.9 0.0 collective-permute-done.came
  15.9 0.9 %finish.1 = (f32[8,128,256]{2,1,0:T(8,128)}, f32[8,128,256]{2,1,0:T(8,128)}) custom-call(f32[8,128,256]{2,1,0:T(8,128)} %get-tuple-element.21.gx_in, f32[8,128,256]{2,1,0:T(8,128)} %get-tuple-element.22.dif_in, f32[8,128,256]{2,1,0:T(8,128)S(1)} %get-tuple-element.15.gx, ...), custom_call_target="tpu_custom_call", output_to_operand_aliasing={{0}: (0, {}), {1}: (1, {})} | custom-call | tf_op jit(solution)/shard_map/finish/pallas_call | solution.py:591
  (1 shorter events, 0.0 us)
Async XLA Ops:
  0.7 13.7 %copy-start = (f32[4,32,128]{2,1,0:T(8,128)S(1)}, f32[4,32,128]{2,1,0:T(8,128)}, u32[]{:S(2)}) copy-start(f32[4,32,128]{2,1,0:T(8,128)} %constant.8.clone.tab) | copy-start | bytes 196612
  0.7 15.2 %collective-permute-start = (f32[5,8,256]{2,1,0:T(8,128)S(1)}, f32[5,8,256]{2,1,0:T(8,128)S(1)}, u32[]{:S(2)}, u32[]{:S(2)}) collective-permute-start(f32[5,8,256]{2,1,0:T(8,128)S(1)} %sums.1), channel_id=1, source_target_pairs={{248,0},{249,1},{250,2},{251,3},{252,4},{253,5},{254,6},{255,7}} | collective-permute-start | bytes 122888 | tf_op jit(solution)/shard_map/ppermute | solution.py:552

commit v8 on v3

--- a/solution.py
+++ b/solution.py
@@ -15,7 +15,9 @@
 SECOND_A = 12.0 / 11.0
 SECOND_B = 3.0 / 11.0
 MESH = pl.DeviceIdType.MESH
+LIMIT = 28 * 1024 * 1024
 STRIP = 24
+SHORT = 16
 REACH = 32
 FULL = 128
 RUN = 8
@@ -80,8 +82,8 @@
     return table
 
 
-def sum_columns(reach):
-    low = [FIRST.low_sum(reach), SECOND.low_sum(reach)]
+def sum_columns(reach, short):
+    low = [FIRST.low_sum(reach), SECOND.low_sum(short)]
     return [-row[::-1] for row in low] + low
 
 
@@ -216,9 +218,10 @@
             load(k_hbm.at[:, rows, :], kap.at[:, rows, :]),
         ]
 
-    high_loads = load_rows(pl.ds(top, STRIP)) + [load(tab_hbm, tab)]
-    low_loads = load_rows(pl.ds(0, STRIP))
-    middle_loads = load_rows(pl.ds(STRIP, top - STRIP))
+    top_rows, other_rows = pl.ds(top, STRIP), pl.ds(0, top)
+    weights_load = load(tab_hbm.at[0:2], tab.at[0:2])
+    f_high_load, k_high_load = load_rows(top_rows)
+    other_loads = [load(tab_hbm.at[2:], tab.at[2:])] + load_rows(other_rows)
     table_load = load(mats_hbm, mats)
 
     ix, iy = lax.axis_index("gx"), lax.axis_index("gy")
@@ -231,6 +234,9 @@
     for neighbour in (left, above):
         pl.semaphore_signal(barrier, inc=1, device_id=neighbour, device_id_type=MESH)
 
+    def tell(semaphore, neighbour):
+        pl.semaphore_signal(semaphore, inc=1, device_id=neighbour, device_id_type=MESH)
+
     def message(place, source, target, device):
         return pltpu.make_async_remote_copy(
             src_ref=source,
@@ -246,36 +252,46 @@
         copy.start()
         return copy
 
-    def take_x_edge(side, edge):
-        for p in range(planes):
-            xs[side, 0, p : p + 1, :] = fld[p, edge : edge + 1, :]
-            xs[side, 1, p : p + 1, :] = kap[p, edge : edge + 1, :]
-
-    def sum_x_edge(side, start, place):
-        with_first, with_second = twice(tab[place, 0:STRIP]), twice(tab[place + 1, 0:STRIP])
+    def f_sums(side, start, place):
+        with_first, with_second = twice(tab[place, 0:STRIP]), twice(tab[place + 1, 0:SHORT])
+        near = start if side == 0 else start + STRIP - SHORT
         for p in range(planes):
             rows = fld[p, start : start + STRIP, :]
-            krows = kap[p, start : start + STRIP, :]
+            few = fld[p, near : near + SHORT, :]
             xs[side, 2, p : p + 1, :] = jnp.sum(rows * with_first, axis=0, keepdims=True)
-            xs[side, 3, p : p + 1, :] = jnp.sum(rows * with_second, axis=0, keepdims=True)
-            xs[side, 4, p : p + 1, :] = jnp.sum(krows * with_first, axis=0, keepdims=True)
-
-    for copy in high_loads:
+            xs[side, 3, p : p + 1, :] = jnp.sum(few * with_second, axis=0, keepdims=True)
+
+    def k_sums(side, start, place):
+        with_first = twice(tab[place, 0:STRIP])
+        for p in range(planes):
+            rows = kap[p, start : start + STRIP, :]
+            xs[side, 4, p : p + 1, :] = jnp.sum(rows * with_first, axis=0, keepdims=True)
+
+    def take_edge(side, place, field, edge):
+        for p in range(planes):
+            xs[side, place, p : p + 1, :] = field[p, edge : edge + 1, :]
+
+    f_high_load.wait()
+    take_edge(1, 0, fld, cells_x - 1)
+    pl.semaphore_wait(barrier, 2)
+    send(1, xs.at[1, 0:1], xr.at[0, 0:1], right)
+    weights_load.wait()
+    f_sums(1, top, 0)
+    k_high_load.wait()
+    take_edge(1, 1, kap, cells_x - 1)
+    send(1, xs.at[1, 1:4], xr.at[0, 1:4], right)
+    k_sums(1, top, 0)
+    send(1, xs.at[1, 4:5], xr.at[0, 4:5], right)
+    to_right = message(1, xs.at[1], xr.at[0], right)
+    tell(left_ready, right)
+    tell(above_ready, below)
+    for copy in other_loads:
         copy.wait()
-    take_x_edge(1, cells_x - 1)
-    pl.semaphore_wait(barrier, 2)
-    to_right = [send(1, xs.at[1, 0:2], xr.at[0, 0:2], right)]
-    sum_x_edge(1, top, 0)
-    to_right.append(send(2, xs.at[1, 2:5], xr.at[0, 2:5], right))
-    pl.semaphore_signal(left_ready, inc=1, device_id=right, device_id_type=MESH)
-    pl.semaphore_signal(above_ready, inc=1, device_id=below, device_id_type=MESH)
-    for copy in low_loads:
-        copy.wait()
-    take_x_edge(0, 0)
-    sum_x_edge(0, 0, 2)
-
-    for copy in middle_loads:
-        copy.wait()
+    take_edge(0, 0, fld, 0)
+    take_edge(0, 1, kap, 0)
+    f_sums(0, 0, 2)
+    k_sums(0, 0, 2)
+
     ys[:, :, 5:8, :] = jnp.zeros((2, planes, 3, 128), jnp.float32)
     lane = lax.broadcasted_iota(jnp.int32, (cells_x, 128), 1)
     for p in range(planes):
@@ -301,9 +317,9 @@
             ys[side, p, 2:3, :] = f_edge
             ys[side, p, 3:4, :] = jnp.sum(k_part * with_first, axis=0, keepdims=True)
             ys[side, p, 4:5, :] = k_edge
-    to_below = send(3, ys.at[0], yr.at[1], below)
+    to_below = send(2, ys.at[0], yr.at[1], below)
     pl.semaphore_wait(above_ready, 1)
-    to_above = send(4, ys.at[1], yr.at[0], above)
+    to_above = send(3, ys.at[1], yr.at[0], above)
 
     to_left = message(0, xs.at[0], xr.at[1], left)
     run_begins = lax.rem(ix, RUN) == 0
@@ -405,10 +421,9 @@
             columns,
             [xh[n, p : p + 1, :] for n in range(5)],
         )
-    for copy in [to_left, to_below, to_above] + to_right:
+    for copy in (to_left, to_below, to_above, to_right):
         copy.wait_send()
-    for copy in to_right:
-        copy.wait_recv()
+    to_right.wait_recv()
     combine(0, xc)
 
 
@@ -445,7 +460,7 @@
 def local(counts, scalar, diffusivity):
     block = scalar.shape
     planes, cells_x, cells_y = block
-    columns = sum_columns(STRIP) + sum_columns(REACH) + high_end_columns()
+    columns = sum_columns(STRIP, SHORT) + sum_columns(REACH, REACH) + high_end_columns()
     tables = (
         jnp.asarray(stacked(columns)),
         jnp.asarray(
@@ -473,13 +488,13 @@
         + [
             pltpu.VMEM(ends_shape, jnp.float32),
             pltpu.SemaphoreType.DMA((8,)),
-            pltpu.SemaphoreType.DMA((5,)),
-            pltpu.SemaphoreType.DMA((5,)),
+            pltpu.SemaphoreType.DMA((4,)),
+            pltpu.SemaphoreType.DMA((4,)),
             pltpu.SemaphoreType.REGULAR,
             pltpu.SemaphoreType.REGULAR,
         ],
         compiler_params=pltpu.CompilerParams(
-            collective_id=0, has_side_effects=True, vmem_limit_bytes=28 * 1024 * 1024
+            collective_id=0, has_side_effects=True, vmem_limit_bytes=LIMIT
         ),
         name="exchange",
     )(*operands)
@@ -490,7 +505,7 @@
         in_specs=[vmem] * 7,
         out_specs=(hbm,) * 3,
         scratch_shapes=[strip_buffer, strip_buffer, pltpu.SemaphoreType.DMA((5,))],
-        compiler_params=pltpu.CompilerParams(vmem_limit_bytes=28 * 1024 * 1024),
+        compiler_params=pltpu.CompilerParams(vmem_limit_bytes=LIMIT),
         name="finish",
     )(*parts, jnp.asarray(stacked(low_end_columns())))
 

time: 13.8 us -> 13.6 us (0.986)
  Pallas kernels: 13 us -> 12.8 us
    pallas_call x1, Pallas kernels: 11.3 us -> 11.1 us  [local(): pl.pallas_call(functools.partial(exchange_kernel, counts), out_shape=(fie...]
where the time goes in v8:
time: 13.6 us; the launch traced here: 13.5 us
  Pallas kernels  12.8 us (94%)
  between operations  0.65 us (5%)
    pallas_call x1, Pallas kernels, local(): pl.pallas_call(functools.partial(exchange_kernel, counts), out_shape=(fie...  11.1 us
    pallas_call x1, Pallas kernels, local(): pl.pallas_call(finish_kernel, out_shape=(field,) * 3, in_specs=[vmem] * 7...  1.7 us

profile of v8, /device:TPU:1, one launch (start us, length us, event | category | flops | bytes accessed | tf_op | source)
XLA Modules:
  0.0 13.5 jit_solution(7797526184942496953)
XLA Ops:
  0.6 0.0 copy-start
  0.6 11.1 %exchange.1 = (f32[8,128,256]{2,1,0:T(8,128)S(1)}, f32[8,128,256]{2,1,0:T(8,128)S(1)}, f32[8,128,256]{2,1,0:T(8,128)S(1)}, f32[8,128,256]{2,1,0:T(8,128)S(1)}, f...) custom-call(f32[8,128,256]{2,1,0:T(8,128)} %f_hbm.1, f32[8,128,256]{2,1,0:T(8,128)} %k_hbm.1, ...), custom_call_target="tpu_custom_call" | custom-call | tf_op jit(solution)/shard_map/exchange/pallas_call | solution.py:478
  11.8 0.0 copy-done
  11.8 1.7 %finish.1 = (f32[8,128,256]{2,1,0:T(8,128)}, f32[8,128,256]{2,1,0:T(8,128)}, f32[8,128,256]{2,1,0:T(8,128)}) custom-call(f32[8,128,256]{2,1,0:T(8,128)S(1)} %get-tuple-element.9.gx, f32[8,128,256]{2,1,0:T(8,128)S(1)} %get-tuple-element.10.gy, f32[8,128,256]{2,1,0:T(8,128)S(1)} %get-tuple-element.11.dif, f32[8,128,256]{2,1,0:T(8,128)S(1)} %get-tuple-element.12.kx, ...), custom_call_target="tpu_custom_call" | custom-call | tf_op jit(solution)/shard_map/finish/pallas_call | solution.py:502
Async XLA Ops:
  0.6 11.2 %copy-start = (f32[4,32,128]{2,1,0:T(8,128)S(1)}, f32[4,32,128]{2,1,0:T(8,128)}, u32[]{:S(2)}) copy-start(f32[4,32,128]{2,1,0:T(8,128)} %constant.8.clone.tab) | copy-start | bytes 196612

commit v9 on v8

--- a/solution.py
+++ b/solution.py
@@ -186,6 +186,7 @@
     kx,
     kap,
     xc,
+    low_tab,
     fld,
     tab,
     mats,
@@ -204,25 +205,23 @@
 ):
     planes, cells_x, cells_y = fld.shape
     top = cells_x - STRIP
-    loads = []
-
-    def load(source, target):
-        copy = pltpu.make_async_copy(source, target, in_sem.at[len(loads)])
+    other_rows = pl.ds(0, top)
+    end_rows, next_rows = pl.ds(cells_x - 8, 8), pl.ds(top, STRIP - 8)
+
+    def load(place, source, target):
+        copy = pltpu.make_async_copy(source, target, in_sem.at[place])
         copy.start()
-        loads.append(copy)
         return copy
 
-    def load_rows(rows):
-        return [
-            load(f_hbm.at[:, rows, :], fld.at[:, rows, :]),
-            load(k_hbm.at[:, rows, :], kap.at[:, rows, :]),
-        ]
-
-    top_rows, other_rows = pl.ds(top, STRIP), pl.ds(0, top)
-    weights_load = load(tab_hbm.at[0:2], tab.at[0:2])
-    f_high_load, k_high_load = load_rows(top_rows)
-    other_loads = [load(tab_hbm.at[2:], tab.at[2:])] + load_rows(other_rows)
-    table_load = load(mats_hbm, mats)
+    f_end_load = load(0, f_hbm.at[:, end_rows, :], fld.at[:, end_rows, :])
+    k_end_load = load(3, k_hbm.at[:, end_rows, :], kap.at[:, end_rows, :])
+    weights_load = load(2, tab_hbm.at[0:2], tab.at[0:2])
+    f_high_load = load(1, f_hbm.at[:, next_rows, :], fld.at[:, next_rows, :])
+    k_high_load = load(6, k_hbm.at[:, next_rows, :], kap.at[:, next_rows, :])
+    other_loads = [
+        load(4, f_hbm.at[:, other_rows, :], fld.at[:, other_rows, :]),
+        load(5, k_hbm.at[:, other_rows, :], kap.at[:, other_rows, :]),
+    ]
 
     ix, iy = lax.axis_index("gx"), lax.axis_index("gy")
     nx, ny = counts
@@ -252,36 +251,38 @@
         copy.start()
         return copy
 
-    def f_sums(side, start, place):
-        with_first, with_second = twice(tab[place, 0:STRIP]), twice(tab[place + 1, 0:SHORT])
-        near = start if side == 0 else start + STRIP - SHORT
+    def sums(side, place, field, start, reach, weights):
+        with_weights = twice(tab[weights, 0:reach])
         for p in range(planes):
-            rows = fld[p, start : start + STRIP, :]
-            few = fld[p, near : near + SHORT, :]
-            xs[side, 2, p : p + 1, :] = jnp.sum(rows * with_first, axis=0, keepdims=True)
-            xs[side, 3, p : p + 1, :] = jnp.sum(few * with_second, axis=0, keepdims=True)
-
-    def k_sums(side, start, place):
-        with_first = twice(tab[place, 0:STRIP])
-        for p in range(planes):
-            rows = kap[p, start : start + STRIP, :]
-            xs[side, 4, p : p + 1, :] = jnp.sum(rows * with_first, axis=0, keepdims=True)
+            rows = field[p, start : start + reach, :]
+            xs[side, place, p : p + 1, :] = jnp.sum(rows * with_weights, axis=0, keepdims=True)
 
     def take_edge(side, place, field, edge):
         for p in range(planes):
             xs[side, place, p : p + 1, :] = field[p, edge : edge + 1, :]
 
-    f_high_load.wait()
+    def send_right(place):
+        send(1, xs.at[1, place : place + 1], xr.at[0, place : place + 1], right)
+
+    f_end_load.wait()
     take_edge(1, 0, fld, cells_x - 1)
     pl.semaphore_wait(barrier, 2)
-    send(1, xs.at[1, 0:1], xr.at[0, 0:1], right)
+    send_right(0)
+    k_end_load.wait()
+    take_edge(1, 1, kap, cells_x - 1)
+    send_right(1)
+    table_load = load(0, mats_hbm, mats)
     weights_load.wait()
-    f_sums(1, top, 0)
+    other_loads.append(load(2, tab_hbm.at[2:12], tab.at[2:12]))
+    f_high_load.wait()
+    sums(1, 2, fld, top, STRIP, 0)
+    send_right(2)
+    low_load = load(1, tab_hbm.at[12:16], low_tab)
+    sums(1, 3, fld, cells_x - SHORT, SHORT, 1)
+    send_right(3)
     k_high_load.wait()
-    take_edge(1, 1, kap, cells_x - 1)
-    send(1, xs.at[1, 1:4], xr.at[0, 1:4], right)
-    k_sums(1, top, 0)
-    send(1, xs.at[1, 4:5], xr.at[0, 4:5], right)
+    sums(1, 4, kap, top, STRIP, 0)
+    send_right(4)
     to_right = message(1, xs.at[1], xr.at[0], right)
     tell(left_ready, right)
     tell(above_ready, below)
@@ -289,8 +290,9 @@
         copy.wait()
     take_edge(0, 0, fld, 0)
     take_edge(0, 1, kap, 0)
-    f_sums(0, 0, 2)
-    k_sums(0, 0, 2)
+    sums(0, 2, fld, 0, STRIP, 2)
+    sums(0, 3, fld, 0, SHORT, 3)
+    sums(0, 4, kap, 0, STRIP, 2)
 
     ys[:, :, 5:8, :] = jnp.zeros((2, planes, 3, 128), jnp.float32)
     lane = lax.broadcasted_iota(jnp.int32, (cells_x, 128), 1)
@@ -331,10 +333,11 @@
     pl.when(jnp.logical_not(run_begins))(send_left)
 
     table_load.wait()
+    low_load.wait()
     x_rows = 4 * cells_x
     y_first = slice(x_rows, x_rows + 3 * cells_y)
     y_second = slice(x_rows + 3 * cells_y, x_rows + 6 * cells_y)
-    end_rows = x_rows + 6 * cells_y
+    ends_from = x_rows + 6 * cells_y
 
     def local_pair(pair, carry):
         tall, ktall = [], []
@@ -381,7 +384,7 @@
             stacks.append(jnp.concatenate([high, ends - high, high, blank], axis=0).T)
         turned = jnp.concatenate(stacks, axis=0).astype(jnp.bfloat16)
         reach = [
-            matmul(turned, mats[end_rows + n * FULL : end_rows + (n + 1) * FULL, :]) for n in range(3)
+            matmul(turned, mats[ends_from + n * FULL : ends_from + (n + 1) * FULL, :]) for n in range(3)
         ]
         for q in range(2):
             p = 2 * pair + q
@@ -460,7 +463,8 @@
 def local(counts, scalar, diffusivity):
     block = scalar.shape
     planes, cells_x, cells_y = block
-    columns = sum_columns(STRIP, SHORT) + sum_columns(REACH, REACH) + high_end_columns()
+    columns = sum_columns(STRIP, SHORT) + sum_columns(REACH, REACH)
+    columns += high_end_columns() + low_end_columns()
     tables = (
         jnp.asarray(stacked(columns)),
         jnp.asarray(
@@ -477,9 +481,9 @@
     ]
     parts = pl.pallas_call(
         functools.partial(exchange_kernel, counts),
-        out_shape=(field,) * 5 + (jax.ShapeDtypeStruct(ends_shape, jnp.float32),),
+        out_shape=(field,) * 5 + (jax.ShapeDtypeStruct(ends_shape, jnp.float32), jax.ShapeDtypeStruct((4, 32, 128), jnp.float32)),
         in_specs=[hbm] * 4,
-        out_specs=(vmem,) * 6,
+        out_specs=(vmem,) * 7,
         scratch_shapes=[field_buffer]
         + [pltpu.VMEM(table.shape, table.dtype) for table in tables]
         + [field_buffer, field_buffer]
@@ -487,7 +491,7 @@
         + [pltpu.VMEM((2, planes, 8, cells_x), jnp.float32)] * 2
         + [
             pltpu.VMEM(ends_shape, jnp.float32),
-            pltpu.SemaphoreType.DMA((8,)),
+            pltpu.SemaphoreType.DMA((7,)),
             pltpu.SemaphoreType.DMA((4,)),
             pltpu.SemaphoreType.DMA((4,)),
             pltpu.SemaphoreType.REGULAR,
@@ -507,7 +511,7 @@
         scratch_shapes=[strip_buffer, strip_buffer, pltpu.SemaphoreType.DMA((5,))],
         compiler_params=pltpu.CompilerParams(vmem_limit_bytes=LIMIT),
         name="finish",
-    )(*parts, jnp.asarray(stacked(low_end_columns())))
+    )(*parts)
 
 
 def solution(mesh):

time: 13.6 us -> 13.6 us (level); the launches traced: 13.5 us -> 13.3 us
    pallas_call x1, Pallas kernels: 11.1 us -> 11 us  [local(): pl.pallas_call(functools.partial(exchange_kernel, counts), out_shape=(fie...]
where the time goes in v9:
time: 13.6 us; the launch traced here: 13.3 us
  Pallas kernels  12.7 us (93%)
  between operations  0.64 us (5%)
    pallas_call x1, Pallas kernels, local(): pl.pallas_call(functools.partial(exchange_kernel, counts), out_shape=(fie...  11 us
    pallas_call x1, Pallas kernels, local(): pl.pallas_call(finish_kernel, out_shape=(field,) * 3, in_specs=[vmem] * 7...  1.7 us

profile of v9, /device:TPU:1, one launch (start us, length us, event | category | flops | bytes accessed | tf_op | source)
XLA Modules:
  0.0 13.3 jit_solution(8718261220013267909)
XLA Ops:
  0.6 11.0 %exchange.1 = (f32[8,128,256]{2,1,0:T(8,128)S(1)}, f32[8,128,256]{2,1,0:T(8,128)S(1)}, f32[8,128,256]{2,1,0:T(8,128)S(1)}, f32[8,128,256]{2,1,0:T(8,128)S(1)}, f...) custom-call(f32[8,128,256]{2,1,0:T(8,128)} %f_hbm.1, f32[8,128,256]{2,1,0:T(8,128)} %k_hbm.1, ...), custom_call_target="tpu_custom_call" | custom-call | tf_op jit(solution)/shard_map/exchange/pallas_call | solution.py:482
  11.6 1.7 %finish.1 = (f32[8,128,256]{2,1,0:T(8,128)}, f32[8,128,256]{2,1,0:T(8,128)}, f32[8,128,256]{2,1,0:T(8,128)}) custom-call(f32[8,128,256]{2,1,0:T(8,128)S(1)} %get-tuple-element.10.gx, f32[8,128,256]{2,1,0:T(8,128)S(1)} %get-tuple-element.11.gy, f32[8,128,256]{2,1,0:T(8,128)S(1)} %get-tuple-element.12.dif, f32[8,128,256]{2,1,0:T(8,128)S(1)} %get-tuple-element.13.kx, ...), custom_call_target="tpu_custom_call" | custom-call | tf_op jit(solution)/shard_map/finish/pallas_call | solution.py:506

commit v10 on v9

--- a/solution.py
+++ b/solution.py
@@ -218,10 +218,13 @@
     weights_load = load(2, tab_hbm.at[0:2], tab.at[0:2])
     f_high_load = load(1, f_hbm.at[:, next_rows, :], fld.at[:, next_rows, :])
     k_high_load = load(6, k_hbm.at[:, next_rows, :], kap.at[:, next_rows, :])
+    table_rest = load(7, tab_hbm.at[2:12], tab.at[2:12])
     other_loads = [
+        table_rest,
         load(4, f_hbm.at[:, other_rows, :], fld.at[:, other_rows, :]),
         load(5, k_hbm.at[:, other_rows, :], kap.at[:, other_rows, :]),
     ]
+    table_load = load(8, mats_hbm, mats)
 
     ix, iy = lax.axis_index("gx"), lax.axis_index("gy")
     nx, ny = counts
@@ -267,13 +270,12 @@
     f_end_load.wait()
     take_edge(1, 0, fld, cells_x - 1)
     pl.semaphore_wait(barrier, 2)
+    tell(left_ready, right)
     send_right(0)
     k_end_load.wait()
     take_edge(1, 1, kap, cells_x - 1)
     send_right(1)
-    table_load = load(0, mats_hbm, mats)
     weights_load.wait()
-    other_loads.append(load(2, tab_hbm.at[2:12], tab.at[2:12]))
     f_high_load.wait()
     sums(1, 2, fld, top, STRIP, 0)
     send_right(2)
@@ -284,7 +286,6 @@
     sums(1, 4, kap, top, STRIP, 0)
     send_right(4)
     to_right = message(1, xs.at[1], xr.at[0], right)
-    tell(left_ready, right)
     tell(above_ready, below)
     for copy in other_loads:
         copy.wait()
@@ -491,7 +492,7 @@
         + [pltpu.VMEM((2, planes, 8, cells_x), jnp.float32)] * 2
         + [
             pltpu.VMEM(ends_shape, jnp.float32),
-            pltpu.SemaphoreType.DMA((7,)),
+            pltpu.SemaphoreType.DMA((9,)),
             pltpu.SemaphoreType.DMA((4,)),
             pltpu.SemaphoreType.DMA((4,)),
             pltpu.SemaphoreType.REGULAR,

time: 13.6 us -> 13.6 us (level)
  no operation moved by 1% of the time
where the time goes in v10:
time: 13.6 us; the launch traced here: 13.3 us
  Pallas kernels  12.7 us (93%)
  between operations  0.64 us (5%)
    pallas_call x1, Pallas kernels, local(): pl.pallas_call(functools.partial(exchange_kernel, counts), out_shape=(fie...  11 us
    pallas_call x1, Pallas kernels, local(): pl.pallas_call(finish_kernel, out_shape=(field,) * 3, in_specs=[vmem] * 7...  1.7 us

profile of v10, /device:TPU:1, one launch (start us, length us, event | category | flops | bytes accessed | tf_op | source)
XLA Modules:
  0.0 13.3 jit_solution(15484647525305408009)
XLA Ops:
  0.6 11.0 %exchange.1 = (f32[8,128,256]{2,1,0:T(8,128)S(1)}, f32[8,128,256]{2,1,0:T(8,128)S(1)}, f32[8,128,256]{2,1,0:T(8,128)S(1)}, f32[8,128,256]{2,1,0:T(8,128)S(1)}, f...) custom-call(f32[8,128,256]{2,1,0:T(8,128)} %f_hbm.1, f32[8,128,256]{2,1,0:T(8,128)} %k_hbm.1, ...), custom_call_target="tpu_custom_call" | custom-call | tf_op jit(solution)/shard_map/exchange/pallas_call | solution.py:483
  11.6 1.7 %finish.1 = (f32[8,128,256]{2,1,0:T(8,128)}, f32[8,128,256]{2,1,0:T(8,128)}, f32[8,128,256]{2,1,0:T(8,128)}) custom-call(f32[8,128,256]{2,1,0:T(8,128)S(1)} %get-tuple-element.10.gx, f32[8,128,256]{2,1,0:T(8,128)S(1)} %get-tuple-element.11.gy, f32[8,128,256]{2,1,0:T(8,128)S(1)} %get-tuple-element.12.dif, f32[8,128,256]{2,1,0:T(8,128)S(1)} %get-tuple-element.13.kx, ...), custom_call_target="tpu_custom_call" | custom-call | tf_op jit(solution)/shard_map/finish/pallas_call | solution.py:507

commit v11 on v10

--- a/solution.py
+++ b/solution.py
@@ -202,6 +202,7 @@
     recv_sem,
     left_ready,
     above_ready,
+    below_ready,
 ):
     planes, cells_x, cells_y = fld.shape
     top = cells_x - STRIP
@@ -232,12 +233,20 @@
     right = (jnp.where(ix == nx - 1, 0, ix + 1), iy)
     below = (ix, jnp.where(iy == 0, ny - 1, iy - 1))
     above = (ix, jnp.where(iy == ny - 1, 0, iy + 1))
+    first_y, last_y, odd = iy == 0, iy == ny - 1, lax.rem(iy, 2) == 1
+    later_y, even = jnp.logical_not(first_y), jnp.logical_not(odd)
     barrier = pltpu.get_barrier_semaphore()
-    for neighbour in (left, above):
-        pl.semaphore_signal(barrier, inc=1, device_id=neighbour, device_id_type=MESH)
-
-    def tell(semaphore, neighbour):
-        pl.semaphore_signal(semaphore, inc=1, device_id=neighbour, device_id_type=MESH)
+
+    def tell(semaphore, neighbour, when=None):
+        def signal():
+            pl.semaphore_signal(semaphore, inc=1, device_id=neighbour, device_id_type=MESH)
+
+        signal() if when is None else pl.when(when)(signal)
+
+    tell(barrier, left)
+    tell(barrier, below, odd | first_y)
+    tell(barrier, above, odd & jnp.logical_not(last_y))
+    heard = 1 + jnp.where(odd, jnp.where(last_y, 1, 0), jnp.where(first_y, 1, 2))
 
     def message(place, source, target, device):
         return pltpu.make_async_remote_copy(
@@ -269,7 +278,7 @@
 
     f_end_load.wait()
     take_edge(1, 0, fld, cells_x - 1)
-    pl.semaphore_wait(barrier, 2)
+    pl.semaphore_wait(barrier, heard)
     tell(left_ready, right)
     send_right(0)
     k_end_load.wait()
@@ -286,7 +295,8 @@
     sums(1, 4, kap, top, STRIP, 0)
     send_right(4)
     to_right = message(1, xs.at[1], xr.at[0], right)
-    tell(above_ready, below)
+    tell(below_ready, above, even | last_y)
+    tell(above_ready, below, even & later_y)
     for copy in other_loads:
         copy.wait()
     take_edge(0, 0, fld, 0)
@@ -320,9 +330,16 @@
             ys[side, p, 2:3, :] = f_edge
             ys[side, p, 3:4, :] = jnp.sum(k_part * with_first, axis=0, keepdims=True)
             ys[side, p, 4:5, :] = k_edge
-    to_below = send(2, ys.at[0], yr.at[1], below)
-    pl.semaphore_wait(above_ready, 1)
-    to_above = send(3, ys.at[1], yr.at[0], above)
+    to_below = message(2, ys.at[0], yr.at[1], below)
+    to_above = message(3, ys.at[1], yr.at[0], above)
+
+    def send_below():
+        pl.when(odd | first_y)(lambda: pl.semaphore_wait(below_ready, 1))
+        to_below.start()
+
+    pl.when(later_y)(send_below)
+    pl.when(odd & jnp.logical_not(last_y))(lambda: pl.semaphore_wait(above_ready, 1))
+    to_above.start()
 
     to_left = message(0, xs.at[0], xr.at[1], left)
     run_begins = lax.rem(ix, RUN) == 0
@@ -365,7 +382,9 @@
             curv[p] = curv[p] + bend[q * cells_x : (q + 1) * cells_x]
         return carry
 
-    lax.fori_loop(0, planes // 2, local_pair, 0)
+    lax.fori_loop(0, planes // 2 - 1, local_pair, 0)
+    pl.when(first_y)(send_below)
+    lax.fori_loop(planes // 2 - 1, planes // 2, local_pair, 0)
 
     to_below.wait_recv()
     to_above.wait_recv()
@@ -497,6 +516,7 @@
             pltpu.SemaphoreType.DMA((4,)),
             pltpu.SemaphoreType.REGULAR,
             pltpu.SemaphoreType.REGULAR,
+            pltpu.SemaphoreType.REGULAR,
         ],
         compiler_params=pltpu.CompilerParams(
             collective_id=0, has_side_effects=True, vmem_limit_bytes=LIMIT

time: 13.6 us -> 13.5 us (level)
  no operation moved by 1% of the time
where the time goes in v11:
time: 13.5 us; the launch traced here: 13.4 us
  Pallas kernels  12.7 us (94%)
  between operations  0.64 us (5%)
    pallas_call x1, Pallas kernels, local(): pl.pallas_call(functools.partial(exchange_kernel, counts), out_shape=(fie...  11 us
    pallas_call x1, Pallas kernels, local(): pl.pallas_call(finish_kernel, out_shape=(field,) * 3, in_specs=[vmem] * 7...  1.7 us

profile of v11, /device:TPU:1, one launch (start us, length us, event | category | flops | bytes accessed | tf_op | source)
XLA Modules:
  0.0 13.4 jit_solution(10808197904035058537)
XLA Ops:
  0.6 11.0 %exchange.1 = (f32[8,128,256]{2,1,0:T(8,128)S(1)}, f32[8,128,256]{2,1,0:T(8,128)S(1)}, f32[8,128,256]{2,1,0:T(8,128)S(1)}, f32[8,128,256]{2,1,0:T(8,128)S(1)}, f...) custom-call(f32[8,128,256]{2,1,0:T(8,128)} %f_hbm.1, f32[8,128,256]{2,1,0:T(8,128)} %k_hbm.1, ...), custom_call_target="tpu_custom_call" | custom-call | tf_op jit(solution)/shard_map/exchange/pallas_call | solution.py:502
  11.7 1.7 %finish.1 = (f32[8,128,256]{2,1,0:T(8,128)}, f32[8,128,256]{2,1,0:T(8,128)}, f32[8,128,256]{2,1,0:T(8,128)}) custom-call(f32[8,128,256]{2,1,0:T(8,128)S(1)} %get-tuple-element.10.gx, f32[8,128,256]{2,1,0:T(8,128)S(1)} %get-tuple-element.11.gy, f32[8,128,256]{2,1,0:T(8,128)S(1)} %get-tuple-element.12.dif, f32[8,128,256]{2,1,0:T(8,128)S(1)} %get-tuple-element.13.kx, ...), custom_call_target="tpu_custom_call" | custom-call | tf_op jit(solution)/shard_map/finish/pallas_call | solution.py:527

commit v12 on v11

--- a/solution.py
+++ b/solution.py
@@ -196,6 +196,7 @@
     xr,
     ys,
     yr,
+    er,
     xh,
     in_sem,
     send_sem,
@@ -276,25 +277,28 @@
     def send_right(place):
         send(1, xs.at[1, place : place + 1], xr.at[0, place : place + 1], right)
 
+    pl.semaphore_wait(barrier, heard)
+    edge_row = pl.ds(cells_x - 1, 1)
+    for place, field in enumerate((f_hbm, k_hbm)):
+        send(4, field.at[:, edge_row, :], er.at[place, :, pl.ds(7, 1), :], right)
+    tell(left_ready, right)
+    weights_load.wait()
     f_end_load.wait()
-    take_edge(1, 0, fld, cells_x - 1)
-    pl.semaphore_wait(barrier, heard)
-    tell(left_ready, right)
-    send_right(0)
-    k_end_load.wait()
-    take_edge(1, 1, kap, cells_x - 1)
-    send_right(1)
-    weights_load.wait()
     f_high_load.wait()
     sums(1, 2, fld, top, STRIP, 0)
     send_right(2)
     low_load = load(1, tab_hbm.at[12:16], low_tab)
     sums(1, 3, fld, cells_x - SHORT, SHORT, 1)
     send_right(3)
+    k_end_load.wait()
     k_high_load.wait()
     sums(1, 4, kap, top, STRIP, 0)
     send_right(4)
-    to_right = message(1, xs.at[1], xr.at[0], right)
+    to_right = message(1, xs.at[1, 2:5], xr.at[0, 2:5], right)
+    both_rows = er.at[:, :, pl.ds(7, 1), :]
+    to_right_edges = message(4, both_rows, both_rows, right)
+    take_edge(1, 0, fld, cells_x - 1)
+    take_edge(1, 1, kap, cells_x - 1)
     tell(below_ready, above, even | last_y)
     tell(above_ready, below, even & later_y)
     for copy in other_loads:
@@ -423,8 +427,9 @@
 
     def combine(side, out):
         sign = 1.0 if side == 0 else -1.0
-        jump = sign * (xs[side, 0] - xr[side, 0])
-        kjump = sign * (xs[side, 1] - xr[side, 1])
+        came, kcame = (er[0, :, 7, :], er[1, :, 7, :]) if side == 0 else (xr[1, 0], xr[1, 1])
+        jump = sign * (xs[side, 0] - came)
+        kjump = sign * (xs[side, 1] - kcame)
         out[0] = FIRST.rho * xr[side, 2] + jump
         out[1] = SECOND.rho * xr[side, 3] + jump
         out[2] = jump
@@ -444,8 +449,9 @@
             columns,
             [xh[n, p : p + 1, :] for n in range(5)],
         )
-    for copy in (to_left, to_below, to_above, to_right):
+    for copy in (to_left, to_below, to_above, to_right, to_right_edges):
         copy.wait_send()
+    to_right_edges.wait_recv()
     to_right.wait_recv()
     combine(0, xc)
 
@@ -510,10 +516,11 @@
         + [pltpu.VMEM((2,) + ends_shape, jnp.float32)] * 2
         + [pltpu.VMEM((2, planes, 8, cells_x), jnp.float32)] * 2
         + [
+            pltpu.VMEM((2, planes, 8, cells_y), jnp.float32),
             pltpu.VMEM(ends_shape, jnp.float32),
             pltpu.SemaphoreType.DMA((9,)),
-            pltpu.SemaphoreType.DMA((4,)),
-            pltpu.SemaphoreType.DMA((4,)),
+            pltpu.SemaphoreType.DMA((5,)),
+            pltpu.SemaphoreType.DMA((5,)),
             pltpu.SemaphoreType.REGULAR,
             pltpu.SemaphoreType.REGULAR,
             pltpu.SemaphoreType.REGULAR,

time: 13.5 us -> 14.1 us (1.044)
  Pallas kernels: 12.7 us -> 13.3 us
    pallas_call x1, Pallas kernels: 11 us -> 11.6 us  [local(): pl.pallas_call(functools.partial(exchange_kernel, counts), out_shape=(fie...]
where the time goes in v12:
time: 14.1 us; the launch traced here: 14 us
  Pallas kernels  13.3 us (94%)
  between operations  0.64 us (5%)
    pallas_call x1, Pallas kernels, local(): pl.pallas_call(functools.partial(exchange_kernel, counts), out_shape=(fie...  11.6 us
    pallas_call x1, Pallas kernels, local(): pl.pallas_call(finish_kernel, out_shape=(field,) * 3, in_specs=[vmem] * 7...  1.7 us

profile of v12, /device:TPU:1, one launch (start us, length us, event | category | flops | bytes accessed | tf_op | source)
XLA Modules:
  0.0 14.0 jit_solution(16823574194541227216)
XLA Ops:
  0.6 11.6 %exchange.1 = (f32[8,128,256]{2,1,0:T(8,128)S(1)}, f32[8,128,256]{2,1,0:T(8,128)S(1)}, f32[8,128,256]{2,1,0:T(8,128)S(1)}, f32[8,128,256]{2,1,0:T(8,128)S(1)}, f...) custom-call(f32[8,128,256]{2,1,0:T(8,128)} %f_hbm.1, f32[8,128,256]{2,1,0:T(8,128)} %k_hbm.1, ...), custom_call_target="tpu_custom_call" | custom-call | tf_op jit(solution)/shard_map/exchange/pallas_call | solution.py:508
  12.3 1.7 %finish.1 = (f32[8,128,256]{2,1,0:T(8,128)}, f32[8,128,256]{2,1,0:T(8,128)}, f32[8,128,256]{2,1,0:T(8,128)}) custom-call(f32[8,128,256]{2,1,0:T(8,128)S(1)} %get-tuple-element.10.gx, f32[8,128,256]{2,1,0:T(8,128)S(1)} %get-tuple-element.11.gy, f32[8,128,256]{2,1,0:T(8,128)S(1)} %get-tuple-element.12.dif, f32[8,128,256]{2,1,0:T(8,128)S(1)} %get-tuple-element.13.kx, ...), custom_call_target="tpu_custom_call" | custom-call | tf_op jit(solution)/shard_map/finish/pallas_call | solution.py:534

commit v13 on v11

--- a/solution.py
+++ b/solution.py
@@ -209,16 +209,16 @@
     other_rows = pl.ds(0, top)
     end_rows, next_rows = pl.ds(cells_x - 8, 8), pl.ds(top, STRIP - 8)
 
-    def load(place, source, target):
+    def load(place, source, target, priority=0):
         copy = pltpu.make_async_copy(source, target, in_sem.at[place])
-        copy.start()
+        copy.start(priority=priority)
         return copy
 
-    f_end_load = load(0, f_hbm.at[:, end_rows, :], fld.at[:, end_rows, :])
-    k_end_load = load(3, k_hbm.at[:, end_rows, :], kap.at[:, end_rows, :])
-    weights_load = load(2, tab_hbm.at[0:2], tab.at[0:2])
-    f_high_load = load(1, f_hbm.at[:, next_rows, :], fld.at[:, next_rows, :])
-    k_high_load = load(6, k_hbm.at[:, next_rows, :], kap.at[:, next_rows, :])
+    f_end_load = load(0, f_hbm.at[:, end_rows, :], fld.at[:, end_rows, :], 1)
+    k_end_load = load(3, k_hbm.at[:, end_rows, :], kap.at[:, end_rows, :], 1)
+    weights_load = load(2, tab_hbm.at[0:2], tab.at[0:2], 1)
+    f_high_load = load(1, f_hbm.at[:, next_rows, :], fld.at[:, next_rows, :], 1)
+    k_high_load = load(6, k_hbm.at[:, next_rows, :], kap.at[:, next_rows, :], 1)
     table_rest = load(7, tab_hbm.at[2:12], tab.at[2:12])
     other_loads = [
         table_rest,

time: 13.5 us -> 13.6 us (level)
  no operation moved by 1% of the time
where the time goes in v13:
time: 13.6 us; the launch traced here: 13.4 us
  Pallas kernels  12.8 us (94%)
  between operations  0.64 us (5%)
    pallas_call x1, Pallas kernels, local(): pl.pallas_call(functools.partial(exchange_kernel, counts), out_shape=(fie...  11.1 us
    pallas_call x1, Pallas kernels, local(): pl.pallas_call(finish_kernel, out_shape=(field,) * 3, in_specs=[vmem] * 7...  1.7 us

profile of v13, /device:TPU:1, one launch (start us, length us, event | category | flops | bytes accessed | tf_op | source)
XLA Modules:
  0.0 13.4 jit_solution(8582403470232121611)
XLA Ops:
  0.6 11.1 %exchange.1 = (f32[8,128,256]{2,1,0:T(8,128)S(1)}, f32[8,128,256]{2,1,0:T(8,128)S(1)}, f32[8,128,256]{2,1,0:T(8,128)S(1)}, f32[8,128,256]{2,1,0:T(8,128)S(1)}, f...) custom-call(f32[8,128,256]{2,1,0:T(8,128)} %f_hbm.1, f32[8,128,256]{2,1,0:T(8,128)} %k_hbm.1, ...), custom_call_target="tpu_custom_call" | custom-call | tf_op jit(solution)/shard_map/exchange/pallas_call | solution.py:502
  11.7 1.7 %finish.1 = (f32[8,128,256]{2,1,0:T(8,128)}, f32[8,128,256]{2,1,0:T(8,128)}, f32[8,128,256]{2,1,0:T(8,128)}) custom-call(f32[8,128,256]{2,1,0:T(8,128)S(1)} %get-tuple-element.10.gx, f32[8,128,256]{2,1,0:T(8,128)S(1)} %get-tuple-element.11.gy, f32[8,128,256]{2,1,0:T(8,128)S(1)} %get-tuple-element.12.dif, f32[8,128,256]{2,1,0:T(8,128)S(1)} %get-tuple-element.13.kx, ...), custom_call_target="tpu_custom_call" | custom-call | tf_op jit(solution)/shard_map/finish/pallas_call | solution.py:527

commit v14 on v11

--- a/solution.py
+++ b/solution.py
@@ -279,8 +279,8 @@
     f_end_load.wait()
     take_edge(1, 0, fld, cells_x - 1)
     pl.semaphore_wait(barrier, heard)
+    send_right(0)
     tell(left_ready, right)
-    send_right(0)
     k_end_load.wait()
     take_edge(1, 1, kap, cells_x - 1)
     send_right(1)

time: 13.5 us -> 13.5 us (level)
  no operation moved by 1% of the time
where the time goes in v14:
time: 13.5 us; the launch traced here: 13.4 us
  Pallas kernels  12.7 us (94%)
  between operations  0.64 us (5%)
    pallas_call x1, Pallas kernels, local(): pl.pallas_call(functools.partial(exchange_kernel, counts), out_shape=(fie...  11 us
    pallas_call x1, Pallas kernels, local(): pl.pallas_call(finish_kernel, out_shape=(field,) * 3, in_specs=[vmem] * 7...  1.7 us

profile of v14, /device:TPU:1, one launch (start us, length us, event | category | flops | bytes accessed | tf_op | source)
XLA Modules:
  0.0 13.4 jit_solution(17142465016504567313)
XLA Ops:
  0.6 11.0 %exchange.1 = (f32[8,128,256]{2,1,0:T(8,128)S(1)}, f32[8,128,256]{2,1,0:T(8,128)S(1)}, f32[8,128,256]{2,1,0:T(8,128)S(1)}, f32[8,128,256]{2,1,0:T(8,128)S(1)}, f...) custom-call(f32[8,128,256]{2,1,0:T(8,128)} %f_hbm.1, f32[8,128,256]{2,1,0:T(8,128)} %k_hbm.1, ...), custom_call_target="tpu_custom_call" | custom-call | tf_op jit(solution)/shard_map/exchange/pallas_call | solution.py:502
  11.7 1.7 %finish.1 = (f32[8,128,256]{2,1,0:T(8,128)}, f32[8,128,256]{2,1,0:T(8,128)}, f32[8,128,256]{2,1,0:T(8,128)}) custom-call(f32[8,128,256]{2,1,0:T(8,128)S(1)} %get-tuple-element.10.gx, f32[8,128,256]{2,1,0:T(8,128)S(1)} %get-tuple-element.11.gy, f32[8,128,256]{2,1,0:T(8,128)S(1)} %get-tuple-element.12.dif, f32[8,128,256]{2,1,0:T(8,128)S(1)} %get-tuple-element.13.kx, ...), custom_call_target="tpu_custom_call" | custom-call | tf_op jit(solution)/shard_map/finish/pallas_call | solution.py:527
